TPU v7x, 128 devices: a whole 4x4x4 slice. The times are simulated.
128 devices in a mesh: row: 16 (over x, y), col: 8 (over z, core).
Axes of the slice: x: 4, y: 4, z: 4, core: 2. Of those that a mesh axis runs over, the one named last changes fastest.
Arguments:
- features: bfloat16 [49152, 256], P(('row', 'col')), may hold values from -6 to 6
- weight: bfloat16 [256, 256], replicated, may hold values from -0.375 to 0.375
- out_bias: float32 [256], replicated, may hold values from -3 to 3
- cotangent: bfloat16 [49152, 256], P(('row', 'col')), may hold values from -6 to 6
- adj_tiles: bfloat16 [16, 8, 24, 16, 128, 128], P('row', 'col'), may hold values from -0.125 to 0.125
- tile_cols: int32 [16, 8, 24, 16], P('row', 'col'), may hold values from 0 to 47, as said below
- tile_counts: int32 [16, 8, 24], P('row', 'col'), may hold values from 1 to 16, as said below
Outputs:
- activated: bfloat16 [49152, 256], P(('row', 'col'))
- grad_features: bfloat16 [49152, 256], P(('row', 'col'))
- grad_weight: float32 [256, 256], replicated
- grad_bias: float32 [256], replicated
Inputs may be any that keep to these rules, and one draw needn't show every extreme that they name: `tile_cols`: within a tile row of a block the 16 column numbers are distinct. `tile_counts`: every block has a tile row whose 16 slots are all live.
All inputs are finite; a program needn't handle non-finite values.
Results may differ from a plain program's by a relative error of at most 0.02.
Values may be sent and summed in bfloat16 or wider, within the bound.
No kernel may reach another device: no remote copies, remote signals or barrier semaphores. Data moves between devices by JAX's collectives and lax.ppermute only.
A program may use at most 192 MiB of HBM per device.

v0:
```python
import jax
import jax.numpy as jnp
from jax import lax
from jax.sharding import PartitionSpec as P


def tile_products(blocks, columns, live_mask, panel_tiles):
    accumulated = jnp.zeros((blocks.shape[0], blocks.shape[2], panel_tiles.shape[2]), jnp.float32)
    for position in range(blocks.shape[1]):
        picked = jnp.take(panel_tiles, columns[:, position], axis=0)
        product = jnp.einsum(
            "tab,tbf->taf", blocks[:, position], picked, preferred_element_type=jnp.float32
        )
        accumulated = accumulated + product * live_mask[:, position, None, None]
    return accumulated


def shards(features, weight, out_bias, cotangent, adj_tiles, tile_cols, tile_counts):
    node_dev = features.shape[0]
    feat_width = features.shape[1]
    tile_size = adj_tiles.shape[-1]
    slot_count = adj_tiles.shape[3]
    tile_rows = adj_tiles.shape[2]
    row_count = lax.axis_size("row")
    col_count = lax.axis_size("col")
    column_tiles = row_count * node_dev // tile_size
    blocks = adj_tiles.reshape(tile_rows, slot_count, tile_size, tile_size)
    columns = tile_cols.reshape(tile_rows, slot_count)
    slot_iota = lax.broadcasted_iota(jnp.int32, (tile_rows, slot_count), 1)
    live_mask = (slot_iota < tile_counts.reshape(tile_rows, 1)).astype(jnp.float32)
    gathered = jnp.dot(
        lax.all_gather(features, "row", axis=0, tiled=True),
        weight,
        preferred_element_type=jnp.float32,
    ).astype(jnp.bfloat16)
    panel_tiles = gathered.reshape(column_tiles, tile_size, feat_width)
    accumulated = tile_products(blocks, columns, live_mask, panel_tiles)
    rounded = accumulated.astype(jnp.bfloat16).astype(jnp.float32)
    summed = lax.psum_scatter(
        rounded.reshape(tile_rows * tile_size, feat_width).astype(jnp.bfloat16),
        "col",
        scatter_dimension=0,
        tiled=True,
    ).astype(jnp.float32)
    preact = summed + out_bias
    sigmoid_val = jax.nn.sigmoid(preact)
    activated = (preact * sigmoid_val).astype(jnp.bfloat16)
    grad_preact = (
        cotangent.astype(jnp.float32) * sigmoid_val * (1.0 + preact * (1.0 - sigmoid_val))
    ).astype(jnp.bfloat16)
    initial = jnp.zeros((column_tiles, tile_size, feat_width), jnp.float32)
    running = initial
    shard_rows = lax.all_gather(grad_preact, "col", axis=0, tiled=True)
    row_tiles = shard_rows.shape[0] // tile_size
    grad_tiles = shard_rows.reshape(row_tiles, tile_size, feat_width)
    for position in range(slot_count):
        product = jnp.einsum(
            "tab,taf->tbf", blocks[:, position], grad_tiles, preferred_element_type=jnp.float32
        )
        running = running.at[columns[:, position]].add(product * live_mask[:, position, None, None])
    back_rounded = running.astype(jnp.bfloat16).astype(jnp.float32)
    grad_projected = lax.psum_scatter(
        back_rounded.reshape(column_tiles * tile_size, feat_width).astype(jnp.bfloat16),
        "row",
        scatter_dimension=0,
        tiled=True,
    )
    grad_features = lax.dot_general(
        grad_projected, weight, (((1,), (1,)), ((), ())), preferred_element_type=jnp.float32
    ).astype(jnp.bfloat16)
    weight_part = lax.dot_general(
        features, grad_projected, (((0,), (0,)), ((), ())), preferred_element_type=jnp.float32
    )
    bias_part = jnp.sum(grad_preact.astype(jnp.float32), axis=0)
    scale_factor = (node_dev * row_count * col_count) ** (-0.5)
    weight_total, bias_total = lax.psum((weight_part, bias_part), ("row", "col"))
    return (activated, grad_features, weight_total * scale_factor, bias_total * scale_factor)


def solution(mesh):
    in_specs = (
        P(("row", "col"), None),
        P(),
        P(),
        P(("row", "col"), None),
        P("row", "col", None, None, None, None),
        P("row", "col", None, None),
        P("row", "col", None),
    )
    out_specs = (P(("row", "col"), None), P(("row", "col"), None), P(), P())
    return jax.shard_map(shards, mesh=mesh, in_specs=in_specs, out_specs=out_specs, check_vma=False)
```

profile of v0, /device:TPU:1, one launch (start us, length us, event | category | flops | bytes accessed | tf_op | source)
XLA Modules:
  0.0 643.5 jit_solution(12031219204387796156)
XLA Ops:
  8.0 11.9 %copy.96 = bf16[1,1,24,16,128,128]{5,4,2,3,1,0:T(8,128)(2,1)} copy(bf16[1,1,24,16,128,128]{5,4,3,2,1,0:T(8,128)(2,1)} %param.13) | data formatting | bytes 25165824 | tf_op args[4]
  20.0 40.4 %all-gather.3.cloned.1.call-done = bf16[6144,256]{1,0:T(8,128)(2,1)} async-done(((bf16[384,256]{1,0:T(8,128)(2,1)}), bf16[6144,256]{1,0:T(8,128)(2,1)}) %all-gather.3.cloned.1.call-update) | async-done | bytes 3145744 | tf_op jit(solution)/shard_map/all_gather | solution.py:32
  95.6 3.6 fusion.13
  99.2 3.6 fusion.15
  102.7 3.6 fusion.17
  106.4 3.6 fusion.19
  133.4 17.8 %bitcast_convert_fusion = bf16[24,128,256]{2,1,0:T(8,128)(2,1)} fusion(f32[24,256,128]{1,2,0:T(8,128)} %fusion.1, f32[24,256,128]{1,2,0:T(8,128)} %fusion.3, f32[24,256,128]{1,2,0:T(8,128)} %fusion.5, f32[24,256,128]{1,2,0:T(8,128)} %fusion.7, f32[24,256,128]{1,2,0:T(8,128)} %fusion.9, f32[24,256,128]{1,2,0:T(8,128)S(1)} %fusion.11, ...), kind=kOutput, calls=%fused_computation.34 | convolution fusion | flops 227278848 | bytes 51119640 | tf_op jit(solution)/shard_map/tab,tbf->taf/dot_general | solution.py:11
  151.3 29.8 %reduce-scatter.3.cloned.1.call-done = bf16[384,256]{1,0:T(8,128)(2,1)} async-done(((bf16[3072,256]{1,0:T(8,128)(2,1)}), bf16[384,256]{1,0:T(8,128)(2,1)}) %reduce-scatter.3.cloned.1.call-update) | async-done | bytes 196624 | tf_op jit(solution)/shard_map/reduce_scatter | solution.py:39
  183.1 26.9 %all-gather.5.cloned.1.call-done = bf16[3072,256]{1,0:T(8,128)(2,1)} async-done(((bf16[384,256]{1,0:T(8,128)(2,1)}), bf16[3072,256]{1,0:T(8,128)(2,1)}) %all-gather.5.cloned.1.call-update) | async-done | bytes 1572880 | tf_op jit(solution)/shard_map/all_gather | solution.py:53
  210.1 4.2 multiply_bitcast_fusion.14
  214.2 3.6 multiply_bitcast_fusion.15
  221.2 3.6 multiply_bitcast_fusion.12
  256.1 9.8 %scatter_fusion = f32[48,128,256]{2,1,0:T(8,128)} fusion(f32[48,128,256]{2,1,0:T(8,128)} %broadcast_in_dim.11, s32[24]{0:T(128)S(1)} %get-tuple-element.49, f32[24,128,256]{2,1,0:T(8,128)} %multiply_bitcast_fusion.15), kind=kCustom, calls=%fused_computation.16 | custom fusion | flops 786432 | bytes 9437280 | tf_op jit(solution)/shard_map/scatter-add | solution.py:60
  265.9 9.4 %scatter_fusion.1 = f32[48,128,256]{2,1,0:T(8,128)} fusion(f32[48,128,256]{2,1,0:T(8,128)} %scatter_fusion, s32[24]{0:T(128)S(1)} %get-tuple-element.50, f32[24,128,256]{2,1,0:T(8,128)} %multiply_bitcast_fusion.14), kind=kCustom, calls=%fused_computation.17 | custom fusion | flops 786432 | bytes 9437280 | tf_op jit(solution)/shard_map/scatter-add | solution.py:60
  275.3 9.5 %scatter_fusion.2 = f32[48,128,256]{2,1,0:T(8,128)} fusion(f32[48,128,256]{2,1,0:T(8,128)} %scatter_fusion.1, s32[24]{0:T(128)S(1)} %get-tuple-element.51, f32[24,128,256]{2,1,0:T(8,128)} %multiply_bitcast_fusion.13), kind=kCustom, calls=%fused_computation.18 | custom fusion | flops 786432 | bytes 9437280 | tf_op jit(solution)/shard_map/scatter-add | solution.py:60
  284.8 9.3 %scatter_fusion.3 = f32[48,128,256]{2,1,0:T(8,128)} fusion(f32[48,128,256]{2,1,0:T(8,128)} %scatter_fusion.2, s32[24]{0:T(128)S(1)} %get-tuple-element.52, f32[24,128,256]{2,1,0:T(8,128)} %multiply_bitcast_fusion.12), kind=kCustom, calls=%fused_computation.19 | custom fusion | flops 786432 | bytes 9437280 | tf_op jit(solution)/shard_map/scatter-add | solution.py:60
  294.1 9.4 %scatter_fusion.4 = f32[48,128,256]{2,1,0:T(8,128)} fusion(f32[48,128,256]{2,1,0:T(8,128)} %scatter_fusion.3, s32[24]{0:T(128)S(1)} %get-tuple-element.53, f32[24,128,256]{2,1,0:T(8,128)} %multiply_bitcast_fusion.11), kind=kCustom, calls=%fused_computation.20 | custom fusion | flops 786432 | bytes 9437280 | tf_op jit(solution)/shard_map/scatter-add | solution.py:60
  303.5 9.3 %scatter_fusion.5 = f32[48,128,256]{2,1,0:T(8,128)} fusion(f32[48,128,256]{2,1,0:T(8,128)} %scatter_fusion.4, s32[24]{0:T(128)S(1)} %get-tuple-element.54, f32[24,128,256]{2,1,0:T(8,128)} %multiply_bitcast_fusion.10), kind=kCustom, calls=%fused_computation.21 | custom fusion | flops 786432 | bytes 9437280 | tf_op jit(solution)/shard_map/scatter-add | solution.py:60
  312.8 9.3 %scatter_fusion.6 = f32[48,128,256]{2,1,0:T(8,128)} fusion(f32[48,128,256]{2,1,0:T(8,128)} %scatter_fusion.5, s32[24]{0:T(128)S(1)} %get-tuple-element.55, f32[24,128,256]{2,1,0:T(8,128)} %multiply_bitcast_fusion.9), kind=kCustom, calls=%fused_computation.22 | custom fusion | flops 786432 | bytes 9437280 | tf_op jit(solution)/shard_map/scatter-add | solution.py:60
  322.1 9.3 %scatter_fusion.7 = f32[48,128,256]{2,1,0:T(8,128)} fusion(f32[48,128,256]{2,1,0:T(8,128)} %scatter_fusion.6, s32[24]{0:T(128)S(1)} %get-tuple-element.56, f32[24,128,256]{2,1,0:T(8,128)} %multiply_bitcast_fusion.8), kind=kCustom, calls=%fused_computation.23 | custom fusion | flops 786432 | bytes 9437280 | tf_op jit(solution)/shard_map/scatter-add | solution.py:60
  331.4 9.5 %scatter_fusion.8 = f32[48,128,256]{2,1,0:T(8,128)} fusion(f32[48,128,256]{2,1,0:T(8,128)} %scatter_fusion.7, s32[24]{0:T(128)S(1)} %get-tuple-element.57, f32[24,128,256]{2,1,0:T(8,128)} %multiply_bitcast_fusion.7), kind=kCustom, calls=%fused_computation.24 | custom fusion | flops 786432 | bytes 9437280 | tf_op jit(solution)/shard_map/scatter-add | solution.py:60
  340.9 9.5 %scatter_fusion.9 = f32[48,128,256]{2,1,0:T(8,128)} fusion(f32[48,128,256]{2,1,0:T(8,128)} %scatter_fusion.8, s32[24]{0:T(128)S(1)} %get-tuple-element.58, f32[24,128,256]{2,1,0:T(8,128)} %multiply_bitcast_fusion.6), kind=kCustom, calls=%fused_computation.25 | custom fusion | flops 786432 | bytes 9437280 | tf_op jit(solution)/shard_map/scatter-add | solution.py:60
  350.4 9.3 %scatter_fusion.10 = f32[48,128,256]{2,1,0:T(8,128)} fusion(f32[48,128,256]{2,1,0:T(8,128)} %scatter_fusion.9, s32[24]{0:T(128)S(1)} %get-tuple-element.59, f32[24,128,256]{2,1,0:T(8,128)} %multiply_bitcast_fusion.5), kind=kCustom, calls=%fused_computation.26 | custom fusion | flops 786432 | bytes 9437280 | tf_op jit(solution)/shard_map/scatter-add | solution.py:60
  359.7 9.5 %scatter_fusion.11 = f32[48,128,256]{2,1,0:T(8,128)} fusion(f32[48,128,256]{2,1,0:T(8,128)} %scatter_fusion.10, s32[24]{0:T(128)S(1)} %get-tuple-element.60, f32[24,128,256]{2,1,0:T(8,128)} %multiply_bitcast_fusion.4), kind=kCustom, calls=%fused_computation.27 | custom fusion | flops 786432 | bytes 9437280 | tf_op jit(solution)/shard_map/scatter-add | solution.py:60
  369.2 9.4 %scatter_fusion.12 = f32[48,128,256]{2,1,0:T(8,128)} fusion(f32[48,128,256]{2,1,0:T(8,128)} %scatter_fusion.11, s32[24]{0:T(128)S(1)} %get-tuple-element.61, f32[24,128,256]{2,1,0:T(8,128)} %multiply_bitcast_fusion.3), kind=kCustom, calls=%fused_computation.28 | custom fusion | flops 786432 | bytes 9437280 | tf_op jit(solution)/shard_map/scatter-add | solution.py:60
  378.6 9.5 %scatter_fusion.13 = f32[48,128,256]{2,1,0:T(8,128)} fusion(f32[48,128,256]{2,1,0:T(8,128)} %scatter_fusion.12, s32[24]{0:T(128)S(1)} %get-tuple-element.62, f32[24,128,256]{2,1,0:T(8,128)} %multiply_bitcast_fusion.2), kind=kCustom, calls=%fused_computation.29 | custom fusion | flops 786432 | bytes 9437280 | tf_op jit(solution)/shard_map/scatter-add | solution.py:60
  388.1 9.2 %scatter_fusion.14 = f32[48,128,256]{2,1,0:T(8,128)} fusion(f32[48,128,256]{2,1,0:T(8,128)} %scatter_fusion.13, s32[24]{0:T(128)S(1)} %get-tuple-element.63, f32[24,128,256]{2,1,0:T(8,128)} %multiply_bitcast_fusion.1), kind=kCustom, calls=%fused_computation.30 | custom fusion | flops 786432 | bytes 9437280 | tf_op jit(solution)/shard_map/scatter-add | solution.py:60
  397.3 8.5 %scatter_fusion.15 = f32[48,128,256]{2,1,0:T(8,128)} fusion(f32[48,128,256]{2,1,0:T(8,128)} %scatter_fusion.14, s32[24]{0:T(128)S(1)} %get-tuple-element.48, f32[24,128,256]{2,1,0:T(8,128)S(1)} %multiply_bitcast_fusion), kind=kCustom, calls=%fused_computation.31 | custom fusion | flops 786432 | bytes 9437280 | tf_op jit(solution)/shard_map/scatter-add | solution.py:60
  405.8 4.9 convert_element_type.48
  410.8 65.4 %psum.15 = f32[256]{0:T(256)S(1)} all-reduce(f32[256]{0:T(256)S(1)} %get-tuple-element.13), channel_id=1, replica_groups=mesh['row'=16,'col'=8] {'row','col'}, use_global_device_ids=true, to_apply=%region_20.22 | all-reduce | flops 256 | bytes 2048 | tf_op jit(solution)/shard_map/psum | solution.py:76
  476.8 8.8 %reduce-scatter.5.cloned.1.call-done = bf16[384,256]{1,0:T(8,128)(2,1)} async-done(((bf16[6144,256]{1,0:T(8,128)(2,1)}), bf16[384,256]{1,0:T(8,128)(2,1)}) %reduce-scatter.5.cloned.1.call-update) | async-done | bytes 196624 | tf_op jit(solution)/shard_map/reduce_scatter | solution.py:62
  489.4 145.6 %all-reduce.2.cloned.1.call-done = f32[256,256]{0,1:T(8,128)} async-done(((f32[256,256]{0,1:T(8,128)}), f32[256,256]{0,1:T(8,128)}) %all-reduce.2.cloned.1.call-update) | async-done | bytes 262160 | tf_op jit(solution)/shard_map/psum | solution.py:76
  (126 shorter events, 102.3 us)
Async XLA Ops:
  7.2 53.3 %copy-start = (bf16[256,256]{1,0:T(8,128)(2,1)S(1)}, bf16[256,256]{1,0:T(8,128)(2,1)}, u32[]{:S(2)}) copy-start(bf16[256,256]{1,0:T(8,128)(2,1)} %param.10) | copy-start | bytes 393220
  7.2 53.2 %all-gather.3.cloned.1.call-start = ((), (), s32[]{:S(2)}) async-start(), calls=%async_computation.2 | async-start | bytes 3342336 | tf_op jit(solution)/shard_map/all_gather | solution.py:32
  7.9 11.9 %copy-start.18 = (s32[1,1,24,16]{2,3,1,0:T(8,128)S(1)}, s32[1,1,24,16]{2,3,1,0:T(8,128)}, u32[]{:S(2)}) copy-start(s32[1,1,24,16]{2,3,1,0:T(8,128)} %param.14) | copy-start | bytes 4612
  7.9 12.1 %copy-start.20 = (s32[1,1,24]{2,1,0:T(1,128)S(1)}, s32[1,1,24]{2,1,0:T(1,128)}, u32[]{:S(2)}) copy-start(s32[1,1,24]{2,1,0:T(1,128)} %param.15) | copy-start | bytes 292
  7.9 173.2 %reduce-scatter.3.cloned.1.call-start = ((), (), s32[]{:S(2)}) async-start(), calls=%async_computation.3 | async-start | bytes 1769472 | tf_op jit(solution)/shard_map/reduce_scatter | solution.py:39
  93.1 2.5 copy-start.15
  93.1 16.8 %slice-start = ((s8[12582912]{0:T(1024)(128)(4,1)}), s8[4194304]{0:T(1024)(128)(4,1)S(1)}, s32[]{:S(2)}) async-start(s8[12582912]{0:T(1024)(128)(4,1)} %bitcast.286), calls=%async_computation.7 | async-start | bytes 8388608
  95.5 3.6 copy-start.13
  95.6 14.4 %slice-start.1 = ((s8[12582912]{0:T(1024)(128)(4,1)}), s8[4194304]{0:T(1024)(128)(4,1)S(1)}, s32[]{:S(2)}) async-start(s8[12582912]{0:T(1024)(128)(4,1)} %bitcast.286), calls=%async_computation.8 | async-start | bytes 8388608
  99.2 3.6 copy-start.14
  102.7 3.6 copy-start.11
  102.7 7.2 %slice-start.2 = ((s8[12582912]{0:T(1024)(128)(4,1)}), s8[4194304]{0:T(1024)(128)(4,1)S(1)}, s32[]{:S(2)}) async-start(s8[12582912]{0:T(1024)(128)(4,1)} %bitcast.286), calls=%async_computation.9 | async-start | bytes 8388608
  106.4 3.6 copy-start.12
  109.9 2.4 copy-start.9
  112.4 2.4 copy-start.10
  114.8 2.3 copy-start.7
  117.0 2.4 copy-start.8
  119.4 2.3 copy-start.5
  121.7 2.3 copy-start.6
  124.0 2.4 copy-start.3
  126.4 2.3 copy-start.4
  128.7 2.5 copy-start.2
  133.4 47.7 %copy-start.17 = (bf16[384,256]{1,0:T(8,128)(2,1)S(1)}, bf16[384,256]{1,0:T(8,128)(2,1)}, u32[]{:S(2)}) copy-start(bf16[384,256]{1,0:T(8,128)(2,1)} %param.12) | copy-start | bytes 589828
  133.4 47.7 %copy-start.19 = (f32[256]{0:T(256)S(1)}, f32[256]{0:T(256)}, u32[]{:S(2)}) copy-start(f32[256]{0:T(256)} %param.11) | copy-start | bytes 3076
  151.3 58.8 %all-gather.5.cloned.1.call-start = ((), (), s32[]{:S(2)}) async-start(), calls=%async_computation.4 | async-start | bytes 1769472 | tf_op jit(solution)/shard_map/all_gather | solution.py:53
  183.0 302.6 %reduce-scatter.5.cloned.1.call-start = ((), (), s32[]{:S(2)}) async-start(), calls=%async_computation.5 | async-start | bytes 3342336 | tf_op jit(solution)/shard_map/reduce_scatter | solution.py:62
  210.1 4.2 copy-start.1
  210.1 18.3 %slice-start.3 = ((s8[12582912]{0:T(1024)(128)(4,1)}), s8[4194304]{0:T(1024)(128)(4,1)S(1)}, s32[]{:S(2)}) async-start(s8[12582912]{0:T(1024)(128)(4,1)} %bitcast.298), calls=%async_computation.10 | async-start | bytes 8388608
  214.2 14.1 %slice-start.4 = ((s8[12582912]{0:T(1024)(128)(4,1)}), s8[4194304]{0:T(1024)(128)(4,1)S(1)}, s32[]{:S(2)}) async-start(s8[12582912]{0:T(1024)(128)(4,1)} %bitcast.298), calls=%async_computation.11 | async-start | bytes 8388608
  221.2 7.1 %slice-start.5 = ((s8[12582912]{0:T(1024)(128)(4,1)}), s8[4194304]{0:T(1024)(128)(4,1)S(1)}, s32[]{:S(2)}) async-start(s8[12582912]{0:T(1024)(128)(4,1)} %bitcast.298), calls=%async_computation.12 | async-start | bytes 8388608
  410.7 74.9 %copy-start.16 = (bf16[384,256]{1,0:T(8,128)(2,1)S(1)}, bf16[384,256]{1,0:T(8,128)(2,1)}, u32[]{:S(2)}) copy-start(bf16[384,256]{1,0:T(8,128)(2,1)} %param.9) | copy-start | bytes 589828
  410.8 224.2 %all-reduce.2.cloned.1.call-start = ((), (), s32[]{:S(2)}) async-start(), calls=%async_computation.6 | async-start | bytes 524288 | tf_op jit(solution)/shard_map/psum | solution.py:76
Sparse Core Ops, SparseCore 0:
  10.2 50.2 all-gather.2
  151.4 29.7 reduce-scatter.2
  183.4 26.6 all-gather.4
  410.9 74.6 reduce-scatter.4
  490.8 144.1 all-reduce.1
where the time goes:
time: 653 us; the launch traced here: 644 us
  waiting for transfers between devices  252 us (39%)
  other arithmetic  158 us (24%)
  matrix products  107 us (16%)
  blocking collectives  65.4 us (10%)
  local copies, waits for them, and re-layouts  46 us (7%)
  between operations  14.2 us (2%)
    scatter-add x16, other arithmetic, shards(): running.at[columns[:, position]]  150 us
    psum x1, waiting for transfers between devices, shards(): lax.psum((weight_part, bias_part), ('row', 'col'))  146 us
    psum x1, blocking collectives, shards(): lax.psum((weight_part, bias_part), ('row', 'col'))  65.4 us
    dot_general x16, matrix products, tile_products(): jnp.einsum('tab,tbf->taf', blocks[:, position], picked, preferred_element...  58 us
    dot_general x16, matrix products, shards(): jnp.einsum('tab,taf->tbf', blocks[:, position], grad_tiles, preferred_ele...  42.6 us
    all_gather x1, waiting for transfers between devices, shards(): lax.all_gather(features, 'row', axis=0, tiled=True)  40.4 us
    reduce_scatter x1, waiting for transfers between devices, shards(): lax.psum_scatter(rounded.reshape(tile_rows * tile_size, feat_width).astyp...  29.8 us
    gather x16, local copies, waits for them, and re-layouts, tile_products(): picked = jnp.take(panel_tiles, columns[:, position], axis=0)  29.8 us
  transfers between devices with their start and end apart: 5, of which 5 were waited for; matrix products, arithmetic and copies ran while one was open for 2% of the time, Pallas kernels for 0%

commit v1 on v0

v1 whole, which is shorter than its diff:
```python
import functools

import jax
import jax.numpy as jnp
from jax import lax
from jax.experimental import pallas as pl
from jax.experimental.pallas import tpu as pltpu
from jax.sharding import PartitionSpec as P


TILE = 128
SLOTS = 16
SIDE = 4
ND = 384
PER = ND // TILE
DUMMY = SIDE * SIDE * PER
BROWS = 16
BF = jnp.bfloat16
F32 = jnp.float32
VM = pl.BlockSpec(memory_space=pltpu.VMEM)


def send_plane(value, first, step):
    pairs = []
    for row in range(SIDE * SIDE):
        for col in range(2 * SIDE):
            x, y = divmod(row, SIDE)
            if (col % 2 == 0) == first:
                x = (x + step) % SIDE
            else:
                y = (y + step) % SIDE
            pairs.append((row * 2 * SIDE + col, (x * SIDE + y) * 2 * SIDE + col))
    return lax.ppermute(value, ("row", "col"), pairs)


def send_row(value, dx, dy):
    pairs = []
    for x in range(SIDE):
        for y in range(SIDE):
            pairs.append((x * SIDE + y, (x + dx) % SIDE * SIDE + (y + dy) % SIDE))
    return lax.ppermute(value, "row", pairs)


def send_col(value, dz, dk):
    pairs = []
    for z in range(SIDE):
        for k in range(2):
            pairs.append((z * 2 + k, (z + dz) % SIDE * 2 + (k ^ dk)))
    return lax.ppermute(value, "col", pairs)


def rel(first, second):
    return (second % SIDE) * SIDE + first % SIDE


def params(mb):
    return pltpu.CompilerParams(vmem_limit_bytes=mb * 1024 * 1024)


def cost(flops, data):
    return pl.CostEstimate(flops=flops, bytes_accessed=data, transcendentals=0)


def sum4(a, b, c, d):
    return (a + c) + (b + d)


def pack_bias(total):
    hi = total.astype(BF)
    lo = (total - hi.astype(F32)).astype(BF)
    rows = lax.broadcasted_iota(jnp.int32, (BROWS, total.shape[1]), 0)
    zero = jnp.zeros((BROWS, total.shape[1]), F32)
    return jnp.where(rows == 0, hi.astype(F32), jnp.where(rows == 1, lo.astype(F32), zero)).astype(BF)


def index_kernel(place, cols, counts, out):
    column = cols[...]
    source = (column * 43) >> 7
    away_x = (place[0] - (source >> 2)) & (SIDE - 1)
    away_y = (place[1] - source) & (SIDE - 1)
    distance = jnp.where(place[2] == 0, away_y * SIDE + away_x, away_x * SIDE + away_y)
    live = lax.broadcasted_iota(jnp.int32, column.shape, 1) < counts[...]
    out[...] = jnp.where(live, distance * PER + (column - source * PER), DUMMY)


def forward_rows(order, index, adj, panel, step, i):
    tile_row = order[step] * PER + i
    total = None
    for pair in range(SLOTS // 2):
        picked = []
        for half in range(2):
            start = pl.multiple_of(index[tile_row, 2 * pair + half] * TILE, TILE)
            picked.append(panel[pl.ds(start, TILE), :])
        left = jnp.concatenate([adj[i, 2 * pair], adj[i, 2 * pair + 1]], axis=1)
        product = jnp.dot(left, jnp.concatenate(picked, axis=0), preferred_element_type=F32)
        total = product if total is None else total + product
    return total.astype(BF)


def forward_first_kernel(order, index, adj, own, f1, f2, f3, s1, s2, s3, m1, m2, m3, out, panel):
    step = pl.program_id(0)

    @pl.when(step == 0)
    def _():
        panel[0:ND, :] = own[...]
        for a, ref in enumerate((f1, f2, f3)):
            panel[rel(a + 1, 0) * ND:(rel(a + 1, 0) + 1) * ND, :] = ref[...]
        for b, (side, many) in enumerate(((s1, m1), (s2, m2), (s3, m3))):
            start = rel(0, b + 1) * ND
            panel[start:start + ND, :] = side[...]
            panel[start + ND:start + SIDE * ND, :] = many[...]
        panel[DUMMY * TILE:, :] = jnp.zeros((TILE, panel.shape[1]), BF)

    for i in range(PER):
        out[step, i * TILE:(i + 1) * TILE, :] = forward_rows(order, index, adj, panel, step, i)


def forward_next_kernel(offset, order, index, adj, panel, out):
    step = pl.program_id(0)
    for i in range(PER):
        out[step, i * TILE:(i + 1) * TILE, :] = forward_rows(order, index, adj, panel, step + offset, i)


def forward(offset, steps, order, index, adj, operands):
    width = operands[0].shape[1]
    first = len(operands) > 1
    shape = jax.ShapeDtypeStruct((steps, ND, width), BF)
    panel = jax.ShapeDtypeStruct(((DUMMY + 1) * TILE, width), BF)
    return pl.pallas_call(
        forward_first_kernel if first else functools.partial(forward_next_kernel, offset),
        out_shape=(shape, panel) if first else shape,
        grid_spec=pltpu.PrefetchScalarGridSpec(
            num_scalar_prefetch=2,
            grid=(steps,),
            in_specs=[pl.BlockSpec((PER, SLOTS, TILE, TILE), lambda s, o, n: (o[s + offset], 0, 0, 0))]
            + [VM] * len(operands),
            out_specs=(VM, VM) if first else VM,
        ),
        compiler_params=params(12),
        cost_estimate=cost(steps * PER * SLOTS * 2 * TILE * TILE * width, steps * PER * SLOTS * TILE * TILE * 2),
        name="forward",
    )(order, index, adj, *operands)


def activation_kernel(keep, recv, r1, r2, r3, weight, bias, cot, act, grad_out, terms):
    agg = keep[0].astype(F32) + recv[0].astype(F32)
    for ref in (r1, r2, r3):
        agg = agg + ref[...].astype(F32)
    agg16 = agg.astype(BF)
    pre = jnp.dot(agg16, weight[...], preferred_element_type=F32) + bias[...]
    sig = 1.0 / (1.0 + jnp.exp(-pre))
    act[...] = (pre * sig).astype(BF)
    grad = (cot[...].astype(F32) * sig * (1.0 + pre * (1.0 - sig))).astype(BF)
    grad_out[...] = grad
    wrows = terms.shape[0] - BROWS
    terms[0:wrows, :] = lax.dot_general(
        agg16, grad, (((0,), (0,)), ((), ())), preferred_element_type=F32
    ).astype(BF)
    terms[wrows:, :] = pack_bias(jnp.sum(grad.astype(F32), axis=0, keepdims=True))


def backward_kernel(offset, count, initial, final, order, index, adj, *refs):
    sources, refs = refs[:count], refs[count:]
    if not initial:
        refs = refs[1:]
    acc, refs = refs[0], refs[1:]
    if final:
        own, sides, many = refs[0], refs[1:SIDE], refs[SIDE:2 * SIDE - 1]
    turned = refs[-1]
    step = pl.program_id(0)

    @pl.when(step == 0)
    def _():
        for s, ref in enumerate(sources):
            for i in range(PER):
                turned[s * PER + i] = ref[i * TILE:(i + 1) * TILE, :].T
        if initial:
            acc[...] = jnp.zeros_like(acc)

    for i in range(PER):
        tile_row = order[step + offset] * PER + i
        left = turned[step * PER + i]
        for pair in range(SLOTS // 2):
            right = jnp.concatenate([adj[i, 2 * pair], adj[i, 2 * pair + 1]], axis=1)
            product = jnp.dot(left, right, preferred_element_type=F32)
            first = index[tile_row, 2 * pair]
            second = index[tile_row, 2 * pair + 1]
            acc[first] = acc[first] + product[:, :TILE]
            acc[second] = acc[second] + product[:, TILE:]

    if final:
        @pl.when(step == count - 1)
        def _():
            for b in (1, 2, 3, 0):
                for a in range(SIDE):
                    if b == 0:
                        out, start = own, a * ND
                    elif a == 0:
                        out, start = sides[b - 1], 0
                    else:
                        out, start = many[b - 1], (a - 1) * ND
                    for n in range(PER):
                        row = start + n * TILE
                        out[row:row + TILE, :] = acc[rel(-a, -b) * PER + n].astype(BF).T


def backward(offset, order, index, adj, sources, acc=None, final=False):
    width = sources[0].shape[1]
    count = len(sources)
    state = jax.ShapeDtypeStruct((DUMMY + 1, width, TILE), F32)
    outs = (state,)
    if final:
        outs += tuple(jax.ShapeDtypeStruct((n * ND, width), BF) for n in (SIDE, 1, 1, 1, 3, 3, 3))
    initial = acc is None
    extra = [] if initial else [acc]
    return pl.pallas_call(
        functools.partial(backward_kernel, offset, count, initial, final),
        out_shape=outs,
        grid_spec=pltpu.PrefetchScalarGridSpec(
            num_scalar_prefetch=2,
            grid=(count,),
            in_specs=[pl.BlockSpec((PER, SLOTS, TILE, TILE), lambda s, o, n: (o[s + offset], 0, 0, 0))]
            + [VM] * (count + len(extra)),
            out_specs=[VM] * len(outs),
            scratch_shapes=[pltpu.VMEM((count * PER, width, TILE), BF)],
        ),
        input_output_aliases={} if initial else {3 + count: 0},
        compiler_params=params(16),
        cost_estimate=cost(count * PER * SLOTS * 2 * TILE * TILE * width, count * PER * SLOTS * TILE * TILE * 2),
        name="backward",
    )(order, index, adj, *sources, *extra)


def add_terms_kernel(t0, t1, t2, t3, out):
    total = sum4(*(ref[...].astype(F32) for ref in (t0, t1, t2, t3)))
    wrows = out.shape[0] - BROWS
    out[0:wrows, :] = total[:wrows].astype(BF)
    out[wrows:, :] = pack_bias(jnp.sum(total[wrows:], axis=0, keepdims=True))


def last_terms_kernel(scale, t0, t1, wout, bout):
    total = t0[...].astype(F32) + t1[...].astype(F32)
    wrows = wout.shape[0]
    wout[...] = total[:wrows] * scale
    bout[...] = jnp.sum(total[wrows:], axis=0, keepdims=True) * scale


def small(kernel, outs, operands):
    return pl.pallas_call(
        kernel,
        out_shape=outs,
        in_specs=[VM] * len(operands),
        out_specs=jax.tree.map(lambda _: VM, outs),
        compiler_params=params(8),
    )(*operands)


def relay_kernel(own, r1, r2, r3, *outs):
    for a, out in enumerate(outs):
        total = own[(a + 1) * ND:(a + 2) * ND, :].astype(F32)
        for ref in (r1, r2, r3):
            total = total + ref[a * ND:(a + 1) * ND, :].astype(F32)
        out[...] = total.astype(BF)


def finish_kernel(own, *refs):
    weight, gfeat = refs[-2:]
    total = own[0:ND, :].astype(F32)
    for ref in refs[:-2]:
        total = total + ref[...].astype(F32)
    gfeat[...] = lax.dot_general(
        total.astype(BF), weight[...], (((1,), (1,)), ((), ())), preferred_element_type=F32
    ).astype(BF)


def shards(features, weight, out_bias, cotangent, adj_tiles, tile_cols, tile_counts):
    row = lax.axis_index("row")
    col = lax.axis_index("col")
    x, y, z, k = row // SIDE, row % SIDE, col // 2, col % 2
    width = features.shape[1]
    tile_rows = adj_tiles.shape[2]
    adj = pltpu.with_memory_space_constraint(adj_tiles.reshape(tile_rows, SLOTS, TILE, TILE), pltpu.HBM)
    place = jnp.stack([x, y, k]).astype(jnp.int32)
    index = pl.pallas_call(
        index_kernel,
        out_shape=jax.ShapeDtypeStruct((tile_rows, SLOTS), jnp.int32),
        in_specs=[pl.BlockSpec(memory_space=pltpu.SMEM), VM, VM],
        out_specs=VM,
        compiler_params=params(4),
        name="index",
    )(place, tile_cols.reshape(tile_rows, SLOTS), tile_counts.reshape(tile_rows, 1))
    other = 1 - k
    onward = [(z + d) % SIDE * 2 for d in range(SIDE)]
    back = [(z - d) % SIDE * 2 for d in range(SIDE)]
    order_forward = jnp.stack(
        [v + other for v in onward] + [v + k for v in onward[1:]] + [onward[0] + k]
    ).astype(jnp.int32)
    order_backward = jnp.stack(
        [back[0] + k, back[0] + other] + [v + k for v in back[1:]] + [v + other for v in back[1:]]
    ).astype(jnp.int32)

    def fan(send, values):
        received = []
        for d in (1, 2, 3):
            received.append(send(values[d - 1], d))
        return received

    first = fan(lambda v, d: send_plane(v, True, d), [features] * 3)
    side = fan(lambda v, d: send_plane(v, False, d), [features] * 3)
    line = jnp.concatenate(first, axis=0)
    many = fan(lambda v, d: send_plane(v, False, d), [line] * 3)
    swap, panel = forward(0, SIDE, order_forward, index, adj, [features, *first, *side, *many])

    recv = send_col(swap, 0, 1)
    away = forward(SIDE, SIDE - 1, order_forward, index, adj, [panel])
    messages = [(away[d - 1].astype(F32) + recv[d].astype(F32)).astype(BF) for d in (1, 2, 3)]
    parts = fan(lambda v, d: send_col(v, d, 0), messages)
    keep = forward(2 * SIDE - 1, 1, order_forward, index, adj, [panel])
    block = jax.ShapeDtypeStruct((ND, width), BF)
    terms = jax.ShapeDtypeStruct((width + BROWS, width), BF)
    activated, grad, along = small(
        activation_kernel, (block, block, terms), [keep, recv, *parts, weight, out_bias.reshape(1, -1), cotangent]
    )

    mine = [grad] + fan(lambda v, d: send_col(v, d, 0), [grad] * 3)
    theirs = [send_col(grad, 0, 1)]
    theirs += fan(lambda v, d: send_col(v, 0, 1), mine[1:])
    along_x = [along] + fan(lambda v, d: send_row(v, d, 0), [along] * 3)
    acc, = backward(0, order_backward, index, adj, [mine[0], theirs[0]])
    along = small(add_terms_kernel, terms, along_x)
    along_y = [along] + fan(lambda v, d: send_row(v, 0, d), [along] * 3)
    acc, = backward(2, order_backward, index, adj, mine[1:], acc)
    acc, own, *blocks = backward(SIDE + 1, order_backward, index, adj, theirs[1:], acc, final=True)

    landed = fan(lambda v, d: send_plane(v, False, d), blocks[3:])
    beside = fan(lambda v, d: send_plane(v, False, d), blocks[:3])
    along = small(add_terms_kernel, terms, along_y)
    along_z = [along] + fan(lambda v, d: send_col(v, d, 0), [along] * 3)
    along = small(add_terms_kernel, terms, along_z)
    partner = send_col(along, 0, 1)
    nodes = features.shape[0] * lax.axis_size("row") * lax.axis_size("col")
    grad_weight, grad_bias = small(
        functools.partial(last_terms_kernel, nodes**-0.5),
        (jax.ShapeDtypeStruct((width, width), F32), jax.ShapeDtypeStruct((1, width), F32)),
        [along, partner],
    )
    onwards = small(relay_kernel, (block,) * 3, [own, *landed])
    last = fan(lambda v, d: send_plane(v, True, d), onwards)
    grad_features = small(finish_kernel, block, [own, *last, *beside, weight])
    return activated, grad_features, grad_weight, grad_bias.reshape(-1)


def solution(mesh):
    in_specs = (
        P(("row", "col"), None),
        P(),
        P(),
        P(("row", "col"), None),
        P("row", "col", None, None, None, None),
        P("row", "col", None, None),
        P("row", "col", None),
    )
    out_specs = (P(("row", "col"), None), P(("row", "col"), None), P(), P())

    return jax.shard_map(shards, mesh=mesh, in_specs=in_specs, out_specs=out_specs, check_vma=False)
```

time: 653 us -> 153 us (0.23); the launches traced: 644 us -> 152 us
  waiting for transfers between devices: 252 us -> 44.1 us
  other arithmetic: 158 us -> 0.21 us
  matrix products: 107 us -> 0 us
  starting transfers between devices: 0.2 us -> 67.2 us
  blocking collectives: 65.4 us -> 0 us
  local copies, waits for them, and re-layouts: 46 us -> 4.67 us
  Pallas kernels: 0 us -> 34.8 us
  between operations: 14.2 us -> 0.8 us
    scatter-add x16 -> x0, other arithmetic: 150 us -> none  [shards(): running.at[columns[:, position]]]
    psum x1 -> x0, waiting for transfers between devices: 146 us -> none  [shards(): lax.psum((weight_part, bias_part), ('row', 'col'))]
    dot_general x35 -> x0, matrix products: 107 us -> none  [the longest x16 58 us: tile_products(): jnp.einsum('tab,tbf->taf', blocks[:, position], picked, preferred_element...]
    all_gather x2 -> x0, waiting for transfers between devices: 67.3 us -> none  [the longest x1 40.4 us: shards(): lax.all_gather(features, 'row', axis=0, tiled=True)]
    ppermute x0 -> x39, starting transfers between devices: none -> 67.2 us  [the longest x15 34.1 us: send_col(): return lax.ppermute(value, 'col', pairs)]
    psum x1 -> x0, blocking collectives: 65.4 us -> none  [shards(): lax.psum((weight_part, bias_part), ('row', 'col'))]
    ppermute x0 -> x39, waiting for transfers between devices: none -> 44.1 us  [the longest x18 22.4 us: send_plane(): return lax.ppermute(value, ('row', 'col'), pairs)]
    reduce_scatter x2 -> x0, waiting for transfers between devices: 38.7 us -> none  [the longest x1 29.8 us: shards(): lax.psum_scatter(rounded.reshape(tile_rows * tile_size, feat_width).astyp...]
  transfers between devices with their start and end apart: 5 -> 39, of which waited for: 5 -> 14; matrix products, arithmetic and copies ran while one was open for 2% -> 2% of each run, Pallas kernels for 0% -> 18%
where the time goes in v1:
time: 153 us; the launch traced here: 152 us
  starting transfers between devices  67.2 us (44%)
  waiting for transfers between devices  44.1 us (29%)
  Pallas kernels  34.8 us (23%)
  local copies, waits for them, and re-layouts  4.67 us (3%)
    ppermute x15, starting transfers between devices, send_col(): return lax.ppermute(value, 'col', pairs)  34.1 us
    ppermute x18, starting transfers between devices, send_plane(): return lax.ppermute(value, ('row', 'col'), pairs)  24.9 us
    ppermute x18, waiting for transfers between devices, send_plane(): return lax.ppermute(value, ('row', 'col'), pairs)  22.4 us
    pallas_call x3, Pallas kernels, backward(): pl.pallas_call(functools.partial(backward_kernel, offset, count, initial,...  17.6 us
    pallas_call x3, Pallas kernels, forward(): pl.pallas_call(forward_first_kernel if first else functools.partial(forwa...  13.3 us
    ppermute x15, waiting for transfers between devices, send_col(): return lax.ppermute(value, 'col', pairs)  13.1 us
    ppermute x6, waiting for transfers between devices, send_row(): return lax.ppermute(value, 'row', pairs)  8.58 us
    ppermute x6, starting transfers between devices, send_row(): return lax.ppermute(value, 'row', pairs)  8.25 us
  transfers between devices with their start and end apart: 39, of which 14 were waited for; matrix products, arithmetic and copies ran while one was open for 2% of the time, Pallas kernels for 18%

profile of v1, /device:TPU:1, one launch (start us, length us, event | category | flops | bytes accessed | tf_op | source)
XLA Modules:
  0.0 151.8 jit_solution(16867302947341917816)
XLA Ops:
  0.6 2.2 %collective-permute-start = (bf16[384,256]{1,0:T(8,128)(2,1)}, bf16[384,256]{1,0:T(8,128)(2,1)S(1)}, u32[]{:S(2)}, u32[]{:S(2)}) collective-permute-start(bf16[384,256]{1,0:T(8,128)(2,1)} %own.1), channel_id=1, source_target_pairs={{0,32},{1,9},{2,34},{3,11},{4,36},{5,13},{6,38},{7,15},{8,40},{9,1... | collective-permute-start | bytes 589832 | tf_op jit(solution)/shard_map/ppermute | solution.py:33
  2.8 2.6 %collective-permute-start.1 = (bf16[384,256]{1,0:T(8,128)(2,1)}, bf16[384,256]{1,0:T(8,128)(2,1)S(1)}, u32[]{:S(2)}, u32[]{:S(2)}) collective-permute-start(bf16[384,256]{1,0:T(8,128)(2,1)} %own.1), channel_id=1, source_target_pairs={{0,64},{1,17},{2,66},{3,19},{4,68},{5,21},{6,70},{7,23},{8,72},{9,... | collective-permute-start | bytes 589832 | tf_op jit(solution)/shard_map/ppermute | solution.py:33
  8.5 2.6 %collective-permute-done.1.f2 = bf16[384,256]{1,0:T(8,128)(2,1)S(1)} collective-permute-done((bf16[384,256]{1,0:T(8,128)(2,1)}, bf16[384,256]{1,0:T(8,128)(2,1)S(1)}, u32[]{:S(2)}, u32[]{:S(2)}) %collective-permute-start.1) | collective-permute-done | bytes 196640 | tf_op jit(solution)/shard_map/ppermute | solution.py:33
  13.4 2.5 %collective-permute-start.7 = (bf16[1152,256]{1,0:T(8,128)(2,1)}, bf16[1152,256]{1,0:T(8,128)(2,1)S(1)}, u32[]{:S(2)}, u32[]{:S(2)}) collective-permute-start(bf16[1152,256]{1,0:T(8,128)(2,1)} %constant_dynamic-update-slice_fusion), channel_id=1, source_target_pairs={{0,16},{1,65},{2,18},{3,67},{4,20},{5,69},{6,22},{7,71},{8,24},{9,... | collective-permute-start | bytes 1769480 | tf_op jit(solution)/shard_map/ppermute | solution.py:33
  18.2 13.2 %collective-permute-done.3.s1 = bf16[384,256]{1,0:T(8,128)(2,1)S(1)} collective-permute-done((bf16[384,256]{1,0:T(8,128)(2,1)}, bf16[384,256]{1,0:T(8,128)(2,1)S(1)}, u32[]{:S(2)}, u32[]{:S(2)}) %collective-permute-start.3) | collective-permute-done | bytes 196640 | tf_op jit(solution)/shard_map/ppermute | solution.py:33
  37.3 5.7 %forward.3 = (bf16[4,384,256]{2,1,0:T(8,128)(2,1)S(1)}, bf16[6272,256]{1,0:T(8,128)(2,1)S(1)}) custom-call(s32[8]{0:T(128)S(1)} %stack.70.order, s32[24,16]{1,0:T(8,128)S(1)} %index.1, bf16[24,16,128,128]{3,2,1,0:T(8,128)(2,1)} %bitcast.30, bf16[384,256]{1,0:T(8,128)(2,1)S(1)} %copy-done.1, bf16[384,256]{1,0:T(8,128)(2,1)S(1)} %collective-permute-done.f1, ...), custom_call_target="tpu_custom_call" | custom-call | flops 1610612736 | bytes 6291456 | tf_op jit(solution)/shard_map/forward/pallas_call | solution.py:129
  43.1 3.1 %collective-permute-start.9 = (bf16[4,384,256]{2,1,0:T(8,128)(2,1)S(1)}, bf16[4,384,256]{2,1,0:T(8,128)(2,1)S(1)}, u32[]{:S(2)}, u32[]{:S(2)}) collective-permute-start(bf16[4,384,256]{2,1,0:T(8,128)(2,1)S(1)} %get-tuple-element.22), channel_id=1, source_target_pairs={{0,1},{1,0},{2,3},{3,2},{4,5},{5,4},{6,7},{7,6},{8,9},{9,8},{10,11... | collective-permute-start | bytes 2359304 | tf_op jit(solution)/shard_map/ppermute | solution.py:49
  46.1 4.8 %forward.5 = bf16[3,384,256]{2,1,0:T(8,128)(2,1)S(1)} custom-call(s32[8]{0:T(128)S(1)} %stack.70.order, s32[24,16]{1,0:T(8,128)S(1)} %index.1, bf16[24,16,128,128]{3,2,1,0:T(8,128)(2,1)} %bitcast.31, bf16[6272,256]{1,0:T(8,128)(2,1)S(1)} %get-tuple-element.21.panel), custom_call_target="tpu_custom_call" | custom-call | flops 1207959552 | bytes 4718592 | tf_op jit(solution)/shard_map/forward/pallas_call | solution.py:129
  52.8 3.3 %collective-permute-start.11 = (bf16[384,256]{1,0:T(8,128)(2,1)S(1)}, bf16[384,256]{1,0:T(8,128)(2,1)S(1)}, u32[]{:S(2)}, u32[]{:S(2)}) collective-permute-start(bf16[384,256]{1,0:T(8,128)(2,1)S(1)} %get-tuple-element.39), channel_id=1, source_target_pairs={{0,4},{1,5},{2,6},{3,7},{4,0},{5,1},{6,2},{7,3},{8,12},{9,13},{10,... | collective-permute-start | bytes 589832 | tf_op jit(solution)/shard_map/ppermute | solution.py:49
  56.8 2.7 %forward.4.keep = bf16[1,384,256]{2,1,0:T(8,128)(2,1)S(1)} custom-call(s32[8]{0:T(128)S(1)} %stack.70.order, s32[24,16]{1,0:T(8,128)S(1)} %index.1, bf16[24,16,128,128]{3,2,1,0:T(8,128)(2,1)} %bitcast.32, bf16[6272,256]{1,0:T(8,128)(2,1)S(1)} %get-tuple-element.21.panel), custom_call_target="tpu_custom_call" | custom-call | flops 402653184 | bytes 1572864 | tf_op jit(solution)/shard_map/forward/pallas_call | solution.py:129
  60.2 5.1 %collective-permute-done.11.r2 = bf16[384,256]{1,0:T(8,128)(2,1)S(1)} collective-permute-done((bf16[384,256]{1,0:T(8,128)(2,1)S(1)}, bf16[384,256]{1,0:T(8,128)(2,1)S(1)}, u32[]{:S(2)}, u32[]{:S(2)}) %collective-permute-start.11) | collective-permute-done | bytes 196640 | tf_op jit(solution)/shard_map/ppermute | solution.py:49
  67.3 1.8 %collective-permute-start.30 = (bf16[272,256]{1,0:T(8,128)(2,1)S(1)}, bf16[272,256]{1,0:T(8,128)(2,1)S(1)}, u32[]{:S(2)}, u32[]{:S(2)}) collective-permute-start(bf16[272,256]{1,0:T(8,128)(2,1)S(1)} %get-tuple-element.35.t0), channel_id=1, source_target_pairs={{0,64},{8,72},{16,80},{24,88},{32,96},{40,104},{48,112},{56,120},{... | collective-permute-start | bytes 417800 | tf_op jit(solution)/shard_map/ppermute | solution.py:41
  70.1 2.5 %collective-permute-start.15 = (bf16[384,256]{1,0:T(8,128)(2,1)S(1)}, bf16[384,256]{1,0:T(8,128)(2,1)S(1)}, u32[]{:S(2)}, u32[]{:S(2)}) collective-permute-start(bf16[384,256]{1,0:T(8,128)(2,1)S(1)} %get-tuple-element.24.refs_0_), channel_id=1, source_target_pairs={{0,4},{1,5},{2,6},{3,7},{4,0},{5,1},{6,2},{7,3},{8,12},{9,13},{10,... | collective-permute-start | bytes 589832 | tf_op jit(solution)/shard_map/ppermute | solution.py:49
  72.9 2.6 %collective-permute-start.19 = (bf16[384,256]{1,0:T(8,128)(2,1)S(1)}, bf16[384,256]{1,0:T(8,128)(2,1)S(1)}, u32[]{:S(2)}, u32[]{:S(2)}) collective-permute-start(bf16[384,256]{1,0:T(8,128)(2,1)S(1)} %get-tuple-element.24.refs_0_), channel_id=1, source_target_pairs={{0,1},{1,0},{2,3},{3,2},{4,5},{5,4},{6,7},{7,6},{8,9},{9,8},{10,11... | collective-permute-start | bytes 589832 | tf_op jit(solution)/shard_map/ppermute | solution.py:49
  78.4 2.3 %collective-permute-done.15.refs_1_ = bf16[384,256]{1,0:T(8,128)(2,1)S(1)} collective-permute-done((bf16[384,256]{1,0:T(8,128)(2,1)S(1)}, bf16[384,256]{1,0:T(8,128)(2,1)S(1)}, u32[]{:S(2)}, u32[]{:S(2)}) %collective-permute-start.15) | collective-permute-done | bytes 196640 | tf_op jit(solution)/shard_map/ppermute | solution.py:49
  80.7 1.9 %collective-permute-start.16 = (bf16[384,256]{1,0:T(8,128)(2,1)S(1)}, bf16[384,256]{1,0:T(8,128)(2,1)S(1)}, u32[]{:S(2)}, u32[]{:S(2)}) collective-permute-start(bf16[384,256]{1,0:T(8,128)(2,1)S(1)} %collective-permute-done.15.refs_1_), channel_id=1, source_target_pairs={{0,1},{1,0},{2,3},{3,2},{4,5},{5,4},{6,7},{7,6},{8,9},{9,8},{10,11... | collective-permute-start | bytes 589832 | tf_op jit(solution)/shard_map/ppermute | solution.py:49
  83.2 4.9 %backward.3.refs_3_ = f32[49,256,128]{2,1,0:T(8,128)S(1)} custom-call(s32[8]{0:T(128)S(1)} %stack.81.order, s32[24,16]{1,0:T(8,128)S(1)} %index.1, bf16[24,16,128,128]{3,2,1,0:T(8,128)(2,1)} %bitcast.33, bf16[384,256]{1,0:T(8,128)(2,1)S(1)} %get-tuple-element.24.refs_0_, bf16[384,256]{1,0:T(8,128)(2,1)S(1)} %collective-permute-done.19.refs_1_), custom_call_target="tpu_custom_call" | custom-call | flops 805306368 | bytes 3145728 | tf_op jit(solution)/shard_map/backward/pallas_call | solution.py:216
  88.1 5.9 %backward.4.refs_3_ = f32[49,256,128]{2,1,0:T(8,128)S(1)} custom-call(s32[8]{0:T(128)S(1)} %stack.81.order, s32[24,16]{1,0:T(8,128)S(1)} %index.1, bf16[24,16,128,128]{3,2,1,0:T(8,128)(2,1)} %bitcast.34, bf16[384,256]{1,0:T(8,128)(2,1)S(1)} %collective-permute-done.13.refs_0_, ...), custom_call_target="tpu_custom_call", output_to_operand_aliasing={{}: (6, {})} | custom-call | flops 1207959552 | bytes 4718592 | tf_op jit(solution)/shard_map/backward/pallas_call | solution.py:216
  94.1 6.8 %backward.5 = (f32[49,256,128]{2,1,0:T(8,128)S(1)}, bf16[1536,256]{1,0:T(8,128)(2,1)S(1)}, bf16[384,256]{1,0:T(8,128)(2,1)S(1)}, bf16[384,256]{1,0:T(8,128)(2,1)...) custom-call(s32[8]{0:T(128)S(1)} %stack.81.order, ...), custom_call_target="tpu_custom_call", output_to_operand_aliasing={{0}: (6, {})} | custom-call | flops 1207959552 | bytes 4718592 | tf_op jit(solution)/shard_map/backward/pallas_call | solution.py:216
  101.4 2.0 %collective-permute-start.21 = (bf16[1152,256]{1,0:T(8,128)(2,1)S(1)}, bf16[1152,256]{1,0:T(8,128)(2,1)S(1)}, u32[]{:S(2)}, u32[]{:S(2)}) collective-permute-start(bf16[1152,256]{1,0:T(8,128)(2,1)S(1)} %get-tuple-element.27), channel_id=1, source_target_pairs={{0,16},{1,65},{2,18},{3,67},{4,20},{5,69},{6,22},{7,71},{8,24},{9,... | collective-permute-start | bytes 1769480 | tf_op jit(solution)/shard_map/ppermute | solution.py:33
  104.2 3.8 %collective-permute-start.33 = (bf16[272,256]{1,0:T(8,128)(2,1)S(1)}, bf16[272,256]{1,0:T(8,128)(2,1)S(1)}, u32[]{:S(2)}, u32[]{:S(2)}) collective-permute-start(bf16[272,256]{1,0:T(8,128)(2,1)S(1)} %shard_map.105.t0), channel_id=1, source_target_pairs={{0,16},{8,24},{16,0},{24,8},{32,48},{40,56},{48,32},{56,40},{64,80... | collective-permute-start | bytes 417800 | tf_op jit(solution)/shard_map/ppermute | solution.py:41
  108.0 3.9 %collective-permute-done.33.t2 = bf16[272,256]{1,0:T(8,128)(2,1)S(1)} collective-permute-done((bf16[272,256]{1,0:T(8,128)(2,1)S(1)}, bf16[272,256]{1,0:T(8,128)(2,1)S(1)}, u32[]{:S(2)}, u32[]{:S(2)}) %collective-permute-start.33) | collective-permute-done | bytes 139296 | tf_op jit(solution)/shard_map/ppermute | solution.py:41
  111.9 4.6 %collective-permute-done.34.t3 = bf16[272,256]{1,0:T(8,128)(2,1)S(1)} collective-permute-done((bf16[272,256]{1,0:T(8,128)(2,1)S(1)}, bf16[272,256]{1,0:T(8,128)(2,1)S(1)}, u32[]{:S(2)}, u32[]{:S(2)}) %collective-permute-start.34) | collective-permute-done | bytes 139296 | tf_op jit(solution)/shard_map/ppermute | solution.py:41
  117.3 2.5 %collective-permute-start.36 = (bf16[272,256]{1,0:T(8,128)(2,1)S(1)}, bf16[272,256]{1,0:T(8,128)(2,1)S(1)}, u32[]{:S(2)}, u32[]{:S(2)}) collective-permute-start(bf16[272,256]{1,0:T(8,128)(2,1)S(1)} %shard_map.106.t0), channel_id=1, source_target_pairs={{0,4},{1,5},{2,6},{3,7},{4,0},{5,1},{6,2},{7,3},{8,12},{9,13},{10,... | collective-permute-start | bytes 417800 | tf_op jit(solution)/shard_map/ppermute | solution.py:49
  119.8 2.3 %collective-permute-done.35.t1 = bf16[272,256]{1,0:T(8,128)(2,1)S(1)} collective-permute-done((bf16[272,256]{1,0:T(8,128)(2,1)S(1)}, bf16[272,256]{1,0:T(8,128)(2,1)S(1)}, u32[]{:S(2)}, u32[]{:S(2)}) %collective-permute-start.35) | collective-permute-done | bytes 139296 | tf_op jit(solution)/shard_map/ppermute | solution.py:49
  124.2 1.8 %collective-permute-done.37.t3 = bf16[272,256]{1,0:T(8,128)(2,1)S(1)} collective-permute-done((bf16[272,256]{1,0:T(8,128)(2,1)S(1)}, bf16[272,256]{1,0:T(8,128)(2,1)S(1)}, u32[]{:S(2)}, u32[]{:S(2)}) %collective-permute-start.37) | collective-permute-done | bytes 139296 | tf_op jit(solution)/shard_map/ppermute | solution.py:49
  126.1 11.6 %collective-permute-start.38 = (bf16[272,256]{1,0:T(8,128)(2,1)S(1)}, bf16[272,256]{1,0:T(8,128)(2,1)S(1)}, u32[]{:S(2)}, u32[]{:S(2)}) collective-permute-start(bf16[272,256]{1,0:T(8,128)(2,1)S(1)} %shard_map.107.t0), channel_id=1, source_target_pairs={{0,1},{1,0},{2,3},{3,2},{4,5},{5,4},{6,7},{7,6},{8,9},{9,8},{10,11... | collective-permute-start | bytes 417800 | tf_op jit(solution)/shard_map/ppermute | solution.py:49
  138.9 1.7 %collective-permute-start.28 = (bf16[384,256]{1,0:T(8,128)(2,1)S(1)}, bf16[384,256]{1,0:T(8,128)(2,1)S(1)}, u32[]{:S(2)}, u32[]{:S(2)}) collective-permute-start(bf16[384,256]{1,0:T(8,128)(2,1)S(1)} %get-tuple-element.34), channel_id=1, source_target_pairs={{0,24},{1,97},{2,26},{3,99},{4,28},{5,101},{6,30},{7,103},{8,0},{9... | collective-permute-start | bytes 589832 | tf_op jit(solution)/shard_map/ppermute | solution.py:33
  140.9 1.7 %collective-permute-start.23 = (bf16[384,256]{1,0:T(8,128)(2,1)S(1)}, bf16[384,256]{1,0:T(8,128)(2,1)S(1)}, u32[]{:S(2)}, u32[]{:S(2)}) collective-permute-start(bf16[384,256]{1,0:T(8,128)(2,1)S(1)} %get-tuple-element.29), channel_id=1, source_target_pairs={{0,32},{1,9},{2,34},{3,11},{4,36},{5,13},{6,38},{7,15},{8,40},{9,1... | collective-permute-start | bytes 589832 | tf_op jit(solution)/shard_map/ppermute | solution.py:33
  142.6 1.9 %collective-permute-start.24 = (bf16[384,256]{1,0:T(8,128)(2,1)S(1)}, bf16[384,256]{1,0:T(8,128)(2,1)S(1)}, u32[]{:S(2)}, u32[]{:S(2)}) collective-permute-start(bf16[384,256]{1,0:T(8,128)(2,1)S(1)} %get-tuple-element.30), channel_id=1, source_target_pairs={{0,64},{1,17},{2,66},{3,19},{4,68},{5,21},{6,70},{7,23},{8,72},{9,... | collective-permute-start | bytes 589832 | tf_op jit(solution)/shard_map/ppermute | solution.py:33
  144.6 2.0 %collective-permute-start.25 = (bf16[384,256]{1,0:T(8,128)(2,1)S(1)}, bf16[384,256]{1,0:T(8,128)(2,1)S(1)}, u32[]{:S(2)}, u32[]{:S(2)}) collective-permute-start(bf16[384,256]{1,0:T(8,128)(2,1)S(1)} %get-tuple-element.31), channel_id=1, source_target_pairs={{0,96},{1,25},{2,98},{3,27},{4,100},{5,29},{6,102},{7,31},{8,104},... | collective-permute-start | bytes 589832 | tf_op jit(solution)/shard_map/ppermute | solution.py:33
  147.3 2.6 %collective-permute-done.24.refs_1_ = bf16[384,256]{1,0:T(8,128)(2,1)S(1)} collective-permute-done((bf16[384,256]{1,0:T(8,128)(2,1)S(1)}, bf16[384,256]{1,0:T(8,128)(2,1)S(1)}, u32[]{:S(2)}, u32[]{:S(2)}) %collective-permute-start.24) | collective-permute-done | bytes 196640 | tf_op jit(solution)/shard_map/ppermute | solution.py:33
  (77 shorter events, 31.9 us)
Async XLA Ops:
  0.6 7.2 %collective-permute-start = (bf16[384,256]{1,0:T(8,128)(2,1)}, bf16[384,256]{1,0:T(8,128)(2,1)S(1)}, u32[]{:S(2)}, u32[]{:S(2)}) collective-permute-start(bf16[384,256]{1,0:T(8,128)(2,1)} %own.1), channel_id=1, source_target_pairs={{0,32},{1,9},{2,34},{3,11},{4,36},{5,13},{6,38},{7,15},{8,40},{9,1... | collective-permute-start | bytes 589832 | tf_op jit(solution)/shard_map/ppermute | solution.py:33
  2.8 8.3 %collective-permute-start.1 = (bf16[384,256]{1,0:T(8,128)(2,1)}, bf16[384,256]{1,0:T(8,128)(2,1)S(1)}, u32[]{:S(2)}, u32[]{:S(2)}) collective-permute-start(bf16[384,256]{1,0:T(8,128)(2,1)} %own.1), channel_id=1, source_target_pairs={{0,64},{1,17},{2,66},{3,19},{4,68},{5,21},{6,70},{7,23},{8,72},{9,... | collective-permute-start | bytes 589832 | tf_op jit(solution)/shard_map/ppermute | solution.py:33
  12.5 23.9 %collective-permute-start.6 = (bf16[1152,256]{1,0:T(8,128)(2,1)}, bf16[1152,256]{1,0:T(8,128)(2,1)S(1)}, u32[]{:S(2)}, u32[]{:S(2)}) collective-permute-start(bf16[1152,256]{1,0:T(8,128)(2,1)} %constant_dynamic-update-slice_fusion), channel_id=1, source_target_pairs={{0,8},{1,33},{2,10},{3,35},{4,12},{5,37},{6,14},{7,39},{8,16},{9,4... | collective-permute-start | bytes 1769480 | tf_op jit(solution)/shard_map/ppermute | solution.py:33
  13.4 23.0 %collective-permute-start.7 = (bf16[1152,256]{1,0:T(8,128)(2,1)}, bf16[1152,256]{1,0:T(8,128)(2,1)S(1)}, u32[]{:S(2)}, u32[]{:S(2)}) collective-permute-start(bf16[1152,256]{1,0:T(8,128)(2,1)} %constant_dynamic-update-slice_fusion), channel_id=1, source_target_pairs={{0,16},{1,65},{2,18},{3,67},{4,20},{5,69},{6,22},{7,71},{8,24},{9,... | collective-permute-start | bytes 1769480 | tf_op jit(solution)/shard_map/ppermute | solution.py:33
  15.9 20.5 %collective-permute-start.8 = (bf16[1152,256]{1,0:T(8,128)(2,1)}, bf16[1152,256]{1,0:T(8,128)(2,1)S(1)}, u32[]{:S(2)}, u32[]{:S(2)}) collective-permute-start(bf16[1152,256]{1,0:T(8,128)(2,1)} %constant_dynamic-update-slice_fusion), channel_id=1, source_target_pairs={{0,24},{1,97},{2,26},{3,99},{4,28},{5,101},{6,30},{7,103},{8,0},{9... | collective-permute-start | bytes 1769480 | tf_op jit(solution)/shard_map/ppermute | solution.py:33
  17.0 14.4 %collective-permute-start.3 = (bf16[384,256]{1,0:T(8,128)(2,1)}, bf16[384,256]{1,0:T(8,128)(2,1)S(1)}, u32[]{:S(2)}, u32[]{:S(2)}) collective-permute-start(bf16[384,256]{1,0:T(8,128)(2,1)} %own.1), channel_id=1, source_target_pairs={{0,8},{1,33},{2,10},{3,35},{4,12},{5,37},{6,14},{7,39},{8,16},{9,4... | collective-permute-start | bytes 589832 | tf_op jit(solution)/shard_map/ppermute | solution.py:33
  17.3 17.3 %collective-permute-start.4 = (bf16[384,256]{1,0:T(8,128)(2,1)}, bf16[384,256]{1,0:T(8,128)(2,1)S(1)}, u32[]{:S(2)}, u32[]{:S(2)}) collective-permute-start(bf16[384,256]{1,0:T(8,128)(2,1)} %own.1), channel_id=1, source_target_pairs={{0,16},{1,65},{2,18},{3,67},{4,20},{5,69},{6,22},{7,71},{8,24},{9,... | collective-permute-start | bytes 589832 | tf_op jit(solution)/shard_map/ppermute | solution.py:33
  43.1 7.9 %collective-permute-start.9 = (bf16[4,384,256]{2,1,0:T(8,128)(2,1)S(1)}, bf16[4,384,256]{2,1,0:T(8,128)(2,1)S(1)}, u32[]{:S(2)}, u32[]{:S(2)}) collective-permute-start(bf16[4,384,256]{2,1,0:T(8,128)(2,1)S(1)} %get-tuple-element.22), channel_id=1, source_target_pairs={{0,1},{1,0},{2,3},{3,2},{4,5},{5,4},{6,7},{7,6},{8,9},{9,8},{10,11... | collective-permute-start | bytes 2359304 | tf_op jit(solution)/shard_map/ppermute | solution.py:49
  51.1 9.1 %collective-permute-start.10 = (bf16[384,256]{1,0:T(8,128)(2,1)S(1)}, bf16[384,256]{1,0:T(8,128)(2,1)S(1)}, u32[]{:S(2)}, u32[]{:S(2)}) collective-permute-start(bf16[384,256]{1,0:T(8,128)(2,1)S(1)} %get-tuple-element.40), channel_id=1, source_target_pairs={{0,2},{1,3},{2,4},{3,5},{4,6},{5,7},{6,0},{7,1},{8,10},{9,11},{10,... | collective-permute-start | bytes 589832 | tf_op jit(solution)/shard_map/ppermute | solution.py:49
  52.8 12.5 %collective-permute-start.11 = (bf16[384,256]{1,0:T(8,128)(2,1)S(1)}, bf16[384,256]{1,0:T(8,128)(2,1)S(1)}, u32[]{:S(2)}, u32[]{:S(2)}) collective-permute-start(bf16[384,256]{1,0:T(8,128)(2,1)S(1)} %get-tuple-element.39), channel_id=1, source_target_pairs={{0,4},{1,5},{2,6},{3,7},{4,0},{5,1},{6,2},{7,3},{8,12},{9,13},{10,... | collective-permute-start | bytes 589832 | tf_op jit(solution)/shard_map/ppermute | solution.py:49
  56.1 9.2 %collective-permute-start.12 = (bf16[384,256]{1,0:T(8,128)(2,1)S(1)}, bf16[384,256]{1,0:T(8,128)(2,1)S(1)}, u32[]{:S(2)}, u32[]{:S(2)}) collective-permute-start(bf16[384,256]{1,0:T(8,128)(2,1)S(1)} %get-tuple-element.38), channel_id=1, source_target_pairs={{0,6},{1,7},{2,0},{3,1},{4,2},{5,3},{6,4},{7,5},{8,14},{9,15},{10,... | collective-permute-start | bytes 589832 | tf_op jit(solution)/shard_map/ppermute | solution.py:49
  66.4 6.5 %collective-permute-start.29 = (bf16[272,256]{1,0:T(8,128)(2,1)S(1)}, bf16[272,256]{1,0:T(8,128)(2,1)S(1)}, u32[]{:S(2)}, u32[]{:S(2)}) collective-permute-start(bf16[272,256]{1,0:T(8,128)(2,1)S(1)} %get-tuple-element.35.t0), channel_id=1, source_target_pairs={{0,32},{8,40},{16,48},{24,56},{32,64},{40,72},{48,80},{56,88},{64,... | collective-permute-start | bytes 417800 | tf_op jit(solution)/shard_map/ppermute | solution.py:41
  67.3 8.1 %collective-permute-start.30 = (bf16[272,256]{1,0:T(8,128)(2,1)S(1)}, bf16[272,256]{1,0:T(8,128)(2,1)S(1)}, u32[]{:S(2)}, u32[]{:S(2)}) collective-permute-start(bf16[272,256]{1,0:T(8,128)(2,1)S(1)} %get-tuple-element.35.t0), channel_id=1, source_target_pairs={{0,64},{8,72},{16,80},{24,88},{32,96},{40,104},{48,112},{56,120},{... | collective-permute-start | bytes 417800 | tf_op jit(solution)/shard_map/ppermute | solution.py:41
  69.1 7.6 %collective-permute-start.13 = (bf16[384,256]{1,0:T(8,128)(2,1)S(1)}, bf16[384,256]{1,0:T(8,128)(2,1)S(1)}, u32[]{:S(2)}, u32[]{:S(2)}) collective-permute-start(bf16[384,256]{1,0:T(8,128)(2,1)S(1)} %get-tuple-element.24.refs_0_), channel_id=1, source_target_pairs={{0,2},{1,3},{2,4},{3,5},{4,6},{5,7},{6,0},{7,1},{8,10},{9,11},{10,... | collective-permute-start | bytes 589832 | tf_op jit(solution)/shard_map/ppermute | solution.py:49
  70.1 10.6 %collective-permute-start.15 = (bf16[384,256]{1,0:T(8,128)(2,1)S(1)}, bf16[384,256]{1,0:T(8,128)(2,1)S(1)}, u32[]{:S(2)}, u32[]{:S(2)}) collective-permute-start(bf16[384,256]{1,0:T(8,128)(2,1)S(1)} %get-tuple-element.24.refs_0_), channel_id=1, source_target_pairs={{0,4},{1,5},{2,6},{3,7},{4,0},{5,1},{6,2},{7,3},{8,12},{9,13},{10,... | collective-permute-start | bytes 589832 | tf_op jit(solution)/shard_map/ppermute | solution.py:49
  72.6 10.1 %collective-permute-start.17 = (bf16[384,256]{1,0:T(8,128)(2,1)S(1)}, bf16[384,256]{1,0:T(8,128)(2,1)S(1)}, u32[]{:S(2)}, u32[]{:S(2)}) collective-permute-start(bf16[384,256]{1,0:T(8,128)(2,1)S(1)} %get-tuple-element.24.refs_0_), channel_id=1, source_target_pairs={{0,6},{1,7},{2,0},{3,1},{4,2},{5,3},{6,4},{7,5},{8,14},{9,15},{10,... | collective-permute-start | bytes 589832 | tf_op jit(solution)/shard_map/ppermute | solution.py:49
  72.9 10.3 %collective-permute-start.19 = (bf16[384,256]{1,0:T(8,128)(2,1)S(1)}, bf16[384,256]{1,0:T(8,128)(2,1)S(1)}, u32[]{:S(2)}, u32[]{:S(2)}) collective-permute-start(bf16[384,256]{1,0:T(8,128)(2,1)S(1)} %get-tuple-element.24.refs_0_), channel_id=1, source_target_pairs={{0,1},{1,0},{2,3},{3,2},{4,5},{5,4},{6,7},{7,6},{8,9},{9,8},{10,11... | collective-permute-start | bytes 589832 | tf_op jit(solution)/shard_map/ppermute | solution.py:49
  75.5 7.3 %collective-permute-start.31 = (bf16[272,256]{1,0:T(8,128)(2,1)S(1)}, bf16[272,256]{1,0:T(8,128)(2,1)S(1)}, u32[]{:S(2)}, u32[]{:S(2)}) collective-permute-start(bf16[272,256]{1,0:T(8,128)(2,1)S(1)} %get-tuple-element.35.t0), channel_id=1, source_target_pairs={{0,96},{8,104},{16,112},{24,120},{32,0},{40,8},{48,16},{56,24},{64... | collective-permute-start | bytes 417800 | tf_op jit(solution)/shard_map/ppermute | solution.py:41
  76.7 17.3 %collective-permute-start.14 = (bf16[384,256]{1,0:T(8,128)(2,1)S(1)}, bf16[384,256]{1,0:T(8,128)(2,1)S(1)}, u32[]{:S(2)}, u32[]{:S(2)}) collective-permute-start(bf16[384,256]{1,0:T(8,128)(2,1)S(1)} %collective-permute-done.13.refs_0_), channel_id=1, source_target_pairs={{0,1},{1,0},{2,3},{3,2},{4,5},{5,4},{6,7},{7,6},{8,9},{9,8},{10,11... | collective-permute-start | bytes 589832 | tf_op jit(solution)/shard_map/ppermute | solution.py:49
  80.7 13.3 %collective-permute-start.16 = (bf16[384,256]{1,0:T(8,128)(2,1)S(1)}, bf16[384,256]{1,0:T(8,128)(2,1)S(1)}, u32[]{:S(2)}, u32[]{:S(2)}) collective-permute-start(bf16[384,256]{1,0:T(8,128)(2,1)S(1)} %collective-permute-done.15.refs_1_), channel_id=1, source_target_pairs={{0,1},{1,0},{2,3},{3,2},{4,5},{5,4},{6,7},{7,6},{8,9},{9,8},{10,11... | collective-permute-start | bytes 589832 | tf_op jit(solution)/shard_map/ppermute | solution.py:49
  82.7 11.4 %collective-permute-start.18 = (bf16[384,256]{1,0:T(8,128)(2,1)S(1)}, bf16[384,256]{1,0:T(8,128)(2,1)S(1)}, u32[]{:S(2)}, u32[]{:S(2)}) collective-permute-start(bf16[384,256]{1,0:T(8,128)(2,1)S(1)} %collective-permute-done.17.refs_2_), channel_id=1, source_target_pairs={{0,1},{1,0},{2,3},{3,2},{4,5},{5,4},{6,7},{7,6},{8,9},{9,8},{10,11... | collective-permute-start | bytes 589832 | tf_op jit(solution)/shard_map/ppermute | solution.py:49
  82.8 25.2 %collective-permute-start.32 = (bf16[272,256]{1,0:T(8,128)(2,1)S(1)}, bf16[272,256]{1,0:T(8,128)(2,1)S(1)}, u32[]{:S(2)}, u32[]{:S(2)}) collective-permute-start(bf16[272,256]{1,0:T(8,128)(2,1)S(1)} %shard_map.105.t0), channel_id=1, source_target_pairs={{0,8},{8,16},{16,24},{24,0},{32,40},{40,48},{48,56},{56,32},{64,72... | collective-permute-start | bytes 417800 | tf_op jit(solution)/shard_map/ppermute | solution.py:41
  100.9 36.8 %collective-permute-start.20 = (bf16[1152,256]{1,0:T(8,128)(2,1)S(1)}, bf16[1152,256]{1,0:T(8,128)(2,1)S(1)}, u32[]{:S(2)}, u32[]{:S(2)}) collective-permute-start(bf16[1152,256]{1,0:T(8,128)(2,1)S(1)} %get-tuple-element.26), channel_id=1, source_target_pairs={{0,8},{1,33},{2,10},{3,35},{4,12},{5,37},{6,14},{7,39},{8,16},{9,4... | collective-permute-start | bytes 1769480 | tf_op jit(solution)/shard_map/ppermute | solution.py:33
  101.4 37.4 %collective-permute-start.21 = (bf16[1152,256]{1,0:T(8,128)(2,1)S(1)}, bf16[1152,256]{1,0:T(8,128)(2,1)S(1)}, u32[]{:S(2)}, u32[]{:S(2)}) collective-permute-start(bf16[1152,256]{1,0:T(8,128)(2,1)S(1)} %get-tuple-element.27), channel_id=1, source_target_pairs={{0,16},{1,65},{2,18},{3,67},{4,20},{5,69},{6,22},{7,71},{8,24},{9,... | collective-permute-start | bytes 1769480 | tf_op jit(solution)/shard_map/ppermute | solution.py:33
  103.4 37.2 %collective-permute-start.22 = (bf16[1152,256]{1,0:T(8,128)(2,1)S(1)}, bf16[1152,256]{1,0:T(8,128)(2,1)S(1)}, u32[]{:S(2)}, u32[]{:S(2)}) collective-permute-start(bf16[1152,256]{1,0:T(8,128)(2,1)S(1)} %get-tuple-element.28), channel_id=1, source_target_pairs={{0,24},{1,97},{2,26},{3,99},{4,28},{5,101},{6,30},{7,103},{8,0},{9... | collective-permute-start | bytes 1769480 | tf_op jit(solution)/shard_map/ppermute | solution.py:33
  104.2 7.8 %collective-permute-start.33 = (bf16[272,256]{1,0:T(8,128)(2,1)S(1)}, bf16[272,256]{1,0:T(8,128)(2,1)S(1)}, u32[]{:S(2)}, u32[]{:S(2)}) collective-permute-start(bf16[272,256]{1,0:T(8,128)(2,1)S(1)} %shard_map.105.t0), channel_id=1, source_target_pairs={{0,16},{8,24},{16,0},{24,8},{32,48},{40,56},{48,32},{56,40},{64,80... | collective-permute-start | bytes 417800 | tf_op jit(solution)/shard_map/ppermute | solution.py:41
  108.0 8.6 %collective-permute-start.34 = (bf16[272,256]{1,0:T(8,128)(2,1)S(1)}, bf16[272,256]{1,0:T(8,128)(2,1)S(1)}, u32[]{:S(2)}, u32[]{:S(2)}) collective-permute-start(bf16[272,256]{1,0:T(8,128)(2,1)S(1)} %shard_map.105.t0), channel_id=1, source_target_pairs={{0,24},{8,0},{16,8},{24,16},{32,56},{40,32},{48,40},{56,48},{64,88... | collective-permute-start | bytes 417800 | tf_op jit(solution)/shard_map/ppermute | solution.py:41
  123.7 20.8 %collective-permute-start.26 = (bf16[384,256]{1,0:T(8,128)(2,1)S(1)}, bf16[384,256]{1,0:T(8,128)(2,1)S(1)}, u32[]{:S(2)}, u32[]{:S(2)}) collective-permute-start(bf16[384,256]{1,0:T(8,128)(2,1)S(1)} %get-tuple-element.32), channel_id=1, source_target_pairs={{0,8},{1,33},{2,10},{3,35},{4,12},{5,37},{6,14},{7,39},{8,16},{9,4... | collective-permute-start | bytes 589832 | tf_op jit(solution)/shard_map/ppermute | solution.py:33
  126.1 16.5 %collective-permute-start.38 = (bf16[272,256]{1,0:T(8,128)(2,1)S(1)}, bf16[272,256]{1,0:T(8,128)(2,1)S(1)}, u32[]{:S(2)}, u32[]{:S(2)}) collective-permute-start(bf16[272,256]{1,0:T(8,128)(2,1)S(1)} %shard_map.107.t0), channel_id=1, source_target_pairs={{0,1},{1,0},{2,3},{3,2},{4,5},{5,4},{6,7},{7,6},{8,9},{9,8},{10,11... | collective-permute-start | bytes 417800 | tf_op jit(solution)/shard_map/ppermute | solution.py:49
  137.7 9.6 %collective-permute-start.27 = (bf16[384,256]{1,0:T(8,128)(2,1)S(1)}, bf16[384,256]{1,0:T(8,128)(2,1)S(1)}, u32[]{:S(2)}, u32[]{:S(2)}) collective-permute-start(bf16[384,256]{1,0:T(8,128)(2,1)S(1)} %get-tuple-element.33), channel_id=1, source_target_pairs={{0,16},{1,65},{2,18},{3,67},{4,20},{5,69},{6,22},{7,71},{8,24},{9,... | collective-permute-start | bytes 589832 | tf_op jit(solution)/shard_map/ppermute | solution.py:33
  138.9 8.4 %collective-permute-start.28 = (bf16[384,256]{1,0:T(8,128)(2,1)S(1)}, bf16[384,256]{1,0:T(8,128)(2,1)S(1)}, u32[]{:S(2)}, u32[]{:S(2)}) collective-permute-start(bf16[384,256]{1,0:T(8,128)(2,1)S(1)} %get-tuple-element.34), channel_id=1, source_target_pairs={{0,24},{1,97},{2,26},{3,99},{4,28},{5,101},{6,30},{7,103},{8,0},{9... | collective-permute-start | bytes 589832 | tf_op jit(solution)/shard_map/ppermute | solution.py:33
  142.6 7.3 %collective-permute-start.24 = (bf16[384,256]{1,0:T(8,128)(2,1)S(1)}, bf16[384,256]{1,0:T(8,128)(2,1)S(1)}, u32[]{:S(2)}, u32[]{:S(2)}) collective-permute-start(bf16[384,256]{1,0:T(8,128)(2,1)S(1)} %get-tuple-element.30), channel_id=1, source_target_pairs={{0,64},{1,17},{2,66},{3,19},{4,68},{5,21},{6,70},{7,23},{8,72},{9,... | collective-permute-start | bytes 589832 | tf_op jit(solution)/shard_map/ppermute | solution.py:33
  (11 other events, 68.4 us)

commit v2 on v1

v2 whole, which is shorter than its diff:
```python
import functools

import jax
import jax.numpy as jnp
from jax import lax
from jax.experimental import pallas as pl
from jax.experimental.pallas import tpu as pltpu
from jax.sharding import PartitionSpec as P


TILE = 128
SLOTS = 16
SIDE = 4
ND = 384
PER = ND // TILE
DUMMY = SIDE * SIDE * PER
BROWS = 16
BF = jnp.bfloat16
F32 = jnp.float32
VM = pl.BlockSpec(memory_space=pltpu.VMEM)
SM = pl.BlockSpec(memory_space=pltpu.SMEM)


def send_plane(value, first, step):
    pairs = []
    for row in range(SIDE * SIDE):
        for col in range(2 * SIDE):
            x, y = divmod(row, SIDE)
            if (col % 2 == 0) == first:
                x = (x + step) % SIDE
            else:
                y = (y + step) % SIDE
            pairs.append((row * 2 * SIDE + col, (x * SIDE + y) * 2 * SIDE + col))
    return lax.ppermute(value, ("row", "col"), pairs)


def trade_row(value, bit, along_x):
    pairs = []
    for x in range(SIDE):
        for y in range(SIDE):
            there = ((x ^ bit), y) if along_x else (x, (y ^ bit))
            pairs.append((x * SIDE + y, there[0] * SIDE + there[1]))
    return lax.ppermute(value, "row", pairs)


def send_col(value, dz, dk):
    pairs = []
    for z in range(SIDE):
        for k in range(2):
            pairs.append((z * 2 + k, (z + dz) % SIDE * 2 + (k ^ dk)))
    return lax.ppermute(value, "col", pairs)


def rel(first, second):
    return (second % SIDE) * SIDE + first % SIDE


def params(mb):
    return pltpu.CompilerParams(vmem_limit_bytes=mb * 1024 * 1024)


def cost(flops, data):
    return pl.CostEstimate(flops=flops, bytes_accessed=data, transcendentals=0)


def sum4(a, b, c, d):
    return (a + c) + (b + d)


def pack_bias(total):
    hi = total.astype(BF)
    lo = (total - hi.astype(F32)).astype(BF)
    rows = lax.broadcasted_iota(jnp.int32, (BROWS, total.shape[1]), 0)
    zero = jnp.zeros((BROWS, total.shape[1]), F32)
    return jnp.where(rows == 0, hi.astype(F32), jnp.where(rows == 1, lo.astype(F32), zero)).astype(BF)


def mark_kernel(out):
    out[...] = jnp.zeros_like(out)


def join_kernel(*refs):
    for n, ref in enumerate(refs[:-1]):
        refs[-1][n * ND:(n + 1) * ND, :] = ref[...]


def load_kernel(source, out, sems):
    parts = sems.shape[0]
    chunk = source.shape[0] // parts
    copies = []
    for n in range(parts):
        part = pl.ds(n * chunk, chunk)
        copies.append(pltpu.make_async_copy(source.at[part], out.at[part], sems.at[n]))
    for n in range(parts + 2):
        if n < parts:
            copies[n].start()
        if n >= 2:
            copies[n - 2].wait()


def index_kernel(place, cols, counts, mark, out):
    column = cols[...]
    source = (column * 43) >> 7
    away_x = (place[0] - (source >> 2)) & (SIDE - 1)
    away_y = (place[1] - source) & (SIDE - 1)
    distance = jnp.where(place[2] == 0, away_y * SIDE + away_x, away_x * SIDE + away_y)
    live = lax.broadcasted_iota(jnp.int32, column.shape, 1) < counts[...]
    out[...] = jnp.where(live, distance * PER + (column - source * PER), DUMMY) + mark[0:1, 0:1]


def forward_steps(offset, steps, order, index, adj, panel, out):
    def body(step, carry):
        for i in range(PER):
            tile_row = order[step + offset] * PER + i
            total = None
            for pair in range(SLOTS // 2):
                picked = []
                for half in range(2):
                    start = pl.multiple_of(index[tile_row, 2 * pair + half] * TILE, TILE)
                    picked.append(panel[pl.ds(start, TILE), :])
                left = jnp.concatenate([adj[tile_row, 2 * pair], adj[tile_row, 2 * pair + 1]], axis=1)
                product = jnp.dot(left, jnp.concatenate(picked, axis=0), preferred_element_type=F32)
                total = product if total is None else total + product
            out[step, i * TILE:(i + 1) * TILE, :] = total.astype(BF)
        return carry

    lax.fori_loop(0, steps, body, 0)


def forward_first_kernel(offset, steps, order, index, adj, own, f1, f2, f3, s1, s2, s3, m1, m2, m3, out, panel):
    panel[0:ND, :] = own[...]
    for a, ref in enumerate((f1, f2, f3)):
        panel[rel(a + 1, 0) * ND:(rel(a + 1, 0) + 1) * ND, :] = ref[...]
    for b, (side, many) in enumerate(((s1, m1), (s2, m2), (s3, m3))):
        start = rel(0, b + 1) * ND
        panel[start:start + ND, :] = side[...]
        panel[start + ND:start + SIDE * ND, :] = many[...]
    panel[DUMMY * TILE:, :] = jnp.zeros((TILE, panel.shape[1]), BF)
    forward_steps(offset, steps, order, index, adj, panel, out)


def forward(offset, steps, order, index, adj, operands):
    width = operands[0].shape[1]
    first = len(operands) > 1
    shape = jax.ShapeDtypeStruct((steps, ND, width), BF)
    panel = jax.ShapeDtypeStruct(((DUMMY + 1) * TILE, width), BF)
    return pl.pallas_call(
        functools.partial(forward_first_kernel if first else forward_steps, offset, steps),
        out_shape=(shape, panel) if first else shape,
        in_specs=[SM, SM] + [VM] * (1 + len(operands)),
        out_specs=(VM, VM) if first else VM,
        compiler_params=params(6),
        cost_estimate=cost(steps * PER * SLOTS * 2 * TILE * TILE * width, steps * PER * SLOTS * TILE * TILE * 2),
    )(order, index, adj, *operands)


def activation_kernel(keep, recv, r1, r2, r3, weight, bias, cot, act, grad_out, terms):
    agg = keep[1].astype(F32) + recv[...].astype(F32)
    for ref in (r1, r2, r3):
        agg = agg + ref[...].astype(F32)
    agg16 = agg.astype(BF)
    pre = jnp.dot(agg16, weight[...], preferred_element_type=F32) + bias[...]
    sig = 1.0 / (1.0 + jnp.exp(-pre))
    act[...] = (pre * sig).astype(BF)
    grad = (cot[...].astype(F32) * sig * (1.0 + pre * (1.0 - sig))).astype(BF)
    grad_out[...] = grad
    wrows = terms.shape[0] - BROWS
    terms[0:wrows, :] = lax.dot_general(
        agg16, grad, (((0,), (0,)), ((), ())), preferred_element_type=F32
    ).astype(BF)
    terms[wrows:, :] = pack_bias(jnp.sum(grad.astype(F32), axis=0, keepdims=True))


def backward_kernel(offset, count, initial, final, order, index, adj, *refs):
    sources, refs = refs[:count], refs[count:]
    if not initial:
        refs = refs[1:]
    acc, refs = refs[0], refs[1:]
    if final:
        own, sides, many = refs[0], refs[1:SIDE], refs[SIDE:2 * SIDE - 1]
    turned, tiles, sems = refs[-3:]

    def fetch(step):
        rows = pl.ds(order[step + offset] * PER, PER)
        return pltpu.make_async_copy(adj.at[rows], tiles.at[step], sems.at[step])

    for step in range(count):
        fetch(step).start()
    for s, ref in enumerate(sources):
        for i in range(PER):
            turned[s * PER + i] = ref[i * TILE:(i + 1) * TILE, :].T
    if initial:
        acc[...] = jnp.zeros_like(acc)

    def body(step, carry):
        fetch(step).wait()
        for i in range(PER):
            tile_row = order[step + offset] * PER + i
            left = turned[step * PER + i]
            for slot in range(SLOTS):
                product = jnp.dot(left, tiles[step, i, slot], preferred_element_type=F32)
                place = index[tile_row, slot]
                acc[place] = acc[place] + product
        return carry

    lax.fori_loop(0, count, body, 0)

    if final:
        for b in (1, 2, 3, 0):
            for a in range(SIDE):
                if b == 0:
                    out, start = own, a * ND
                elif a == 0:
                    out, start = sides[b - 1], 0
                else:
                    out, start = many[b - 1], (a - 1) * ND
                for n in range(PER):
                    row = start + n * TILE
                    out[row:row + TILE, :] = acc[rel(-a, -b) * PER + n].astype(BF).T


def backward(offset, order, index, adj, sources, acc=None, final=False):
    width = sources[0].shape[1]
    count = len(sources)
    state = jax.ShapeDtypeStruct((DUMMY + 1, width, TILE), F32)
    outs = (state,)
    if final:
        outs += tuple(jax.ShapeDtypeStruct((n * ND, width), BF) for n in (SIDE, 1, 1, 1, 3, 3, 3))
    initial = acc is None
    extra = [] if initial else [acc]
    return pl.pallas_call(
        functools.partial(backward_kernel, offset, count, initial, final),
        out_shape=outs,
        in_specs=[SM, SM, pl.BlockSpec(memory_space=pltpu.HBM)] + [VM] * (count + len(extra)),
        out_specs=[VM] * len(outs),
        scratch_shapes=[
            pltpu.VMEM((count * PER, width, TILE), BF),
            pltpu.VMEM((count, PER, SLOTS, TILE, TILE), BF),
            pltpu.SemaphoreType.DMA((count,)),
        ],
        input_output_aliases={} if initial else {3 + count: 0},
        compiler_params=params(8),
        cost_estimate=cost(count * PER * SLOTS * 2 * TILE * TILE * width, count * PER * SLOTS * TILE * TILE * 2),
    )(order, index, adj, *sources, *extra)


def add_terms_kernel(*refs):
    terms, out = [ref[...].astype(F32) for ref in refs[:-1]], refs[-1]
    total = sum4(*terms) if len(terms) == SIDE else terms[0] + terms[1]
    wrows = out.shape[0] - BROWS
    out[0:wrows, :] = total[:wrows].astype(BF)
    out[wrows:, :] = pack_bias(jnp.sum(total[wrows:], axis=0, keepdims=True))


def last_terms_kernel(scale, t0, t1, wout, bout):
    total = t0[...].astype(F32) + t1[...].astype(F32)
    wrows = wout.shape[0]
    wout[...] = total[:wrows] * scale
    bout[...] = jnp.sum(total[wrows:], axis=0, keepdims=True) * scale


def small(kernel, outs, operands):
    return pl.pallas_call(
        kernel,
        out_shape=outs,
        in_specs=[VM] * len(operands),
        out_specs=jax.tree.map(lambda _: VM, outs),
        compiler_params=params(8),
    )(*operands)


def relay_kernel(own, r1, r2, r3, *outs):
    for a, out in enumerate(outs):
        total = own[(a + 1) * ND:(a + 2) * ND, :].astype(F32)
        for ref in (r1, r2, r3):
            total = total + ref[a * ND:(a + 1) * ND, :].astype(F32)
        out[...] = total.astype(BF)


def finish_kernel(own, *refs):
    weight, gfeat = refs[-2:]
    total = own[0:ND, :].astype(F32)
    for ref in refs[:-2]:
        total = total + ref[...].astype(F32)
    gfeat[...] = lax.dot_general(
        total.astype(BF), weight[...], (((1,), (1,)), ((), ())), preferred_element_type=F32
    ).astype(BF)


def shards(features, weight, out_bias, cotangent, adj_tiles, tile_cols, tile_counts):
    row = lax.axis_index("row")
    col = lax.axis_index("col")
    x, y, z, k = row // SIDE, row % SIDE, col // 2, col % 2
    width = features.shape[1]
    tile_rows = adj_tiles.shape[2]
    adj = pltpu.with_memory_space_constraint(adj_tiles.reshape(tile_rows, SLOTS, TILE, TILE), pltpu.HBM)
    mark = small(mark_kernel, jax.ShapeDtypeStruct((8, 128), jnp.int32), [])
    place = jnp.stack([x, y, k]).astype(jnp.int32)
    index = pl.pallas_call(
        index_kernel,
        out_shape=jax.ShapeDtypeStruct((tile_rows, SLOTS), jnp.int32),
        in_specs=[SM, VM, VM, VM],
        out_specs=VM,
        compiler_params=params(1),
    )(place, tile_cols.reshape(tile_rows, SLOTS), tile_counts.reshape(tile_rows, 1), mark)
    held = pl.pallas_call(
        load_kernel,
        out_shape=jax.ShapeDtypeStruct(adj.shape, adj.dtype),
        in_specs=[pl.BlockSpec(memory_space=pltpu.HBM)],
        out_specs=VM,
        scratch_shapes=[pltpu.SemaphoreType.DMA((12,))],
        compiler_params=params(1),
    )(adj)
    other = 1 - k
    onward = [(z + d) % SIDE * 2 for d in range(SIDE)]
    back = [(z - d) % SIDE * 2 for d in range(SIDE)]
    order_forward = jnp.stack(
        [v + other for v in onward[1:]] + [v + k for v in onward[1:]] + [onward[0] + other, onward[0] + k]
    ).astype(jnp.int32)
    order_backward = jnp.stack(
        [back[0] + k, back[0] + other] + [v + k for v in back[1:]] + [v + other for v in back[1:]]
    ).astype(jnp.int32)

    def fan(send, values):
        received = []
        for d in (1, 2, 3):
            received.append(send(values[d - 1], d))
        return received

    first = fan(lambda v, d: send_plane(v, True, d), [features] * 3)
    side = fan(lambda v, d: send_plane(v, False, d), [features] * 3)
    line = small(join_kernel, jax.ShapeDtypeStruct((3 * ND, width), BF), first)
    many = fan(lambda v, d: send_plane(v, False, d), [line] * 3)
    swap, panel = forward(0, 3, order_forward, index, held, [features, *first, *side, *many])

    recv = send_col(swap, 0, 1)
    away = forward(3, 3, order_forward, index, held, [panel])
    messages = [(away[d].astype(F32) + recv[d].astype(F32)).astype(BF) for d in range(3)]
    parts = fan(lambda v, d: send_col(v, d, 0), messages)
    keep = forward(6, 2, order_forward, index, held, [panel])
    recv = send_col(keep[0], 0, 1)
    block = jax.ShapeDtypeStruct((ND, width), BF)
    terms = jax.ShapeDtypeStruct((width + BROWS, width), BF)
    activated, grad, along = small(
        activation_kernel,
        (block, block, terms),
        [keep, recv, *parts, weight, out_bias.reshape(1, -1), cotangent],
    )

    mine = [grad] + fan(lambda v, d: send_col(v, d, 0), [grad] * 3)
    theirs = [send_col(grad, 0, 1)]
    theirs += fan(lambda v, d: send_col(v, 0, 1), mine[1:])
    other_terms = trade_row(along, 1, True)
    acc, = backward(0, order_backward, index, adj, [mine[0], theirs[0]])
    along = small(add_terms_kernel, terms, [along, other_terms])
    other_terms = trade_row(along, 2, True)
    acc, = backward(2, order_backward, index, adj, mine[1:], acc)
    along = small(add_terms_kernel, terms, [along, other_terms])
    other_terms = trade_row(along, 1, False)
    acc, own, *blocks = backward(SIDE + 1, order_backward, index, adj, theirs[1:], acc, final=True)

    landed = fan(lambda v, d: send_plane(v, False, d), blocks[3:])
    beside = fan(lambda v, d: send_plane(v, False, d), blocks[:3])
    along = small(add_terms_kernel, terms, [along, other_terms])
    along_z = [along] + fan(lambda v, d: send_col(v, d, 0), [along] * 3)
    along = small(add_terms_kernel, terms, along_z)
    other_terms = send_col(along, 0, 1)
    along = small(add_terms_kernel, terms, [along, other_terms])
    other_terms = trade_row(along, 2, False)
    nodes = features.shape[0] * lax.axis_size("row") * lax.axis_size("col")
    grad_weight, grad_bias = small(
        functools.partial(last_terms_kernel, nodes**-0.5),
        (jax.ShapeDtypeStruct((width, width), F32), jax.ShapeDtypeStruct((1, width), F32)),
        [along, other_terms],
    )
    onwards = small(relay_kernel, (block,) * 3, [own, *landed])
    last = fan(lambda v, d: send_plane(v, True, d), onwards)
    grad_features = small(finish_kernel, block, [own, *last, *beside, weight])
    return activated, grad_features, grad_weight, grad_bias.reshape(-1)


def solution(mesh):
    in_specs = (
        P(("row", "col"), None),
        P(),
        P(),
        P(("row", "col"), None),
        P("row", "col", None, None, None, None),
        P("row", "col", None, None),
        P("row", "col", None),
    )
    out_specs = (P(("row", "col"), None), P(("row", "col"), None), P(), P())

    return jax.shard_map(shards, mesh=mesh, in_specs=in_specs, out_specs=out_specs, check_vma=False)
```

time: 153 us -> 151 us (0.987)
  starting transfers between devices: 67.2 us -> 45.3 us
  waiting for transfers between devices: 44.1 us -> 55.4 us
  local copies, waits for them, and re-layouts: 4.67 us -> 13.5 us
    ppermute x15 -> x16, starting transfers between devices: 34.1 us -> 18.7 us  [send_col(): return lax.ppermute(value, 'col', pairs)]
    ppermute x15 -> x16, waiting for transfers between devices: 13.1 us -> 28 us  [send_col(): return lax.ppermute(value, 'col', pairs)]
    unnamed x11 -> x23, local copies, waits for them, and re-layouts: 3.07 us -> 11.9 us
    ppermute x6 -> x4, waiting for transfers between devices: 8.58 us -> 0.01 us  [trade_row(): return lax.ppermute(value, 'row', pairs)]
    ppermute x18, waiting for transfers between devices: 22.4 us -> 27.4 us  [send_plane(): return lax.ppermute(value, ('row', 'col'), pairs)]
    ppermute x6 -> x4, starting transfers between devices: 8.25 us -> 4.93 us  [trade_row(): return lax.ppermute(value, 'row', pairs)]
    ppermute x18, starting transfers between devices: 24.9 us -> 21.6 us  [send_plane(): return lax.ppermute(value, ('row', 'col'), pairs)]
    pallas_call x3, Pallas kernels: 17.6 us -> 15.4 us  [backward(): pl.pallas_call(functools.partial(backward_kernel, offset, count, initial,...]
  transfers between devices with their start and end apart: 39 -> 38, of which waited for: 14 -> 14; matrix products, arithmetic and copies ran while one was open for 2% -> 2% of each run, Pallas kernels for 18% -> 19%
where the time goes in v2:
time: 151 us; the launch traced here: 149 us
  waiting for transfers between devices  55.4 us (37%)
  starting transfers between devices  45.3 us (30%)
  Pallas kernels  33.3 us (22%)
  local copies, waits for them, and re-layouts  13.5 us (9%)
    ppermute x16, waiting for transfers between devices, send_col(): return lax.ppermute(value, 'col', pairs)  28 us
    ppermute x18, waiting for transfers between devices, send_plane(): return lax.ppermute(value, ('row', 'col'), pairs)  27.4 us
    ppermute x18, starting transfers between devices, send_plane(): return lax.ppermute(value, ('row', 'col'), pairs)  21.6 us
    ppermute x16, starting transfers between devices, send_col(): return lax.ppermute(value, 'col', pairs)  18.7 us
    pallas_call x3, Pallas kernels, backward(): pl.pallas_call(functools.partial(backward_kernel, offset, count, initial,...  15.4 us
    unnamed x23, local copies, waits for them, and re-layouts  11.9 us
    pallas_call x3, Pallas kernels, forward(): pl.pallas_call(functools.partial(forward_first_kernel if first else forwa...  7.79 us
    pallas_call x1, Pallas kernels, shards(): pl.pallas_call(load_kernel, out_shape=jax.ShapeDtypeStruct(adj.shape, adj...  6.1 us
  transfers between devices with their start and end apart: 38, of which 14 were waited for; matrix products, arithmetic and copies ran while one was open for 2% of the time, Pallas kernels for 19%

profile of v2, /device:TPU:1, one launch (start us, length us, event | category | flops | bytes accessed | tf_op | source)
XLA Modules:
  0.0 148.5 jit_solution(1151275084530235022)
XLA Ops:
  0.6 3.6 %collective-permute-start.2 = (bf16[384,256]{1,0:T(8,128)(2,1)}, bf16[384,256]{1,0:T(8,128)(2,1)S(1)}, u32[]{:S(2)}, u32[]{:S(2)}) collective-permute-start(bf16[384,256]{1,0:T(8,128)(2,1)} %own.1), channel_id=1, source_target_pairs={{0,96},{1,25},{2,98},{3,27},{4,100},{5,29},{6,102},{7,31},{8,104},... | collective-permute-start | bytes 589832 | tf_op jit(solution)/shard_map/ppermute | solution.py:34
  5.3 4.0 %collective-permute-done.2.refs_2_.f3 = bf16[384,256]{1,0:T(8,128)(2,1)S(1)} collective-permute-done((bf16[384,256]{1,0:T(8,128)(2,1)}, bf16[384,256]{1,0:T(8,128)(2,1)S(1)}, u32[]{:S(2)}, u32[]{:S(2)}) %collective-permute-start.2) | collective-permute-done | bytes 196640 | tf_op jit(solution)/shard_map/ppermute | solution.py:34
  10.8 2.1 %collective-permute-done.refs_0_.f1 = bf16[384,256]{1,0:T(8,128)(2,1)S(1)} collective-permute-done((bf16[384,256]{1,0:T(8,128)(2,1)}, bf16[384,256]{1,0:T(8,128)(2,1)S(1)}, u32[]{:S(2)}, u32[]{:S(2)}) %collective-permute-start) | collective-permute-done | bytes 196640 | tf_op jit(solution)/shard_map/ppermute | solution.py:34
  12.9 2.3 %collective-permute-start.8 = (bf16[1152,256]{1,0:T(8,128)(2,1)S(1)}, bf16[1152,256]{1,0:T(8,128)(2,1)S(1)}, u32[]{:S(2)}, u32[]{:S(2)}) collective-permute-start(bf16[1152,256]{1,0:T(8,128)(2,1)S(1)} %shard_map.105), channel_id=1, source_target_pairs={{0,24},{1,97},{2,26},{3,99},{4,28},{5,101},{6,30},{7,103},{8,0},{9... | collective-permute-start | bytes 1769480 | tf_op jit(solution)/shard_map/ppermute | solution.py:34
  16.3 1.8 %collective-permute-start.4 = (bf16[384,256]{1,0:T(8,128)(2,1)}, bf16[384,256]{1,0:T(8,128)(2,1)S(1)}, u32[]{:S(2)}, u32[]{:S(2)}) collective-permute-start(bf16[384,256]{1,0:T(8,128)(2,1)} %own.1), channel_id=1, source_target_pairs={{0,16},{1,65},{2,18},{3,67},{4,20},{5,69},{6,22},{7,71},{8,24},{9,... | collective-permute-start | bytes 589832 | tf_op jit(solution)/shard_map/ppermute | solution.py:34
  19.0 15.0 %collective-permute-done.4.s2 = bf16[384,256]{1,0:T(8,128)(2,1)S(1)} collective-permute-done((bf16[384,256]{1,0:T(8,128)(2,1)}, bf16[384,256]{1,0:T(8,128)(2,1)S(1)}, u32[]{:S(2)}, u32[]{:S(2)}) %collective-permute-start.4) | collective-permute-done | bytes 196640 | tf_op jit(solution)/shard_map/ppermute | solution.py:34
  36.7 6.1 %shard_map.104.adj = bf16[24,16,128,128]{3,2,1,0:T(8,128)(2,1)S(1)} custom-call(bf16[24,16,128,128]{3,2,1,0:T(8,128)(2,1)} %bitcast.34), custom_call_target="tpu_custom_call" | custom-call | tf_op jit(solution)/shard_map/pallas_call | solution.py:306
  42.8 4.6 %copy-done = bf16[24,16,128,128]{3,2,1,0:T(8,128)(2,1)} copy-done((bf16[24,16,128,128]{3,2,1,0:T(8,128)(2,1)}, bf16[24,16,128,128]{3,2,1,0:T(8,128)(2,1)S(1)}, u32[]{:S(2)}) %copy-start) | copy-done | bytes 12582936
  49.6 4.6 %copy-done.1 = bf16[24,16,128,128]{3,2,1,0:T(8,128)(2,1)S(1)} copy-done((bf16[24,16,128,128]{3,2,1,0:T(8,128)(2,1)S(1)}, bf16[24,16,128,128]{3,2,1,0:T(8,128)(2,1)}, u32[]{:S(2)}) %copy-start.1) | copy-done | bytes 12582936
  54.2 3.2 %shard_map.106 = (bf16[3,384,256]{2,1,0:T(8,128)(2,1)S(1)}, bf16[6272,256]{1,0:T(8,128)(2,1)S(1)}) custom-call(s32[8]{0:T(128)S(1)} %stack.70.order, s32[24,16]{1,0:T(8,128)S(1)} %shard_map.103.index, bf16[24,16,128,128]{3,2,1,0:T(8,128)(2,1)S(1)} %copy-done.1, bf16[384,256]{1,0:T(8,128)(2,1)S(1)} %copy-done.3, ...), custom_call_target="tpu_custom_call" | custom-call | flops 1207959552 | bytes 4718592 | tf_op jit(solution)/shard_map/pallas_call | solution.py:147
  57.4 3.6 %collective-permute-start.10 = (bf16[3,384,256]{2,1,0:T(8,128)(2,1)S(1)}, bf16[3,384,256]{2,1,0:T(8,128)(2,1)S(1)}, u32[]{:S(2)}, u32[]{:S(2)}) collective-permute-start(bf16[3,384,256]{2,1,0:T(8,128)(2,1)S(1)} %get-tuple-element.22), channel_id=1, source_target_pairs={{0,1},{1,0},{2,3},{3,2},{4,5},{5,4},{6,7},{7,6},{8,9},{9,8},{10,11... | collective-permute-start | bytes 1769480 | tf_op jit(solution)/shard_map/ppermute | solution.py:51
  61.0 2.0 %shard_map.107.keep = bf16[2,384,256]{2,1,0:T(8,128)(2,1)S(1)} custom-call(s32[8]{0:T(128)S(1)} %stack.70.order, s32[24,16]{1,0:T(8,128)S(1)} %shard_map.103.index, bf16[24,16,128,128]{3,2,1,0:T(8,128)(2,1)S(1)} %copy-done.1, bf16[6272,256]{1,0:T(8,128)(2,1)S(1)} %get-tuple-element.21.panel), custom_call_target="tpu_custom_call" | custom-call | flops 805306368 | bytes 3145728 | tf_op jit(solution)/shard_map/pallas_call | solution.py:147
  63.2 2.6 %shard_map.108 = bf16[3,384,256]{2,1,0:T(8,128)(2,1)S(1)} custom-call(s32[8]{0:T(128)S(1)} %stack.70.order, s32[24,16]{1,0:T(8,128)S(1)} %shard_map.103.index, bf16[24,16,128,128]{3,2,1,0:T(8,128)(2,1)S(1)} %bitcast.31, bf16[6272,256]{1,0:T(8,128)(2,1)S(1)} %get-tuple-element.21.panel), custom_call_target="tpu_custom_call" | custom-call | flops 1207959552 | bytes 4718592 | tf_op jit(solution)/shard_map/pallas_call | solution.py:147
  66.0 3.8 %collective-permute-start.13 = (bf16[384,256]{1,0:T(8,128)(2,1)S(1)}, bf16[384,256]{1,0:T(8,128)(2,1)S(1)}, u32[]{:S(2)}, u32[]{:S(2)}) collective-permute-start(bf16[384,256]{1,0:T(8,128)(2,1)S(1)} %get-tuple-element.38), channel_id=1, source_target_pairs={{0,6},{1,7},{2,0},{3,1},{4,2},{5,3},{6,4},{7,5},{8,14},{9,15},{10,... | collective-permute-start | bytes 589832 | tf_op jit(solution)/shard_map/ppermute | solution.py:51
  70.5 7.2 %collective-permute-done.13.r3 = bf16[384,256]{1,0:T(8,128)(2,1)S(1)} collective-permute-done((bf16[384,256]{1,0:T(8,128)(2,1)S(1)}, bf16[384,256]{1,0:T(8,128)(2,1)S(1)}, u32[]{:S(2)}, u32[]{:S(2)}) %collective-permute-start.13) | collective-permute-done | bytes 196640 | tf_op jit(solution)/shard_map/ppermute | solution.py:51
  77.7 4.1 %collective-permute-done.11.r1 = bf16[384,256]{1,0:T(8,128)(2,1)S(1)} collective-permute-done((bf16[384,256]{1,0:T(8,128)(2,1)S(1)}, bf16[384,256]{1,0:T(8,128)(2,1)S(1)}, u32[]{:S(2)}, u32[]{:S(2)}) %collective-permute-start.11) | collective-permute-done | bytes 196640 | tf_op jit(solution)/shard_map/ppermute | solution.py:51
  85.7 2.9 %collective-permute-done.18.refs_2_ = bf16[384,256]{1,0:T(8,128)(2,1)S(1)} collective-permute-done((bf16[384,256]{1,0:T(8,128)(2,1)S(1)}, bf16[384,256]{1,0:T(8,128)(2,1)S(1)}, u32[]{:S(2)}, u32[]{:S(2)}) %collective-permute-start.18) | collective-permute-done | bytes 196640 | tf_op jit(solution)/shard_map/ppermute | solution.py:51
  88.5 2.9 %collective-permute-start.19 = (bf16[384,256]{1,0:T(8,128)(2,1)S(1)}, bf16[384,256]{1,0:T(8,128)(2,1)S(1)}, u32[]{:S(2)}, u32[]{:S(2)}) collective-permute-start(bf16[384,256]{1,0:T(8,128)(2,1)S(1)} %collective-permute-done.18.refs_2_), channel_id=1, source_target_pairs={{0,1},{1,0},{2,3},{3,2},{4,5},{5,4},{6,7},{7,6},{8,9},{9,8},{10,11... | collective-permute-start | bytes 589832 | tf_op jit(solution)/shard_map/ppermute | solution.py:51
  91.4 2.4 %collective-permute-start.17 = (bf16[384,256]{1,0:T(8,128)(2,1)S(1)}, bf16[384,256]{1,0:T(8,128)(2,1)S(1)}, u32[]{:S(2)}, u32[]{:S(2)}) collective-permute-start(bf16[384,256]{1,0:T(8,128)(2,1)S(1)} %collective-permute-done.16.refs_1_), channel_id=1, source_target_pairs={{0,1},{1,0},{2,3},{3,2},{4,5},{5,4},{6,7},{7,6},{8,9},{9,8},{10,11... | collective-permute-start | bytes 589832 | tf_op jit(solution)/shard_map/ppermute | solution.py:51
  96.8 4.2 %shard_map.110.refs_3_ = f32[49,256,128]{2,1,0:T(8,128)S(1)} custom-call(s32[8]{0:T(128)S(1)} %stack.81.order, s32[24,16]{1,0:T(8,128)S(1)} %shard_map.103.index, bf16[24,16,128,128]{3,2,1,0:T(8,128)(2,1)} %bitcast.35, bf16[384,256]{1,0:T(8,128)(2,1)S(1)} %get-tuple-element.24.refs_0_, bf16[384,256]{1,0:T(8,128)(2,1)S(1)} %collective-permute-done.20.refs_1_), custom_call_target="tpu_custom_call" | custom-call | flops 805306368 | bytes 3145728 | tf_op jit(solution)/shard_map/pallas_call | solution.py:231
  101.0 5.2 %shard_map.111.refs_3_ = f32[49,256,128]{2,1,0:T(8,128)S(1)} custom-call(s32[8]{0:T(128)S(1)} %stack.81.order, s32[24,16]{1,0:T(8,128)S(1)} %shard_map.103.index, bf16[24,16,128,128]{3,2,1,0:T(8,128)(2,1)} %bitcast.36, bf16[384,256]{1,0:T(8,128)(2,1)S(1)} %collective-permute-done.14.refs_0_, ...), custom_call_target="tpu_custom_call", output_to_operand_aliasing={{}: (6, {})} | custom-call | flops 1207959552 | bytes 4718592 | tf_op jit(solution)/shard_map/pallas_call | solution.py:231
  106.2 1.8 %collective-permute-start.32 = (bf16[272,256]{1,0:T(8,128)(2,1)S(1)}, bf16[272,256]{1,0:T(8,128)(2,1)S(1)}, u32[]{:S(2)}, u32[]{:S(2)}) collective-permute-start(bf16[272,256]{1,0:T(8,128)(2,1)S(1)} %shard_map.116.refs_0_), channel_id=1, source_target_pairs={{0,8},{8,0},{16,24},{24,16},{32,40},{40,32},{48,56},{56,48},{64,72... | collective-permute-start | bytes 417800 | tf_op jit(solution)/shard_map/ppermute | solution.py:43
  108.1 6.0 %shard_map.112 = (f32[49,256,128]{2,1,0:T(8,128)S(1)}, bf16[1536,256]{1,0:T(8,128)(2,1)S(1)}, bf16[384,256]{1,0:T(8,128)(2,1)S(1)}, bf16[384,256]{1,0:T(8,128)(2...) custom-call(s32[8]{0:T(128)S(1)} %stack.81.order, ...), custom_call_target="tpu_custom_call", output_to_operand_aliasing={{0}: (6, {})} | custom-call | flops 1207959552 | bytes 4718592 | tf_op jit(solution)/shard_map/pallas_call | solution.py:231
  114.5 2.2 %collective-permute-start.22 = (bf16[1152,256]{1,0:T(8,128)(2,1)S(1)}, bf16[1152,256]{1,0:T(8,128)(2,1)S(1)}, u32[]{:S(2)}, u32[]{:S(2)}) collective-permute-start(bf16[1152,256]{1,0:T(8,128)(2,1)S(1)} %get-tuple-element.27), channel_id=1, source_target_pairs={{0,16},{1,65},{2,18},{3,67},{4,20},{5,69},{6,22},{7,71},{8,24},{9,... | collective-permute-start | bytes 1769480 | tf_op jit(solution)/shard_map/ppermute | solution.py:34
  116.7 2.0 %collective-permute-start.23 = (bf16[1152,256]{1,0:T(8,128)(2,1)S(1)}, bf16[1152,256]{1,0:T(8,128)(2,1)S(1)}, u32[]{:S(2)}, u32[]{:S(2)}) collective-permute-start(bf16[1152,256]{1,0:T(8,128)(2,1)S(1)} %get-tuple-element.28), channel_id=1, source_target_pairs={{0,24},{1,97},{2,26},{3,99},{4,28},{5,101},{6,30},{7,103},{8,0},{9... | collective-permute-start | bytes 1769480 | tf_op jit(solution)/shard_map/ppermute | solution.py:34
  119.7 4.8 %collective-permute-done.35.refs_3_ = bf16[272,256]{1,0:T(8,128)(2,1)S(1)} collective-permute-done((bf16[272,256]{1,0:T(8,128)(2,1)S(1)}, bf16[272,256]{1,0:T(8,128)(2,1)S(1)}, u32[]{:S(2)}, u32[]{:S(2)}) %collective-permute-start.35) | collective-permute-done | bytes 139296 | tf_op jit(solution)/shard_map/ppermute | solution.py:51
  124.5 1.9 %collective-permute-done.34.refs_2_ = bf16[272,256]{1,0:T(8,128)(2,1)S(1)} collective-permute-done((bf16[272,256]{1,0:T(8,128)(2,1)S(1)}, bf16[272,256]{1,0:T(8,128)(2,1)S(1)}, u32[]{:S(2)}, u32[]{:S(2)}) %collective-permute-start.34) | collective-permute-done | bytes 139296 | tf_op jit(solution)/shard_map/ppermute | solution.py:51
  126.4 4.7 %collective-permute-done.33.refs_1_ = bf16[272,256]{1,0:T(8,128)(2,1)S(1)} collective-permute-done((bf16[272,256]{1,0:T(8,128)(2,1)S(1)}, bf16[272,256]{1,0:T(8,128)(2,1)S(1)}, u32[]{:S(2)}, u32[]{:S(2)}) %collective-permute-start.33) | collective-permute-done | bytes 139296 | tf_op jit(solution)/shard_map/ppermute | solution.py:51
  133.0 2.3 %collective-permute-start.37 = (bf16[272,256]{1,0:T(8,128)(2,1)S(1)}, bf16[272,256]{1,0:T(8,128)(2,1)S(1)}, u32[]{:S(2)}, u32[]{:S(2)}) collective-permute-start(bf16[272,256]{1,0:T(8,128)(2,1)S(1)} %shard_map.119.t0), channel_id=1, source_target_pairs={{0,16},{8,24},{16,0},{24,8},{32,48},{40,56},{48,32},{56,40},{64,80... | collective-permute-start | bytes 417800 | tf_op jit(solution)/shard_map/ppermute | solution.py:43
  135.3 1.6 %collective-permute-start.28 = (bf16[384,256]{1,0:T(8,128)(2,1)S(1)}, bf16[384,256]{1,0:T(8,128)(2,1)S(1)}, u32[]{:S(2)}, u32[]{:S(2)}) collective-permute-start(bf16[384,256]{1,0:T(8,128)(2,1)S(1)} %get-tuple-element.33), channel_id=1, source_target_pairs={{0,16},{1,65},{2,18},{3,67},{4,20},{5,69},{6,22},{7,71},{8,24},{9,... | collective-permute-start | bytes 589832 | tf_op jit(solution)/shard_map/ppermute | solution.py:34
  138.4 2.2 %collective-permute-start.25 = (bf16[384,256]{1,0:T(8,128)(2,1)S(1)}, bf16[384,256]{1,0:T(8,128)(2,1)S(1)}, u32[]{:S(2)}, u32[]{:S(2)}) collective-permute-start(bf16[384,256]{1,0:T(8,128)(2,1)S(1)} %get-tuple-element.30), channel_id=1, source_target_pairs={{0,64},{1,17},{2,66},{3,19},{4,68},{5,21},{6,70},{7,23},{8,72},{9,... | collective-permute-start | bytes 589832 | tf_op jit(solution)/shard_map/ppermute | solution.py:34
  143.0 4.5 %collective-permute-done.24.refs_0_ = bf16[384,256]{1,0:T(8,128)(2,1)S(1)} collective-permute-done((bf16[384,256]{1,0:T(8,128)(2,1)S(1)}, bf16[384,256]{1,0:T(8,128)(2,1)S(1)}, u32[]{:S(2)}, u32[]{:S(2)}) %collective-permute-start.24) | collective-permute-done | bytes 196640 | tf_op jit(solution)/shard_map/ppermute | solution.py:34
  (93 shorter events, 25.8 us)
Async XLA Ops:
  0.6 8.7 %collective-permute-start.2 = (bf16[384,256]{1,0:T(8,128)(2,1)}, bf16[384,256]{1,0:T(8,128)(2,1)S(1)}, u32[]{:S(2)}, u32[]{:S(2)}) collective-permute-start(bf16[384,256]{1,0:T(8,128)(2,1)} %own.1), channel_id=1, source_target_pairs={{0,96},{1,25},{2,98},{3,27},{4,100},{5,29},{6,102},{7,31},{8,104},... | collective-permute-start | bytes 589832 | tf_op jit(solution)/shard_map/ppermute | solution.py:34
  4.3 6.6 %collective-permute-start.1 = (bf16[384,256]{1,0:T(8,128)(2,1)}, bf16[384,256]{1,0:T(8,128)(2,1)S(1)}, u32[]{:S(2)}, u32[]{:S(2)}) collective-permute-start(bf16[384,256]{1,0:T(8,128)(2,1)} %own.1), channel_id=1, source_target_pairs={{0,64},{1,17},{2,66},{3,19},{4,68},{5,21},{6,70},{7,23},{8,72},{9,... | collective-permute-start | bytes 589832 | tf_op jit(solution)/shard_map/ppermute | solution.py:34
  4.6 8.3 %collective-permute-start = (bf16[384,256]{1,0:T(8,128)(2,1)}, bf16[384,256]{1,0:T(8,128)(2,1)S(1)}, u32[]{:S(2)}, u32[]{:S(2)}) collective-permute-start(bf16[384,256]{1,0:T(8,128)(2,1)} %own.1), channel_id=1, source_target_pairs={{0,32},{1,9},{2,34},{3,11},{4,36},{5,13},{6,38},{7,15},{8,40},{9,1... | collective-permute-start | bytes 589832 | tf_op jit(solution)/shard_map/ppermute | solution.py:34
  12.9 36.7 %collective-permute-start.8 = (bf16[1152,256]{1,0:T(8,128)(2,1)S(1)}, bf16[1152,256]{1,0:T(8,128)(2,1)S(1)}, u32[]{:S(2)}, u32[]{:S(2)}) collective-permute-start(bf16[1152,256]{1,0:T(8,128)(2,1)S(1)} %shard_map.105), channel_id=1, source_target_pairs={{0,24},{1,97},{2,26},{3,99},{4,28},{5,101},{6,30},{7,103},{8,0},{9... | collective-permute-start | bytes 1769480 | tf_op jit(solution)/shard_map/ppermute | solution.py:34
  15.2 34.4 %collective-permute-start.7 = (bf16[1152,256]{1,0:T(8,128)(2,1)S(1)}, bf16[1152,256]{1,0:T(8,128)(2,1)S(1)}, u32[]{:S(2)}, u32[]{:S(2)}) collective-permute-start(bf16[1152,256]{1,0:T(8,128)(2,1)S(1)} %shard_map.105), channel_id=1, source_target_pairs={{0,16},{1,65},{2,18},{3,67},{4,20},{5,69},{6,22},{7,71},{8,24},{9,... | collective-permute-start | bytes 1769480 | tf_op jit(solution)/shard_map/ppermute | solution.py:34
  15.7 33.9 %collective-permute-start.6 = (bf16[1152,256]{1,0:T(8,128)(2,1)S(1)}, bf16[1152,256]{1,0:T(8,128)(2,1)S(1)}, u32[]{:S(2)}, u32[]{:S(2)}) collective-permute-start(bf16[1152,256]{1,0:T(8,128)(2,1)S(1)} %shard_map.105), channel_id=1, source_target_pairs={{0,8},{1,33},{2,10},{3,35},{4,12},{5,37},{6,14},{7,39},{8,16},{9,4... | collective-permute-start | bytes 1769480 | tf_op jit(solution)/shard_map/ppermute | solution.py:34
  16.3 17.7 %collective-permute-start.4 = (bf16[384,256]{1,0:T(8,128)(2,1)}, bf16[384,256]{1,0:T(8,128)(2,1)S(1)}, u32[]{:S(2)}, u32[]{:S(2)}) collective-permute-start(bf16[384,256]{1,0:T(8,128)(2,1)} %own.1), channel_id=1, source_target_pairs={{0,16},{1,65},{2,18},{3,67},{4,20},{5,69},{6,22},{7,71},{8,24},{9,... | collective-permute-start | bytes 589832 | tf_op jit(solution)/shard_map/ppermute | solution.py:34
  18.2 31.4 %collective-permute-start.3 = (bf16[384,256]{1,0:T(8,128)(2,1)}, bf16[384,256]{1,0:T(8,128)(2,1)S(1)}, u32[]{:S(2)}, u32[]{:S(2)}) collective-permute-start(bf16[384,256]{1,0:T(8,128)(2,1)} %own.1), channel_id=1, source_target_pairs={{0,8},{1,33},{2,10},{3,35},{4,12},{5,37},{6,14},{7,39},{8,16},{9,4... | collective-permute-start | bytes 589832 | tf_op jit(solution)/shard_map/ppermute | solution.py:34
  34.0 15.6 %collective-permute-start.5 = (bf16[384,256]{1,0:T(8,128)(2,1)}, bf16[384,256]{1,0:T(8,128)(2,1)}, u32[]{:S(2)}, u32[]{:S(2)}) collective-permute-start(bf16[384,256]{1,0:T(8,128)(2,1)} %own.1), channel_id=1, source_target_pairs={{0,24},{1,97},{2,26},{3,99},{4,28},{5,101},{6,30},{7,103},{8,0},{9... | collective-permute-start | bytes 589832 | tf_op jit(solution)/shard_map/ppermute | solution.py:34
  57.4 8.4 %collective-permute-start.10 = (bf16[3,384,256]{2,1,0:T(8,128)(2,1)S(1)}, bf16[3,384,256]{2,1,0:T(8,128)(2,1)S(1)}, u32[]{:S(2)}, u32[]{:S(2)}) collective-permute-start(bf16[3,384,256]{2,1,0:T(8,128)(2,1)S(1)} %get-tuple-element.22), channel_id=1, source_target_pairs={{0,1},{1,0},{2,3},{3,2},{4,5},{5,4},{6,7},{7,6},{8,9},{9,8},{10,11... | collective-permute-start | bytes 1769480 | tf_op jit(solution)/shard_map/ppermute | solution.py:51
  63.1 7.4 %collective-permute-start.9 = (bf16[384,256]{1,0:T(8,128)(2,1)S(1)}, bf16[384,256]{1,0:T(8,128)(2,1)S(1)}, u32[]{:S(2)}, u32[]{:S(2)}) collective-permute-start(bf16[384,256]{1,0:T(8,128)(2,1)S(1)} %slice_bitcast_fusion), channel_id=1, source_target_pairs={{0,1},{1,0},{2,3},{3,2},{4,5},{5,4},{6,7},{7,6},{8,9},{9,8},{10,11... | collective-permute-start | bytes 589832 | tf_op jit(solution)/shard_map/ppermute | solution.py:51
  66.0 11.7 %collective-permute-start.13 = (bf16[384,256]{1,0:T(8,128)(2,1)S(1)}, bf16[384,256]{1,0:T(8,128)(2,1)S(1)}, u32[]{:S(2)}, u32[]{:S(2)}) collective-permute-start(bf16[384,256]{1,0:T(8,128)(2,1)S(1)} %get-tuple-element.38), channel_id=1, source_target_pairs={{0,6},{1,7},{2,0},{3,1},{4,2},{5,3},{6,4},{7,5},{8,14},{9,15},{10,... | collective-permute-start | bytes 589832 | tf_op jit(solution)/shard_map/ppermute | solution.py:51
  69.8 7.9 %collective-permute-start.12 = (bf16[384,256]{1,0:T(8,128)(2,1)S(1)}, bf16[384,256]{1,0:T(8,128)(2,1)S(1)}, u32[]{:S(2)}, u32[]{:S(2)}) collective-permute-start(bf16[384,256]{1,0:T(8,128)(2,1)S(1)} %get-tuple-element.39), channel_id=1, source_target_pairs={{0,4},{1,5},{2,6},{3,7},{4,0},{5,1},{6,2},{7,3},{8,12},{9,13},{10,... | collective-permute-start | bytes 589832 | tf_op jit(solution)/shard_map/ppermute | solution.py:51
  69.8 12.0 %collective-permute-start.11 = (bf16[384,256]{1,0:T(8,128)(2,1)S(1)}, bf16[384,256]{1,0:T(8,128)(2,1)S(1)}, u32[]{:S(2)}, u32[]{:S(2)}) collective-permute-start(bf16[384,256]{1,0:T(8,128)(2,1)S(1)} %get-tuple-element.40), channel_id=1, source_target_pairs={{0,2},{1,3},{2,4},{3,5},{4,6},{5,7},{6,0},{7,1},{8,10},{9,11},{10,... | collective-permute-start | bytes 589832 | tf_op jit(solution)/shard_map/ppermute | solution.py:51
  82.9 8.6 %collective-permute-start.16 = (bf16[384,256]{1,0:T(8,128)(2,1)S(1)}, bf16[384,256]{1,0:T(8,128)(2,1)S(1)}, u32[]{:S(2)}, u32[]{:S(2)}) collective-permute-start(bf16[384,256]{1,0:T(8,128)(2,1)S(1)} %get-tuple-element.24.refs_0_), channel_id=1, source_target_pairs={{0,4},{1,5},{2,6},{3,7},{4,0},{5,1},{6,2},{7,3},{8,12},{9,13},{10,... | collective-permute-start | bytes 589832 | tf_op jit(solution)/shard_map/ppermute | solution.py:51
  83.5 11.9 %collective-permute-start.14 = (bf16[384,256]{1,0:T(8,128)(2,1)S(1)}, bf16[384,256]{1,0:T(8,128)(2,1)S(1)}, u32[]{:S(2)}, u32[]{:S(2)}) collective-permute-start(bf16[384,256]{1,0:T(8,128)(2,1)S(1)} %get-tuple-element.24.refs_0_), channel_id=1, source_target_pairs={{0,2},{1,3},{2,4},{3,5},{4,6},{5,7},{6,0},{7,1},{8,10},{9,11},{10,... | collective-permute-start | bytes 589832 | tf_op jit(solution)/shard_map/ppermute | solution.py:51
  84.3 12.5 %collective-permute-start.20 = (bf16[384,256]{1,0:T(8,128)(2,1)S(1)}, bf16[384,256]{1,0:T(8,128)(2,1)S(1)}, u32[]{:S(2)}, u32[]{:S(2)}) collective-permute-start(bf16[384,256]{1,0:T(8,128)(2,1)S(1)} %get-tuple-element.24.refs_0_), channel_id=1, source_target_pairs={{0,1},{1,0},{2,3},{3,2},{4,5},{5,4},{6,7},{7,6},{8,9},{9,8},{10,11... | collective-permute-start | bytes 589832 | tf_op jit(solution)/shard_map/ppermute | solution.py:51
  85.7 10.3 %collective-permute-start.30 = (bf16[272,256]{1,0:T(8,128)(2,1)S(1)}, bf16[272,256]{1,0:T(8,128)(2,1)S(1)}, u32[]{:S(2)}, u32[]{:S(2)}) collective-permute-start(bf16[272,256]{1,0:T(8,128)(2,1)S(1)} %get-tuple-element.35.refs_0_), channel_id=1, source_target_pairs={{0,32},{8,40},{16,48},{24,56},{32,0},{40,8},{48,16},{56,24},{64,96... | collective-permute-start | bytes 417800 | tf_op jit(solution)/shard_map/ppermute | solution.py:43
  88.5 19.5 %collective-permute-start.19 = (bf16[384,256]{1,0:T(8,128)(2,1)S(1)}, bf16[384,256]{1,0:T(8,128)(2,1)S(1)}, u32[]{:S(2)}, u32[]{:S(2)}) collective-permute-start(bf16[384,256]{1,0:T(8,128)(2,1)S(1)} %collective-permute-done.18.refs_2_), channel_id=1, source_target_pairs={{0,1},{1,0},{2,3},{3,2},{4,5},{5,4},{6,7},{7,6},{8,9},{9,8},{10,11... | collective-permute-start | bytes 589832 | tf_op jit(solution)/shard_map/ppermute | solution.py:51
  91.4 16.6 %collective-permute-start.17 = (bf16[384,256]{1,0:T(8,128)(2,1)S(1)}, bf16[384,256]{1,0:T(8,128)(2,1)S(1)}, u32[]{:S(2)}, u32[]{:S(2)}) collective-permute-start(bf16[384,256]{1,0:T(8,128)(2,1)S(1)} %collective-permute-done.16.refs_1_), channel_id=1, source_target_pairs={{0,1},{1,0},{2,3},{3,2},{4,5},{5,4},{6,7},{7,6},{8,9},{9,8},{10,11... | collective-permute-start | bytes 589832 | tf_op jit(solution)/shard_map/ppermute | solution.py:51
  95.3 12.7 %collective-permute-start.15 = (bf16[384,256]{1,0:T(8,128)(2,1)S(1)}, bf16[384,256]{1,0:T(8,128)(2,1)S(1)}, u32[]{:S(2)}, u32[]{:S(2)}) collective-permute-start(bf16[384,256]{1,0:T(8,128)(2,1)S(1)} %collective-permute-done.14.refs_0_), channel_id=1, source_target_pairs={{0,1},{1,0},{2,3},{3,2},{4,5},{5,4},{6,7},{7,6},{8,9},{9,8},{10,11... | collective-permute-start | bytes 589832 | tf_op jit(solution)/shard_map/ppermute | solution.py:51
  96.0 10.1 %collective-permute-start.31 = (bf16[272,256]{1,0:T(8,128)(2,1)S(1)}, bf16[272,256]{1,0:T(8,128)(2,1)S(1)}, u32[]{:S(2)}, u32[]{:S(2)}) collective-permute-start(bf16[272,256]{1,0:T(8,128)(2,1)S(1)} %shard_map.115.refs_0_), channel_id=1, source_target_pairs={{0,64},{8,72},{16,80},{24,88},{32,96},{40,104},{48,112},{56,120},{... | collective-permute-start | bytes 417800 | tf_op jit(solution)/shard_map/ppermute | solution.py:43
  106.2 12.5 %collective-permute-start.32 = (bf16[272,256]{1,0:T(8,128)(2,1)S(1)}, bf16[272,256]{1,0:T(8,128)(2,1)S(1)}, u32[]{:S(2)}, u32[]{:S(2)}) collective-permute-start(bf16[272,256]{1,0:T(8,128)(2,1)S(1)} %shard_map.116.refs_0_), channel_id=1, source_target_pairs={{0,8},{8,0},{16,24},{24,16},{32,40},{40,32},{48,56},{56,48},{64,72... | collective-permute-start | bytes 417800 | tf_op jit(solution)/shard_map/ppermute | solution.py:43
  114.1 21.2 %collective-permute-start.21 = (bf16[1152,256]{1,0:T(8,128)(2,1)S(1)}, bf16[1152,256]{1,0:T(8,128)(2,1)S(1)}, u32[]{:S(2)}, u32[]{:S(2)}) collective-permute-start(bf16[1152,256]{1,0:T(8,128)(2,1)S(1)} %get-tuple-element.26), channel_id=1, source_target_pairs={{0,8},{1,33},{2,10},{3,35},{4,12},{5,37},{6,14},{7,39},{8,16},{9,4... | collective-permute-start | bytes 1769480 | tf_op jit(solution)/shard_map/ppermute | solution.py:34
  114.5 22.4 %collective-permute-start.22 = (bf16[1152,256]{1,0:T(8,128)(2,1)S(1)}, bf16[1152,256]{1,0:T(8,128)(2,1)S(1)}, u32[]{:S(2)}, u32[]{:S(2)}) collective-permute-start(bf16[1152,256]{1,0:T(8,128)(2,1)S(1)} %get-tuple-element.27), channel_id=1, source_target_pairs={{0,16},{1,65},{2,18},{3,67},{4,20},{5,69},{6,22},{7,71},{8,24},{9,... | collective-permute-start | bytes 1769480 | tf_op jit(solution)/shard_map/ppermute | solution.py:34
  116.7 21.3 %collective-permute-start.23 = (bf16[1152,256]{1,0:T(8,128)(2,1)S(1)}, bf16[1152,256]{1,0:T(8,128)(2,1)S(1)}, u32[]{:S(2)}, u32[]{:S(2)}) collective-permute-start(bf16[1152,256]{1,0:T(8,128)(2,1)S(1)} %get-tuple-element.28), channel_id=1, source_target_pairs={{0,24},{1,97},{2,26},{3,99},{4,28},{5,101},{6,30},{7,103},{8,0},{9... | collective-permute-start | bytes 1769480 | tf_op jit(solution)/shard_map/ppermute | solution.py:34
  119.7 6.7 %collective-permute-start.34 = (bf16[272,256]{1,0:T(8,128)(2,1)S(1)}, bf16[272,256]{1,0:T(8,128)(2,1)S(1)}, u32[]{:S(2)}, u32[]{:S(2)}) collective-permute-start(bf16[272,256]{1,0:T(8,128)(2,1)S(1)} %shard_map.117.refs_0_), channel_id=1, source_target_pairs={{0,4},{1,5},{2,6},{3,7},{4,0},{5,1},{6,2},{7,3},{8,12},{9,13},{10,... | collective-permute-start | bytes 417800 | tf_op jit(solution)/shard_map/ppermute | solution.py:51
  133.0 7.6 %collective-permute-start.37 = (bf16[272,256]{1,0:T(8,128)(2,1)S(1)}, bf16[272,256]{1,0:T(8,128)(2,1)S(1)}, u32[]{:S(2)}, u32[]{:S(2)}) collective-permute-start(bf16[272,256]{1,0:T(8,128)(2,1)S(1)} %shard_map.119.t0), channel_id=1, source_target_pairs={{0,16},{8,24},{16,0},{24,8},{32,48},{40,56},{48,32},{56,40},{64,80... | collective-permute-start | bytes 417800 | tf_op jit(solution)/shard_map/ppermute | solution.py:43
  135.3 7.4 %collective-permute-start.28 = (bf16[384,256]{1,0:T(8,128)(2,1)S(1)}, bf16[384,256]{1,0:T(8,128)(2,1)S(1)}, u32[]{:S(2)}, u32[]{:S(2)}) collective-permute-start(bf16[384,256]{1,0:T(8,128)(2,1)S(1)} %get-tuple-element.33), channel_id=1, source_target_pairs={{0,16},{1,65},{2,18},{3,67},{4,20},{5,69},{6,22},{7,71},{8,24},{9,... | collective-permute-start | bytes 589832 | tf_op jit(solution)/shard_map/ppermute | solution.py:34
  138.3 9.2 %collective-permute-start.24 = (bf16[384,256]{1,0:T(8,128)(2,1)S(1)}, bf16[384,256]{1,0:T(8,128)(2,1)S(1)}, u32[]{:S(2)}, u32[]{:S(2)}) collective-permute-start(bf16[384,256]{1,0:T(8,128)(2,1)S(1)} %get-tuple-element.29), channel_id=1, source_target_pairs={{0,32},{1,9},{2,34},{3,11},{4,36},{5,13},{6,38},{7,15},{8,40},{9,1... | collective-permute-start | bytes 589832 | tf_op jit(solution)/shard_map/ppermute | solution.py:34
  138.4 9.1 %collective-permute-start.25 = (bf16[384,256]{1,0:T(8,128)(2,1)S(1)}, bf16[384,256]{1,0:T(8,128)(2,1)S(1)}, u32[]{:S(2)}, u32[]{:S(2)}) collective-permute-start(bf16[384,256]{1,0:T(8,128)(2,1)S(1)} %get-tuple-element.30), channel_id=1, source_target_pairs={{0,64},{1,17},{2,66},{3,19},{4,68},{5,21},{6,70},{7,23},{8,72},{9,... | collective-permute-start | bytes 589832 | tf_op jit(solution)/shard_map/ppermute | solution.py:34
  140.6 7.0 %collective-permute-start.26 = (bf16[384,256]{1,0:T(8,128)(2,1)S(1)}, bf16[384,256]{1,0:T(8,128)(2,1)S(1)}, u32[]{:S(2)}, u32[]{:S(2)}) collective-permute-start(bf16[384,256]{1,0:T(8,128)(2,1)S(1)} %get-tuple-element.31), channel_id=1, source_target_pairs={{0,96},{1,25},{2,98},{3,27},{4,100},{5,29},{6,102},{7,31},{8,104},... | collective-permute-start | bytes 589832 | tf_op jit(solution)/shard_map/ppermute | solution.py:34
  (17 other events, 132.2 us)

commit v3 on v2

--- a/solution.py
+++ b/solution.py
@@ -177,7 +177,7 @@
         refs = refs[1:]
     acc, refs = refs[0], refs[1:]
     if final:
-        own, sides, many = refs[0], refs[1:SIDE], refs[SIDE:2 * SIDE - 1]
+        many = refs[:3]
     turned, tiles, sems = refs[-3:]
 
     def fetch(step):
@@ -206,17 +206,22 @@
     lax.fori_loop(0, count, body, 0)
 
     if final:
-        for b in (1, 2, 3, 0):
-            for a in range(SIDE):
-                if b == 0:
-                    out, start = own, a * ND
-                elif a == 0:
-                    out, start = sides[b - 1], 0
-                else:
-                    out, start = many[b - 1], (a - 1) * ND
-                for n in range(PER):
-                    row = start + n * TILE
-                    out[row:row + TILE, :] = acc[rel(-a, -b) * PER + n].astype(BF).T
+        for b in (1, 2, 3):
+            for a in (1, 2, 3):
+                turn_block(acc, a, b, many[b - 1], (a - 1) * ND)
+
+
+def turn_block(acc, a, b, out, start):
+    for n in range(PER):
+        row = start + n * TILE
+        out[row:row + TILE, :] = acc[rel(-a, -b) * PER + n].astype(BF).T
+
+
+def rest_kernel(acc, own, *sides):
+    for a in (1, 2, 3, 0):
+        turn_block(acc, a, 0, own, a * ND)
+    for b in (1, 2, 3):
+        turn_block(acc, 0, b, sides[b - 1], 0)
 
 
 def backward(offset, order, index, adj, sources, acc=None, final=False):
@@ -225,7 +230,7 @@
     state = jax.ShapeDtypeStruct((DUMMY + 1, width, TILE), F32)
     outs = (state,)
     if final:
-        outs += tuple(jax.ShapeDtypeStruct((n * ND, width), BF) for n in (SIDE, 1, 1, 1, 3, 3, 3))
+        outs += tuple(jax.ShapeDtypeStruct((n * ND, width), BF) for n in (3, 3, 3))
     initial = acc is None
     extra = [] if initial else [acc]
     return pl.pallas_call(
@@ -351,22 +356,24 @@
     theirs = [send_col(grad, 0, 1)]
     theirs += fan(lambda v, d: send_col(v, 0, 1), mine[1:])
     other_terms = trade_row(along, 1, True)
+    along = small(add_terms_kernel, terms, [along, other_terms])
+    other_terms = trade_row(along, 2, True)
     acc, = backward(0, order_backward, index, adj, [mine[0], theirs[0]])
     along = small(add_terms_kernel, terms, [along, other_terms])
-    other_terms = trade_row(along, 2, True)
+    other_terms = trade_row(along, 1, False)
     acc, = backward(2, order_backward, index, adj, mine[1:], acc)
     along = small(add_terms_kernel, terms, [along, other_terms])
-    other_terms = trade_row(along, 1, False)
-    acc, own, *blocks = backward(SIDE + 1, order_backward, index, adj, theirs[1:], acc, final=True)
-
-    landed = fan(lambda v, d: send_plane(v, False, d), blocks[3:])
-    beside = fan(lambda v, d: send_plane(v, False, d), blocks[:3])
+    other_terms = trade_row(along, 2, False)
+    acc, *blocks = backward(SIDE + 1, order_backward, index, adj, theirs[1:], acc, final=True)
+
+    landed = fan(lambda v, d: send_plane(v, False, d), blocks)
+    own, *blocks = small(rest_kernel, (jax.ShapeDtypeStruct((SIDE * ND, width), BF),) + (block,) * 3, [acc])
+
+    beside = fan(lambda v, d: send_plane(v, False, d), blocks)
     along = small(add_terms_kernel, terms, [along, other_terms])
     along_z = [along] + fan(lambda v, d: send_col(v, d, 0), [along] * 3)
     along = small(add_terms_kernel, terms, along_z)
     other_terms = send_col(along, 0, 1)
-    along = small(add_terms_kernel, terms, [along, other_terms])
-    other_terms = trade_row(along, 2, False)
     nodes = features.shape[0] * lax.axis_size("row") * lax.axis_size("col")
     grad_weight, grad_bias = small(
         functools.partial(last_terms_kernel, nodes**-0.5),

time: 151 us -> 162 us (1.073); the launches traced: 149 us -> 161 us
  starting transfers between devices: 45.3 us -> 54.4 us
  waiting for transfers between devices: 55.4 us -> 59.2 us
    ppermute x16, starting transfers between devices: 18.7 us -> 27.7 us  [send_col(): return lax.ppermute(value, 'col', pairs)]
    ppermute x4, waiting for transfers between devices: 0.01 us -> 6.91 us  [trade_row(): return lax.ppermute(value, 'row', pairs)]
    ppermute x16, waiting for transfers between devices: 28 us -> 23.7 us  [send_col(): return lax.ppermute(value, 'col', pairs)]
    ppermute x18, starting transfers between devices: 21.6 us -> 23.7 us  [send_plane(): return lax.ppermute(value, ('row', 'col'), pairs)]
    ppermute x4, starting transfers between devices: 4.93 us -> 3.02 us  [trade_row(): return lax.ppermute(value, 'row', pairs)]
    pallas_call x11 -> x12, Pallas kernels: 3.41 us -> 3.8 us  [small(): pl.pallas_call(kernel, out_shape=outs, in_specs=[VM] * len(operands), out...]
  transfers between devices with their start and end apart: 38 -> 38, of which waited for: 14 -> 15; matrix products, arithmetic and copies ran while one was open for 2% -> 2% of each run, Pallas kernels for 19% -> 17%
where the time goes in v3:
time: 162 us; the launch traced here: 161 us
  waiting for transfers between devices  59.2 us (37%)
  starting transfers between devices  54.4 us (34%)
  Pallas kernels  33.3 us (21%)
  local copies, waits for them, and re-layouts  13.5 us (8%)
    ppermute x18, waiting for transfers between devices, send_plane(): return lax.ppermute(value, ('row', 'col'), pairs)  28.6 us
    ppermute x16, starting transfers between devices, send_col(): return lax.ppermute(value, 'col', pairs)  27.7 us
    ppermute x18, starting transfers between devices, send_plane(): return lax.ppermute(value, ('row', 'col'), pairs)  23.7 us
    ppermute x16, waiting for transfers between devices, send_col(): return lax.ppermute(value, 'col', pairs)  23.7 us
    pallas_call x3, Pallas kernels, backward(): pl.pallas_call(functools.partial(backward_kernel, offset, count, initial,...  15 us
    unnamed x23, local copies, waits for them, and re-layouts  11.9 us
    pallas_call x3, Pallas kernels, forward(): pl.pallas_call(functools.partial(forward_first_kernel if first else forwa...  7.79 us
    ppermute x4, waiting for transfers between devices, trade_row(): return lax.ppermute(value, 'row', pairs)  6.91 us
  transfers between devices with their start and end apart: 38, of which 15 were waited for; matrix products, arithmetic and copies ran while one was open for 2% of the time, Pallas kernels for 17%

profile of v3, /device:TPU:1, one launch (start us, length us, event | category | flops | bytes accessed | tf_op | source)
XLA Modules:
  0.0 161.5 jit_solution(2237961766634670928)
XLA Ops:
  0.6 3.6 %collective-permute-start.2 = (bf16[384,256]{1,0:T(8,128)(2,1)}, bf16[384,256]{1,0:T(8,128)(2,1)S(1)}, u32[]{:S(2)}, u32[]{:S(2)}) collective-permute-start(bf16[384,256]{1,0:T(8,128)(2,1)} %own.1), channel_id=1, source_target_pairs={{0,96},{1,25},{2,98},{3,27},{4,100},{5,29},{6,102},{7,31},{8,104},... | collective-permute-start | bytes 589832 | tf_op jit(solution)/shard_map/ppermute | solution.py:34
  5.3 4.0 %collective-permute-done.2.refs_2_.f3 = bf16[384,256]{1,0:T(8,128)(2,1)S(1)} collective-permute-done((bf16[384,256]{1,0:T(8,128)(2,1)}, bf16[384,256]{1,0:T(8,128)(2,1)S(1)}, u32[]{:S(2)}, u32[]{:S(2)}) %collective-permute-start.2) | collective-permute-done | bytes 196640 | tf_op jit(solution)/shard_map/ppermute | solution.py:34
  10.8 2.1 %collective-permute-done.refs_0_.f1 = bf16[384,256]{1,0:T(8,128)(2,1)S(1)} collective-permute-done((bf16[384,256]{1,0:T(8,128)(2,1)}, bf16[384,256]{1,0:T(8,128)(2,1)S(1)}, u32[]{:S(2)}, u32[]{:S(2)}) %collective-permute-start) | collective-permute-done | bytes 196640 | tf_op jit(solution)/shard_map/ppermute | solution.py:34
  12.9 2.3 %collective-permute-start.8 = (bf16[1152,256]{1,0:T(8,128)(2,1)S(1)}, bf16[1152,256]{1,0:T(8,128)(2,1)S(1)}, u32[]{:S(2)}, u32[]{:S(2)}) collective-permute-start(bf16[1152,256]{1,0:T(8,128)(2,1)S(1)} %shard_map.105), channel_id=1, source_target_pairs={{0,24},{1,97},{2,26},{3,99},{4,28},{5,101},{6,30},{7,103},{8,0},{9... | collective-permute-start | bytes 1769480 | tf_op jit(solution)/shard_map/ppermute | solution.py:34
  16.3 1.8 %collective-permute-start.4 = (bf16[384,256]{1,0:T(8,128)(2,1)}, bf16[384,256]{1,0:T(8,128)(2,1)S(1)}, u32[]{:S(2)}, u32[]{:S(2)}) collective-permute-start(bf16[384,256]{1,0:T(8,128)(2,1)} %own.1), channel_id=1, source_target_pairs={{0,16},{1,65},{2,18},{3,67},{4,20},{5,69},{6,22},{7,71},{8,24},{9,... | collective-permute-start | bytes 589832 | tf_op jit(solution)/shard_map/ppermute | solution.py:34
  19.0 15.0 %collective-permute-done.4.s2 = bf16[384,256]{1,0:T(8,128)(2,1)S(1)} collective-permute-done((bf16[384,256]{1,0:T(8,128)(2,1)}, bf16[384,256]{1,0:T(8,128)(2,1)S(1)}, u32[]{:S(2)}, u32[]{:S(2)}) %collective-permute-start.4) | collective-permute-done | bytes 196640 | tf_op jit(solution)/shard_map/ppermute | solution.py:34
  36.7 6.1 %shard_map.104.adj = bf16[24,16,128,128]{3,2,1,0:T(8,128)(2,1)S(1)} custom-call(bf16[24,16,128,128]{3,2,1,0:T(8,128)(2,1)} %bitcast.34), custom_call_target="tpu_custom_call" | custom-call | tf_op jit(solution)/shard_map/pallas_call | solution.py:311
  42.8 4.6 %copy-done = bf16[24,16,128,128]{3,2,1,0:T(8,128)(2,1)} copy-done((bf16[24,16,128,128]{3,2,1,0:T(8,128)(2,1)}, bf16[24,16,128,128]{3,2,1,0:T(8,128)(2,1)S(1)}, u32[]{:S(2)}) %copy-start) | copy-done | bytes 12582936
  49.6 4.6 %copy-done.1 = bf16[24,16,128,128]{3,2,1,0:T(8,128)(2,1)S(1)} copy-done((bf16[24,16,128,128]{3,2,1,0:T(8,128)(2,1)S(1)}, bf16[24,16,128,128]{3,2,1,0:T(8,128)(2,1)}, u32[]{:S(2)}) %copy-start.1) | copy-done | bytes 12582936
  54.2 3.2 %shard_map.106 = (bf16[3,384,256]{2,1,0:T(8,128)(2,1)S(1)}, bf16[6272,256]{1,0:T(8,128)(2,1)S(1)}) custom-call(s32[8]{0:T(128)S(1)} %stack.70.order, s32[24,16]{1,0:T(8,128)S(1)} %shard_map.103.index, bf16[24,16,128,128]{3,2,1,0:T(8,128)(2,1)S(1)} %copy-done.1, bf16[384,256]{1,0:T(8,128)(2,1)S(1)} %copy-done.3, ...), custom_call_target="tpu_custom_call" | custom-call | flops 1207959552 | bytes 4718592 | tf_op jit(solution)/shard_map/pallas_call | solution.py:147
  57.4 3.6 %collective-permute-start.10 = (bf16[3,384,256]{2,1,0:T(8,128)(2,1)S(1)}, bf16[3,384,256]{2,1,0:T(8,128)(2,1)S(1)}, u32[]{:S(2)}, u32[]{:S(2)}) collective-permute-start(bf16[3,384,256]{2,1,0:T(8,128)(2,1)S(1)} %get-tuple-element.23), channel_id=1, source_target_pairs={{0,1},{1,0},{2,3},{3,2},{4,5},{5,4},{6,7},{7,6},{8,9},{9,8},{10,11... | collective-permute-start | bytes 1769480 | tf_op jit(solution)/shard_map/ppermute | solution.py:51
  61.0 2.0 %shard_map.107.keep = bf16[2,384,256]{2,1,0:T(8,128)(2,1)S(1)} custom-call(s32[8]{0:T(128)S(1)} %stack.70.order, s32[24,16]{1,0:T(8,128)S(1)} %shard_map.103.index, bf16[24,16,128,128]{3,2,1,0:T(8,128)(2,1)S(1)} %copy-done.1, bf16[6272,256]{1,0:T(8,128)(2,1)S(1)} %get-tuple-element.22.panel), custom_call_target="tpu_custom_call" | custom-call | flops 805306368 | bytes 3145728 | tf_op jit(solution)/shard_map/pallas_call | solution.py:147
  63.3 2.6 %shard_map.108 = bf16[3,384,256]{2,1,0:T(8,128)(2,1)S(1)} custom-call(s32[8]{0:T(128)S(1)} %stack.70.order, s32[24,16]{1,0:T(8,128)S(1)} %shard_map.103.index, bf16[24,16,128,128]{3,2,1,0:T(8,128)(2,1)S(1)} %bitcast.31, bf16[6272,256]{1,0:T(8,128)(2,1)S(1)} %get-tuple-element.22.panel), custom_call_target="tpu_custom_call" | custom-call | flops 1207959552 | bytes 4718592 | tf_op jit(solution)/shard_map/pallas_call | solution.py:147
  66.0 3.8 %collective-permute-start.13 = (bf16[384,256]{1,0:T(8,128)(2,1)S(1)}, bf16[384,256]{1,0:T(8,128)(2,1)S(1)}, u32[]{:S(2)}, u32[]{:S(2)}) collective-permute-start(bf16[384,256]{1,0:T(8,128)(2,1)S(1)} %get-tuple-element.40), channel_id=1, source_target_pairs={{0,6},{1,7},{2,0},{3,1},{4,2},{5,3},{6,4},{7,5},{8,14},{9,15},{10,... | collective-permute-start | bytes 589832 | tf_op jit(solution)/shard_map/ppermute | solution.py:51
  70.5 7.2 %collective-permute-done.13.r3 = bf16[384,256]{1,0:T(8,128)(2,1)S(1)} collective-permute-done((bf16[384,256]{1,0:T(8,128)(2,1)S(1)}, bf16[384,256]{1,0:T(8,128)(2,1)S(1)}, u32[]{:S(2)}, u32[]{:S(2)}) %collective-permute-start.13) | collective-permute-done | bytes 196640 | tf_op jit(solution)/shard_map/ppermute | solution.py:51
  77.7 4.1 %collective-permute-done.11.r1 = bf16[384,256]{1,0:T(8,128)(2,1)S(1)} collective-permute-done((bf16[384,256]{1,0:T(8,128)(2,1)S(1)}, bf16[384,256]{1,0:T(8,128)(2,1)S(1)}, u32[]{:S(2)}, u32[]{:S(2)}) %collective-permute-start.11) | collective-permute-done | bytes 196640 | tf_op jit(solution)/shard_map/ppermute | solution.py:51
  85.7 2.9 %collective-permute-done.18.refs_2_ = bf16[384,256]{1,0:T(8,128)(2,1)S(1)} collective-permute-done((bf16[384,256]{1,0:T(8,128)(2,1)S(1)}, bf16[384,256]{1,0:T(8,128)(2,1)S(1)}, u32[]{:S(2)}, u32[]{:S(2)}) %collective-permute-start.18) | collective-permute-done | bytes 196640 | tf_op jit(solution)/shard_map/ppermute | solution.py:51
  88.5 2.9 %collective-permute-start.19 = (bf16[384,256]{1,0:T(8,128)(2,1)S(1)}, bf16[384,256]{1,0:T(8,128)(2,1)S(1)}, u32[]{:S(2)}, u32[]{:S(2)}) collective-permute-start(bf16[384,256]{1,0:T(8,128)(2,1)S(1)} %collective-permute-done.18.refs_2_), channel_id=1, source_target_pairs={{0,1},{1,0},{2,3},{3,2},{4,5},{5,4},{6,7},{7,6},{8,9},{9,8},{10,11... | collective-permute-start | bytes 589832 | tf_op jit(solution)/shard_map/ppermute | solution.py:51
  91.4 2.4 %collective-permute-start.17 = (bf16[384,256]{1,0:T(8,128)(2,1)S(1)}, bf16[384,256]{1,0:T(8,128)(2,1)S(1)}, u32[]{:S(2)}, u32[]{:S(2)}) collective-permute-start(bf16[384,256]{1,0:T(8,128)(2,1)S(1)} %collective-permute-done.16.refs_1_), channel_id=1, source_target_pairs={{0,1},{1,0},{2,3},{3,2},{4,5},{5,4},{6,7},{7,6},{8,9},{9,8},{10,11... | collective-permute-start | bytes 589832 | tf_op jit(solution)/shard_map/ppermute | solution.py:51
  96.8 4.2 %shard_map.110.refs_3_ = f32[49,256,128]{2,1,0:T(8,128)S(1)} custom-call(s32[8]{0:T(128)S(1)} %stack.81.order, s32[24,16]{1,0:T(8,128)S(1)} %shard_map.103.index, bf16[24,16,128,128]{3,2,1,0:T(8,128)(2,1)} %bitcast.35, bf16[384,256]{1,0:T(8,128)(2,1)S(1)} %get-tuple-element.25.refs_0_, bf16[384,256]{1,0:T(8,128)(2,1)S(1)} %collective-permute-done.20.refs_1_), custom_call_target="tpu_custom_call" | custom-call | flops 805306368 | bytes 3145728 | tf_op jit(solution)/shard_map/pallas_call | solution.py:236
  101.0 5.2 %shard_map.111.refs_3_ = f32[49,256,128]{2,1,0:T(8,128)S(1)} custom-call(s32[8]{0:T(128)S(1)} %stack.81.order, s32[24,16]{1,0:T(8,128)S(1)} %shard_map.103.index, bf16[24,16,128,128]{3,2,1,0:T(8,128)(2,1)} %bitcast.36, bf16[384,256]{1,0:T(8,128)(2,1)S(1)} %collective-permute-done.14.refs_0_, ...), custom_call_target="tpu_custom_call", output_to_operand_aliasing={{}: (6, {})} | custom-call | flops 1207959552 | bytes 4718592 | tf_op jit(solution)/shard_map/pallas_call | solution.py:236
  108.0 5.7 %shard_map.112 = (f32[49,256,128]{2,1,0:T(8,128)S(1)}, bf16[1152,256]{1,0:T(8,128)(2,1)S(1)}, bf16[1152,256]{1,0:T(8,128)(2,1)S(1)}, bf16[1152,256]{1,0:T(8,128)(2,1)S(1)}) custom-call(s32[8]{0:T(128)S(1)} %stack.81.order, s32[24,16]{1,0:T(8,128)S(1)} %shard_map.103.index, bf16[24,16,128,128]{3,2,1,0:T(8,128)(2,1)} %bitcast.37, ...), custom_call_target="tpu_custom_call", output_to_operand_aliasing={{0}: (6, {})} | custom-call | flops 1207959552 | bytes 4718592 | tf_op jit(solution)/shard_map/pallas_call | solution.py:236
  114.1 2.2 %collective-permute-start.22 = (bf16[1152,256]{1,0:T(8,128)(2,1)S(1)}, bf16[1152,256]{1,0:T(8,128)(2,1)S(1)}, u32[]{:S(2)}, u32[]{:S(2)}) collective-permute-start(bf16[1152,256]{1,0:T(8,128)(2,1)S(1)} %get-tuple-element.29), channel_id=1, source_target_pairs={{0,16},{1,65},{2,18},{3,67},{4,20},{5,69},{6,22},{7,71},{8,24},{9,... | collective-permute-start | bytes 1769480 | tf_op jit(solution)/shard_map/ppermute | solution.py:34
  116.3 2.0 %collective-permute-start.23 = (bf16[1152,256]{1,0:T(8,128)(2,1)S(1)}, bf16[1152,256]{1,0:T(8,128)(2,1)S(1)}, u32[]{:S(2)}, u32[]{:S(2)}) collective-permute-start(bf16[1152,256]{1,0:T(8,128)(2,1)S(1)} %get-tuple-element.30), channel_id=1, source_target_pairs={{0,24},{1,97},{2,26},{3,99},{4,28},{5,101},{6,30},{7,103},{8,0},{9... | collective-permute-start | bytes 1769480 | tf_op jit(solution)/shard_map/ppermute | solution.py:34
  118.8 6.9 %collective-permute-done.33.refs_1_ = bf16[272,256]{1,0:T(8,128)(2,1)S(1)} collective-permute-done((bf16[272,256]{1,0:T(8,128)(2,1)S(1)}, bf16[272,256]{1,0:T(8,128)(2,1)S(1)}, u32[]{:S(2)}, u32[]{:S(2)}) %collective-permute-start.33) | collective-permute-done | bytes 139296 | tf_op jit(solution)/shard_map/ppermute | solution.py:43
  126.7 3.3 %collective-permute-done.36.refs_3_ = bf16[272,256]{1,0:T(8,128)(2,1)S(1)} collective-permute-done((bf16[272,256]{1,0:T(8,128)(2,1)S(1)}, bf16[272,256]{1,0:T(8,128)(2,1)S(1)}, u32[]{:S(2)}, u32[]{:S(2)}) %collective-permute-start.36) | collective-permute-done | bytes 139296 | tf_op jit(solution)/shard_map/ppermute | solution.py:51
  132.1 3.0 %collective-permute-done.34.refs_1_ = bf16[272,256]{1,0:T(8,128)(2,1)S(1)} collective-permute-done((bf16[272,256]{1,0:T(8,128)(2,1)S(1)}, bf16[272,256]{1,0:T(8,128)(2,1)S(1)}, u32[]{:S(2)}, u32[]{:S(2)}) %collective-permute-start.34) | collective-permute-done | bytes 139296 | tf_op jit(solution)/shard_map/ppermute | solution.py:51
  135.2 9.8 %collective-permute-start.37 = (bf16[272,256]{1,0:T(8,128)(2,1)S(1)}, bf16[272,256]{1,0:T(8,128)(2,1)S(1)}, u32[]{:S(2)}, u32[]{:S(2)}) collective-permute-start(bf16[272,256]{1,0:T(8,128)(2,1)S(1)} %shard_map.120.t0), channel_id=1, source_target_pairs={{0,1},{1,0},{2,3},{3,2},{4,5},{5,4},{6,7},{7,6},{8,9},{9,8},{10,11... | collective-permute-start | bytes 417800 | tf_op jit(solution)/shard_map/ppermute | solution.py:51
  145.0 2.4 %collective-permute-start.28 = (bf16[384,256]{1,0:T(8,128)(2,1)S(1)}, bf16[384,256]{1,0:T(8,128)(2,1)S(1)}, u32[]{:S(2)}, u32[]{:S(2)}) collective-permute-start(bf16[384,256]{1,0:T(8,128)(2,1)S(1)} %get-tuple-element.35), channel_id=1, source_target_pairs={{0,16},{1,65},{2,18},{3,67},{4,20},{5,69},{6,22},{7,71},{8,24},{9,... | collective-permute-start | bytes 589832 | tf_op jit(solution)/shard_map/ppermute | solution.py:34
  148.1 3.2 %collective-permute-start.24 = (bf16[384,256]{1,0:T(8,128)(2,1)S(1)}, bf16[384,256]{1,0:T(8,128)(2,1)S(1)}, u32[]{:S(2)}, u32[]{:S(2)}) collective-permute-start(bf16[384,256]{1,0:T(8,128)(2,1)S(1)} %get-tuple-element.31), channel_id=1, source_target_pairs={{0,32},{1,9},{2,34},{3,11},{4,36},{5,13},{6,38},{7,15},{8,40},{9,1... | collective-permute-start | bytes 589832 | tf_op jit(solution)/shard_map/ppermute | solution.py:34
  151.3 2.1 %collective-permute-start.25 = (bf16[384,256]{1,0:T(8,128)(2,1)S(1)}, bf16[384,256]{1,0:T(8,128)(2,1)S(1)}, u32[]{:S(2)}, u32[]{:S(2)}) collective-permute-start(bf16[384,256]{1,0:T(8,128)(2,1)S(1)} %get-tuple-element.32), channel_id=1, source_target_pairs={{0,64},{1,17},{2,66},{3,19},{4,68},{5,21},{6,70},{7,23},{8,72},{9,... | collective-permute-start | bytes 589832 | tf_op jit(solution)/shard_map/ppermute | solution.py:34
  155.2 3.6 %collective-permute-done.25.refs_1_ = bf16[384,256]{1,0:T(8,128)(2,1)S(1)} collective-permute-done((bf16[384,256]{1,0:T(8,128)(2,1)S(1)}, bf16[384,256]{1,0:T(8,128)(2,1)S(1)}, u32[]{:S(2)}, u32[]{:S(2)}) %collective-permute-start.25) | collective-permute-done | bytes 196640 | tf_op jit(solution)/shard_map/ppermute | solution.py:34
  (94 shorter events, 28.5 us)
Async XLA Ops:
  0.6 8.7 %collective-permute-start.2 = (bf16[384,256]{1,0:T(8,128)(2,1)}, bf16[384,256]{1,0:T(8,128)(2,1)S(1)}, u32[]{:S(2)}, u32[]{:S(2)}) collective-permute-start(bf16[384,256]{1,0:T(8,128)(2,1)} %own.1), channel_id=1, source_target_pairs={{0,96},{1,25},{2,98},{3,27},{4,100},{5,29},{6,102},{7,31},{8,104},... | collective-permute-start | bytes 589832 | tf_op jit(solution)/shard_map/ppermute | solution.py:34
  4.6 8.3 %collective-permute-start = (bf16[384,256]{1,0:T(8,128)(2,1)}, bf16[384,256]{1,0:T(8,128)(2,1)S(1)}, u32[]{:S(2)}, u32[]{:S(2)}) collective-permute-start(bf16[384,256]{1,0:T(8,128)(2,1)} %own.1), channel_id=1, source_target_pairs={{0,32},{1,9},{2,34},{3,11},{4,36},{5,13},{6,38},{7,15},{8,40},{9,1... | collective-permute-start | bytes 589832 | tf_op jit(solution)/shard_map/ppermute | solution.py:34
  12.9 36.6 %collective-permute-start.8 = (bf16[1152,256]{1,0:T(8,128)(2,1)S(1)}, bf16[1152,256]{1,0:T(8,128)(2,1)S(1)}, u32[]{:S(2)}, u32[]{:S(2)}) collective-permute-start(bf16[1152,256]{1,0:T(8,128)(2,1)S(1)} %shard_map.105), channel_id=1, source_target_pairs={{0,24},{1,97},{2,26},{3,99},{4,28},{5,101},{6,30},{7,103},{8,0},{9... | collective-permute-start | bytes 1769480 | tf_op jit(solution)/shard_map/ppermute | solution.py:34
  15.2 34.4 %collective-permute-start.7 = (bf16[1152,256]{1,0:T(8,128)(2,1)S(1)}, bf16[1152,256]{1,0:T(8,128)(2,1)S(1)}, u32[]{:S(2)}, u32[]{:S(2)}) collective-permute-start(bf16[1152,256]{1,0:T(8,128)(2,1)S(1)} %shard_map.105), channel_id=1, source_target_pairs={{0,16},{1,65},{2,18},{3,67},{4,20},{5,69},{6,22},{7,71},{8,24},{9,... | collective-permute-start | bytes 1769480 | tf_op jit(solution)/shard_map/ppermute | solution.py:34
  15.7 33.9 %collective-permute-start.6 = (bf16[1152,256]{1,0:T(8,128)(2,1)S(1)}, bf16[1152,256]{1,0:T(8,128)(2,1)S(1)}, u32[]{:S(2)}, u32[]{:S(2)}) collective-permute-start(bf16[1152,256]{1,0:T(8,128)(2,1)S(1)} %shard_map.105), channel_id=1, source_target_pairs={{0,8},{1,33},{2,10},{3,35},{4,12},{5,37},{6,14},{7,39},{8,16},{9,4... | collective-permute-start | bytes 1769480 | tf_op jit(solution)/shard_map/ppermute | solution.py:34
  16.3 17.7 %collective-permute-start.4 = (bf16[384,256]{1,0:T(8,128)(2,1)}, bf16[384,256]{1,0:T(8,128)(2,1)S(1)}, u32[]{:S(2)}, u32[]{:S(2)}) collective-permute-start(bf16[384,256]{1,0:T(8,128)(2,1)} %own.1), channel_id=1, source_target_pairs={{0,16},{1,65},{2,18},{3,67},{4,20},{5,69},{6,22},{7,71},{8,24},{9,... | collective-permute-start | bytes 589832 | tf_op jit(solution)/shard_map/ppermute | solution.py:34
  18.2 31.4 %collective-permute-start.3 = (bf16[384,256]{1,0:T(8,128)(2,1)}, bf16[384,256]{1,0:T(8,128)(2,1)S(1)}, u32[]{:S(2)}, u32[]{:S(2)}) collective-permute-start(bf16[384,256]{1,0:T(8,128)(2,1)} %own.1), channel_id=1, source_target_pairs={{0,8},{1,33},{2,10},{3,35},{4,12},{5,37},{6,14},{7,39},{8,16},{9,4... | collective-permute-start | bytes 589832 | tf_op jit(solution)/shard_map/ppermute | solution.py:34
  34.0 15.6 %collective-permute-start.5 = (bf16[384,256]{1,0:T(8,128)(2,1)}, bf16[384,256]{1,0:T(8,128)(2,1)}, u32[]{:S(2)}, u32[]{:S(2)}) collective-permute-start(bf16[384,256]{1,0:T(8,128)(2,1)} %own.1), channel_id=1, source_target_pairs={{0,24},{1,97},{2,26},{3,99},{4,28},{5,101},{6,30},{7,103},{8,0},{9... | collective-permute-start | bytes 589832 | tf_op jit(solution)/shard_map/ppermute | solution.py:34
  57.4 8.4 %collective-permute-start.10 = (bf16[3,384,256]{2,1,0:T(8,128)(2,1)S(1)}, bf16[3,384,256]{2,1,0:T(8,128)(2,1)S(1)}, u32[]{:S(2)}, u32[]{:S(2)}) collective-permute-start(bf16[3,384,256]{2,1,0:T(8,128)(2,1)S(1)} %get-tuple-element.23), channel_id=1, source_target_pairs={{0,1},{1,0},{2,3},{3,2},{4,5},{5,4},{6,7},{7,6},{8,9},{9,8},{10,11... | collective-permute-start | bytes 1769480 | tf_op jit(solution)/shard_map/ppermute | solution.py:51
  63.1 7.4 %collective-permute-start.9 = (bf16[384,256]{1,0:T(8,128)(2,1)S(1)}, bf16[384,256]{1,0:T(8,128)(2,1)S(1)}, u32[]{:S(2)}, u32[]{:S(2)}) collective-permute-start(bf16[384,256]{1,0:T(8,128)(2,1)S(1)} %slice_bitcast_fusion), channel_id=1, source_target_pairs={{0,1},{1,0},{2,3},{3,2},{4,5},{5,4},{6,7},{7,6},{8,9},{9,8},{10,11... | collective-permute-start | bytes 589832 | tf_op jit(solution)/shard_map/ppermute | solution.py:51
  66.0 11.7 %collective-permute-start.13 = (bf16[384,256]{1,0:T(8,128)(2,1)S(1)}, bf16[384,256]{1,0:T(8,128)(2,1)S(1)}, u32[]{:S(2)}, u32[]{:S(2)}) collective-permute-start(bf16[384,256]{1,0:T(8,128)(2,1)S(1)} %get-tuple-element.40), channel_id=1, source_target_pairs={{0,6},{1,7},{2,0},{3,1},{4,2},{5,3},{6,4},{7,5},{8,14},{9,15},{10,... | collective-permute-start | bytes 589832 | tf_op jit(solution)/shard_map/ppermute | solution.py:51
  69.8 7.9 %collective-permute-start.12 = (bf16[384,256]{1,0:T(8,128)(2,1)S(1)}, bf16[384,256]{1,0:T(8,128)(2,1)S(1)}, u32[]{:S(2)}, u32[]{:S(2)}) collective-permute-start(bf16[384,256]{1,0:T(8,128)(2,1)S(1)} %get-tuple-element.41), channel_id=1, source_target_pairs={{0,4},{1,5},{2,6},{3,7},{4,0},{5,1},{6,2},{7,3},{8,12},{9,13},{10,... | collective-permute-start | bytes 589832 | tf_op jit(solution)/shard_map/ppermute | solution.py:51
  69.8 12.0 %collective-permute-start.11 = (bf16[384,256]{1,0:T(8,128)(2,1)S(1)}, bf16[384,256]{1,0:T(8,128)(2,1)S(1)}, u32[]{:S(2)}, u32[]{:S(2)}) collective-permute-start(bf16[384,256]{1,0:T(8,128)(2,1)S(1)} %get-tuple-element.42), channel_id=1, source_target_pairs={{0,2},{1,3},{2,4},{3,5},{4,6},{5,7},{6,0},{7,1},{8,10},{9,11},{10,... | collective-permute-start | bytes 589832 | tf_op jit(solution)/shard_map/ppermute | solution.py:51
  82.9 8.6 %collective-permute-start.16 = (bf16[384,256]{1,0:T(8,128)(2,1)S(1)}, bf16[384,256]{1,0:T(8,128)(2,1)S(1)}, u32[]{:S(2)}, u32[]{:S(2)}) collective-permute-start(bf16[384,256]{1,0:T(8,128)(2,1)S(1)} %get-tuple-element.25.refs_0_), channel_id=1, source_target_pairs={{0,4},{1,5},{2,6},{3,7},{4,0},{5,1},{6,2},{7,3},{8,12},{9,13},{10,... | collective-permute-start | bytes 589832 | tf_op jit(solution)/shard_map/ppermute | solution.py:51
  83.4 11.9 %collective-permute-start.14 = (bf16[384,256]{1,0:T(8,128)(2,1)S(1)}, bf16[384,256]{1,0:T(8,128)(2,1)S(1)}, u32[]{:S(2)}, u32[]{:S(2)}) collective-permute-start(bf16[384,256]{1,0:T(8,128)(2,1)S(1)} %get-tuple-element.25.refs_0_), channel_id=1, source_target_pairs={{0,2},{1,3},{2,4},{3,5},{4,6},{5,7},{6,0},{7,1},{8,10},{9,11},{10,... | collective-permute-start | bytes 589832 | tf_op jit(solution)/shard_map/ppermute | solution.py:51
  84.3 12.5 %collective-permute-start.20 = (bf16[384,256]{1,0:T(8,128)(2,1)S(1)}, bf16[384,256]{1,0:T(8,128)(2,1)S(1)}, u32[]{:S(2)}, u32[]{:S(2)}) collective-permute-start(bf16[384,256]{1,0:T(8,128)(2,1)S(1)} %get-tuple-element.25.refs_0_), channel_id=1, source_target_pairs={{0,1},{1,0},{2,3},{3,2},{4,5},{5,4},{6,7},{7,6},{8,9},{9,8},{10,11... | collective-permute-start | bytes 589832 | tf_op jit(solution)/shard_map/ppermute | solution.py:51
  85.7 10.3 %collective-permute-start.30 = (bf16[272,256]{1,0:T(8,128)(2,1)S(1)}, bf16[272,256]{1,0:T(8,128)(2,1)S(1)}, u32[]{:S(2)}, u32[]{:S(2)}) collective-permute-start(bf16[272,256]{1,0:T(8,128)(2,1)S(1)} %get-tuple-element.37.refs_0_), channel_id=1, source_target_pairs={{0,32},{8,40},{16,48},{24,56},{32,0},{40,8},{48,16},{56,24},{64,96... | collective-permute-start | bytes 417800 | tf_op jit(solution)/shard_map/ppermute | solution.py:43
  88.5 19.5 %collective-permute-start.19 = (bf16[384,256]{1,0:T(8,128)(2,1)S(1)}, bf16[384,256]{1,0:T(8,128)(2,1)S(1)}, u32[]{:S(2)}, u32[]{:S(2)}) collective-permute-start(bf16[384,256]{1,0:T(8,128)(2,1)S(1)} %collective-permute-done.18.refs_2_), channel_id=1, source_target_pairs={{0,1},{1,0},{2,3},{3,2},{4,5},{5,4},{6,7},{7,6},{8,9},{9,8},{10,11... | collective-permute-start | bytes 589832 | tf_op jit(solution)/shard_map/ppermute | solution.py:51
  91.4 16.6 %collective-permute-start.17 = (bf16[384,256]{1,0:T(8,128)(2,1)S(1)}, bf16[384,256]{1,0:T(8,128)(2,1)S(1)}, u32[]{:S(2)}, u32[]{:S(2)}) collective-permute-start(bf16[384,256]{1,0:T(8,128)(2,1)S(1)} %collective-permute-done.16.refs_1_), channel_id=1, source_target_pairs={{0,1},{1,0},{2,3},{3,2},{4,5},{5,4},{6,7},{7,6},{8,9},{9,8},{10,11... | collective-permute-start | bytes 589832 | tf_op jit(solution)/shard_map/ppermute | solution.py:51
  95.3 12.7 %collective-permute-start.15 = (bf16[384,256]{1,0:T(8,128)(2,1)S(1)}, bf16[384,256]{1,0:T(8,128)(2,1)S(1)}, u32[]{:S(2)}, u32[]{:S(2)}) collective-permute-start(bf16[384,256]{1,0:T(8,128)(2,1)S(1)} %collective-permute-done.14.refs_0_), channel_id=1, source_target_pairs={{0,1},{1,0},{2,3},{3,2},{4,5},{5,4},{6,7},{7,6},{8,9},{9,8},{10,11... | collective-permute-start | bytes 589832 | tf_op jit(solution)/shard_map/ppermute | solution.py:51
  96.0 10.1 %collective-permute-start.31 = (bf16[272,256]{1,0:T(8,128)(2,1)S(1)}, bf16[272,256]{1,0:T(8,128)(2,1)S(1)}, u32[]{:S(2)}, u32[]{:S(2)}) collective-permute-start(bf16[272,256]{1,0:T(8,128)(2,1)S(1)} %shard_map.116.refs_0_), channel_id=1, source_target_pairs={{0,64},{8,72},{16,80},{24,88},{32,96},{40,104},{48,112},{56,120},{... | collective-permute-start | bytes 417800 | tf_op jit(solution)/shard_map/ppermute | solution.py:43
  106.2 12.1 %collective-permute-start.32 = (bf16[272,256]{1,0:T(8,128)(2,1)S(1)}, bf16[272,256]{1,0:T(8,128)(2,1)S(1)}, u32[]{:S(2)}, u32[]{:S(2)}) collective-permute-start(bf16[272,256]{1,0:T(8,128)(2,1)S(1)} %shard_map.117.refs_0_), channel_id=1, source_target_pairs={{0,8},{8,0},{16,24},{24,16},{32,40},{40,32},{48,56},{56,48},{64,72... | collective-permute-start | bytes 417800 | tf_op jit(solution)/shard_map/ppermute | solution.py:43
  113.7 31.3 %collective-permute-start.21 = (bf16[1152,256]{1,0:T(8,128)(2,1)S(1)}, bf16[1152,256]{1,0:T(8,128)(2,1)S(1)}, u32[]{:S(2)}, u32[]{:S(2)}) collective-permute-start(bf16[1152,256]{1,0:T(8,128)(2,1)S(1)} %get-tuple-element.28), channel_id=1, source_target_pairs={{0,8},{1,33},{2,10},{3,35},{4,12},{5,37},{6,14},{7,39},{8,16},{9,4... | collective-permute-start | bytes 1769480 | tf_op jit(solution)/shard_map/ppermute | solution.py:34
  114.1 33.3 %collective-permute-start.22 = (bf16[1152,256]{1,0:T(8,128)(2,1)S(1)}, bf16[1152,256]{1,0:T(8,128)(2,1)S(1)}, u32[]{:S(2)}, u32[]{:S(2)}) collective-permute-start(bf16[1152,256]{1,0:T(8,128)(2,1)S(1)} %get-tuple-element.29), channel_id=1, source_target_pairs={{0,16},{1,65},{2,18},{3,67},{4,20},{5,69},{6,22},{7,71},{8,24},{9,... | collective-permute-start | bytes 1769480 | tf_op jit(solution)/shard_map/ppermute | solution.py:34
  116.3 31.4 %collective-permute-start.23 = (bf16[1152,256]{1,0:T(8,128)(2,1)S(1)}, bf16[1152,256]{1,0:T(8,128)(2,1)S(1)}, u32[]{:S(2)}, u32[]{:S(2)}) collective-permute-start(bf16[1152,256]{1,0:T(8,128)(2,1)S(1)} %get-tuple-element.30), channel_id=1, source_target_pairs={{0,24},{1,97},{2,26},{3,99},{4,28},{5,101},{6,30},{7,103},{8,0},{9... | collective-permute-start | bytes 1769480 | tf_op jit(solution)/shard_map/ppermute | solution.py:34
  118.4 7.3 %collective-permute-start.33 = (bf16[272,256]{1,0:T(8,128)(2,1)S(1)}, bf16[272,256]{1,0:T(8,128)(2,1)S(1)}, u32[]{:S(2)}, u32[]{:S(2)}) collective-permute-start(bf16[272,256]{1,0:T(8,128)(2,1)S(1)} %shard_map.118.refs_0_), channel_id=1, source_target_pairs={{0,16},{8,24},{16,0},{24,8},{32,48},{40,56},{48,32},{56,40},{64,80... | collective-permute-start | bytes 417800 | tf_op jit(solution)/shard_map/ppermute | solution.py:43
  132.1 19.2 %collective-permute-start.27 = (bf16[384,256]{1,0:T(8,128)(2,1)S(1)}, bf16[384,256]{1,0:T(8,128)(2,1)S(1)}, u32[]{:S(2)}, u32[]{:S(2)}) collective-permute-start(bf16[384,256]{1,0:T(8,128)(2,1)S(1)} %get-tuple-element.34), channel_id=1, source_target_pairs={{0,8},{1,33},{2,10},{3,35},{4,12},{5,37},{6,14},{7,39},{8,16},{9,4... | collective-permute-start | bytes 589832 | tf_op jit(solution)/shard_map/ppermute | solution.py:34
  135.2 18.1 %collective-permute-start.37 = (bf16[272,256]{1,0:T(8,128)(2,1)S(1)}, bf16[272,256]{1,0:T(8,128)(2,1)S(1)}, u32[]{:S(2)}, u32[]{:S(2)}) collective-permute-start(bf16[272,256]{1,0:T(8,128)(2,1)S(1)} %shard_map.120.t0), channel_id=1, source_target_pairs={{0,1},{1,0},{2,3},{3,2},{4,5},{5,4},{6,7},{7,6},{8,9},{9,8},{10,11... | collective-permute-start | bytes 417800 | tf_op jit(solution)/shard_map/ppermute | solution.py:51
  145.0 9.5 %collective-permute-start.28 = (bf16[384,256]{1,0:T(8,128)(2,1)S(1)}, bf16[384,256]{1,0:T(8,128)(2,1)S(1)}, u32[]{:S(2)}, u32[]{:S(2)}) collective-permute-start(bf16[384,256]{1,0:T(8,128)(2,1)S(1)} %get-tuple-element.35), channel_id=1, source_target_pairs={{0,16},{1,65},{2,18},{3,67},{4,20},{5,69},{6,22},{7,71},{8,24},{9,... | collective-permute-start | bytes 589832 | tf_op jit(solution)/shard_map/ppermute | solution.py:34
  148.1 7.1 %collective-permute-start.24 = (bf16[384,256]{1,0:T(8,128)(2,1)S(1)}, bf16[384,256]{1,0:T(8,128)(2,1)S(1)}, u32[]{:S(2)}, u32[]{:S(2)}) collective-permute-start(bf16[384,256]{1,0:T(8,128)(2,1)S(1)} %get-tuple-element.31), channel_id=1, source_target_pairs={{0,32},{1,9},{2,34},{3,11},{4,36},{5,13},{6,38},{7,15},{8,40},{9,1... | collective-permute-start | bytes 589832 | tf_op jit(solution)/shard_map/ppermute | solution.py:34
  151.3 7.5 %collective-permute-start.25 = (bf16[384,256]{1,0:T(8,128)(2,1)S(1)}, bf16[384,256]{1,0:T(8,128)(2,1)S(1)}, u32[]{:S(2)}, u32[]{:S(2)}) collective-permute-start(bf16[384,256]{1,0:T(8,128)(2,1)S(1)} %get-tuple-element.32), channel_id=1, source_target_pairs={{0,64},{1,17},{2,66},{3,19},{4,68},{5,21},{6,70},{7,23},{8,72},{9,... | collective-permute-start | bytes 589832 | tf_op jit(solution)/shard_map/ppermute | solution.py:34
  153.3 7.1 %collective-permute-start.26 = (bf16[384,256]{1,0:T(8,128)(2,1)S(1)}, bf16[384,256]{1,0:T(8,128)(2,1)S(1)}, u32[]{:S(2)}, u32[]{:S(2)}) collective-permute-start(bf16[384,256]{1,0:T(8,128)(2,1)S(1)} %get-tuple-element.33), channel_id=1, source_target_pairs={{0,96},{1,25},{2,98},{3,27},{4,100},{5,29},{6,102},{7,31},{8,104},... | collective-permute-start | bytes 589832 | tf_op jit(solution)/shard_map/ppermute | solution.py:34
  (17 other events, 133.9 us)

commit v4 on v3

--- a/solution.py
+++ b/solution.py
@@ -154,7 +154,7 @@
     )(order, index, adj, *operands)
 
 
-def activation_kernel(keep, recv, r1, r2, r3, weight, bias, cot, act, grad_out, terms):
+def activation_kernel(keep, recv, r1, r2, r3, weight, bias, cot, act, grad_out, both):
     agg = keep[1].astype(F32) + recv[...].astype(F32)
     for ref in (r1, r2, r3):
         agg = agg + ref[...].astype(F32)
@@ -164,11 +164,12 @@
     act[...] = (pre * sig).astype(BF)
     grad = (cot[...].astype(F32) * sig * (1.0 + pre * (1.0 - sig))).astype(BF)
     grad_out[...] = grad
-    wrows = terms.shape[0] - BROWS
-    terms[0:wrows, :] = lax.dot_general(
+    both[0:ND, :] = grad
+    wrows = both.shape[0] - BROWS
+    both[ND:wrows, :] = lax.dot_general(
         agg16, grad, (((0,), (0,)), ((), ())), preferred_element_type=F32
     ).astype(BF)
-    terms[wrows:, :] = pack_bias(jnp.sum(grad.astype(F32), axis=0, keepdims=True))
+    both[wrows:, :] = pack_bias(jnp.sum(grad.astype(F32), axis=0, keepdims=True))
 
 
 def backward_kernel(offset, count, initial, final, order, index, adj, *refs):
@@ -252,6 +253,13 @@
 def add_terms_kernel(*refs):
     terms, out = [ref[...].astype(F32) for ref in refs[:-1]], refs[-1]
     total = sum4(*terms) if len(terms) == SIDE else terms[0] + terms[1]
+    wrows = out.shape[0] - BROWS
+    out[0:wrows, :] = total[:wrows].astype(BF)
+    out[wrows:, :] = pack_bias(jnp.sum(total[wrows:], axis=0, keepdims=True))
+
+
+def pair_terms_kernel(mine, theirs, out):
+    total = mine[ND:, :].astype(F32) + theirs[ND:, :].astype(F32)
     wrows = out.shape[0] - BROWS
     out[0:wrows, :] = total[:wrows].astype(BF)
     out[wrows:, :] = pack_bias(jnp.sum(total[wrows:], axis=0, keepdims=True))
@@ -346,24 +354,24 @@
     recv = send_col(keep[0], 0, 1)
     block = jax.ShapeDtypeStruct((ND, width), BF)
     terms = jax.ShapeDtypeStruct((width + BROWS, width), BF)
-    activated, grad, along = small(
+    both = jax.ShapeDtypeStruct((ND + width + BROWS, width), BF)
+    activated, grad, both = small(
         activation_kernel,
-        (block, block, terms),
+        (block, block, both),
         [keep, recv, *parts, weight, out_bias.reshape(1, -1), cotangent],
     )
 
     mine = [grad] + fan(lambda v, d: send_col(v, d, 0), [grad] * 3)
-    theirs = [send_col(grad, 0, 1)]
+    theirs = [send_col(both, 0, 1)]
+    along = small(pair_terms_kernel, terms, [both, theirs[0]])
     theirs += fan(lambda v, d: send_col(v, 0, 1), mine[1:])
     other_terms = trade_row(along, 1, True)
+    acc, = backward(0, order_backward, index, adj, [mine[0], theirs[0]])
     along = small(add_terms_kernel, terms, [along, other_terms])
     other_terms = trade_row(along, 2, True)
-    acc, = backward(0, order_backward, index, adj, [mine[0], theirs[0]])
+    acc, = backward(2, order_backward, index, adj, mine[1:], acc)
     along = small(add_terms_kernel, terms, [along, other_terms])
     other_terms = trade_row(along, 1, False)
-    acc, = backward(2, order_backward, index, adj, mine[1:], acc)
-    along = small(add_terms_kernel, terms, [along, other_terms])
-    other_terms = trade_row(along, 2, False)
     acc, *blocks = backward(SIDE + 1, order_backward, index, adj, theirs[1:], acc, final=True)
 
     landed = fan(lambda v, d: send_plane(v, False, d), blocks)
@@ -373,7 +381,7 @@
     along = small(add_terms_kernel, terms, [along, other_terms])
     along_z = [along] + fan(lambda v, d: send_col(v, d, 0), [along] * 3)
     along = small(add_terms_kernel, terms, along_z)
-    other_terms = send_col(along, 0, 1)
+    other_terms = trade_row(along, 2, False)
     nodes = features.shape[0] * lax.axis_size("row") * lax.axis_size("col")
     grad_weight, grad_bias = small(
         functools.partial(last_terms_kernel, nodes**-0.5),

time: 162 us -> 162 us (level)
  the two profiles are of different devices: /device:TPU:1 before, /device:TPU:0 now
where the time goes in v4:
time: 162 us
  waiting for transfers between devices  76.7 us (47%)
  starting transfers between devices  37.4 us (23%)
  Pallas kernels  33.3 us (21%)
  local copies, waits for them, and re-layouts  13.5 us (8%)
    ppermute x15, waiting for transfers between devices, send_col(): return lax.ppermute(value, 'col', pairs)  32.2 us
    ppermute x18, waiting for transfers between devices, send_plane(): return lax.ppermute(value, ('row', 'col'), pairs)  28.1 us
    ppermute x18, starting transfers between devices, send_plane(): return lax.ppermute(value, ('row', 'col'), pairs)  24.2 us
    ppermute x4, waiting for transfers between devices, trade_row(): return lax.ppermute(value, 'row', pairs)  16.4 us
    pallas_call x3, Pallas kernels, backward(): pl.pallas_call(functools.partial(backward_kernel, offset, count, initial,...  15 us
    unnamed x23, local copies, waits for them, and re-layouts  11.9 us
    ppermute x15, starting transfers between devices, send_col(): return lax.ppermute(value, 'col', pairs)  9.2 us
    pallas_call x3, Pallas kernels, forward(): pl.pallas_call(functools.partial(forward_first_kernel if first else forwa...  7.79 us
  transfers between devices with their start and end apart: 37, of which 16 were waited for; matrix products, arithmetic and copies ran while one was open for 2% of the time, Pallas kernels for 17%

profile of v4, /device:TPU:0, one launch (start us, length us, event | category | flops | bytes accessed | tf_op | source)
XLA Modules:
  0.0 162.0 jit_solution(14068022787286588870)
XLA Ops:
  0.6 2.9 %collective-permute-start.2 = (bf16[384,256]{1,0:T(8,128)(2,1)}, bf16[384,256]{1,0:T(8,128)(2,1)S(1)}, u32[]{:S(2)}, u32[]{:S(2)}) collective-permute-start(bf16[384,256]{1,0:T(8,128)(2,1)} %own.1), channel_id=1, source_target_pairs={{0,96},{1,25},{2,98},{3,27},{4,100},{5,29},{6,102},{7,31},{8,104},... | collective-permute-start | bytes 589832 | tf_op jit(solution)/shard_map/ppermute | solution.py:34
  5.3 4.0 %collective-permute-done.2.refs_2_.f3 = bf16[384,256]{1,0:T(8,128)(2,1)S(1)} collective-permute-done((bf16[384,256]{1,0:T(8,128)(2,1)}, bf16[384,256]{1,0:T(8,128)(2,1)S(1)}, u32[]{:S(2)}, u32[]{:S(2)}) %collective-permute-start.2) | collective-permute-done | bytes 196640 | tf_op jit(solution)/shard_map/ppermute | solution.py:34
  9.2 1.8 %collective-permute-done.1.refs_1_.f2 = bf16[384,256]{1,0:T(8,128)(2,1)S(1)} collective-permute-done((bf16[384,256]{1,0:T(8,128)(2,1)}, bf16[384,256]{1,0:T(8,128)(2,1)S(1)}, u32[]{:S(2)}, u32[]{:S(2)}) %collective-permute-start.1) | collective-permute-done | bytes 196640 | tf_op jit(solution)/shard_map/ppermute | solution.py:34
  11.1 2.0 %collective-permute-done.refs_0_.f1 = bf16[384,256]{1,0:T(8,128)(2,1)S(1)} collective-permute-done((bf16[384,256]{1,0:T(8,128)(2,1)}, bf16[384,256]{1,0:T(8,128)(2,1)S(1)}, u32[]{:S(2)}, u32[]{:S(2)}) %collective-permute-start) | collective-permute-done | bytes 196640 | tf_op jit(solution)/shard_map/ppermute | solution.py:34
  13.1 3.1 %collective-permute-start.8 = (bf16[1152,256]{1,0:T(8,128)(2,1)S(1)}, bf16[1152,256]{1,0:T(8,128)(2,1)S(1)}, u32[]{:S(2)}, u32[]{:S(2)}) collective-permute-start(bf16[1152,256]{1,0:T(8,128)(2,1)S(1)} %shard_map.105), channel_id=1, source_target_pairs={{0,24},{1,97},{2,26},{3,99},{4,28},{5,101},{6,30},{7,103},{8,0},{9... | collective-permute-start | bytes 1769480 | tf_op jit(solution)/shard_map/ppermute | solution.py:34
  17.8 1.9 %collective-permute-start.4 = (bf16[384,256]{1,0:T(8,128)(2,1)}, bf16[384,256]{1,0:T(8,128)(2,1)S(1)}, u32[]{:S(2)}, u32[]{:S(2)}) collective-permute-start(bf16[384,256]{1,0:T(8,128)(2,1)} %own.1), channel_id=1, source_target_pairs={{0,16},{1,65},{2,18},{3,67},{4,20},{5,69},{6,22},{7,71},{8,24},{9,... | collective-permute-start | bytes 589832 | tf_op jit(solution)/shard_map/ppermute | solution.py:34
  20.9 15.2 %collective-permute-done.4.s2 = bf16[384,256]{1,0:T(8,128)(2,1)S(1)} collective-permute-done((bf16[384,256]{1,0:T(8,128)(2,1)}, bf16[384,256]{1,0:T(8,128)(2,1)S(1)}, u32[]{:S(2)}, u32[]{:S(2)}) %collective-permute-start.4) | collective-permute-done | bytes 196640 | tf_op jit(solution)/shard_map/ppermute | solution.py:34
  38.9 6.1 %shard_map.104.adj = bf16[24,16,128,128]{3,2,1,0:T(8,128)(2,1)S(1)} custom-call(bf16[24,16,128,128]{3,2,1,0:T(8,128)(2,1)} %bitcast.34), custom_call_target="tpu_custom_call" | custom-call | tf_op jit(solution)/shard_map/pallas_call | solution.py:319
  45.0 4.6 %copy-done = bf16[24,16,128,128]{3,2,1,0:T(8,128)(2,1)} copy-done((bf16[24,16,128,128]{3,2,1,0:T(8,128)(2,1)}, bf16[24,16,128,128]{3,2,1,0:T(8,128)(2,1)S(1)}, u32[]{:S(2)}) %copy-start) | copy-done | bytes 12582936
  51.8 4.6 %copy-done.1 = bf16[24,16,128,128]{3,2,1,0:T(8,128)(2,1)S(1)} copy-done((bf16[24,16,128,128]{3,2,1,0:T(8,128)(2,1)S(1)}, bf16[24,16,128,128]{3,2,1,0:T(8,128)(2,1)}, u32[]{:S(2)}) %copy-start.1) | copy-done | bytes 12582936
  56.4 3.2 %shard_map.106 = (bf16[3,384,256]{2,1,0:T(8,128)(2,1)S(1)}, bf16[6272,256]{1,0:T(8,128)(2,1)S(1)}) custom-call(s32[8]{0:T(128)S(1)} %stack.70.order, s32[24,16]{1,0:T(8,128)S(1)} %shard_map.103.index, bf16[24,16,128,128]{3,2,1,0:T(8,128)(2,1)S(1)} %copy-done.1, bf16[384,256]{1,0:T(8,128)(2,1)S(1)} %copy-done.3, ...), custom_call_target="tpu_custom_call" | custom-call | flops 1207959552 | bytes 4718592 | tf_op jit(solution)/shard_map/pallas_call | solution.py:147
  59.7 2.0 %shard_map.107.keep = bf16[2,384,256]{2,1,0:T(8,128)(2,1)S(1)} custom-call(s32[8]{0:T(128)S(1)} %stack.70.order, s32[24,16]{1,0:T(8,128)S(1)} %shard_map.103.index, bf16[24,16,128,128]{3,2,1,0:T(8,128)(2,1)S(1)} %copy-done.1, bf16[6272,256]{1,0:T(8,128)(2,1)S(1)} %get-tuple-element.22.panel), custom_call_target="tpu_custom_call" | custom-call | flops 805306368 | bytes 3145728 | tf_op jit(solution)/shard_map/pallas_call | solution.py:147
  62.3 2.6 %shard_map.108 = bf16[3,384,256]{2,1,0:T(8,128)(2,1)S(1)} custom-call(s32[8]{0:T(128)S(1)} %stack.70.order, s32[24,16]{1,0:T(8,128)S(1)} %shard_map.103.index, bf16[24,16,128,128]{3,2,1,0:T(8,128)(2,1)S(1)} %bitcast.31, bf16[6272,256]{1,0:T(8,128)(2,1)S(1)} %get-tuple-element.22.panel), custom_call_target="tpu_custom_call" | custom-call | flops 1207959552 | bytes 4718592 | tf_op jit(solution)/shard_map/pallas_call | solution.py:147
  65.1 4.1 %collective-permute-start.13 = (bf16[384,256]{1,0:T(8,128)(2,1)S(1)}, bf16[384,256]{1,0:T(8,128)(2,1)S(1)}, u32[]{:S(2)}, u32[]{:S(2)}) collective-permute-start(bf16[384,256]{1,0:T(8,128)(2,1)S(1)} %get-tuple-element.40), channel_id=1, source_target_pairs={{0,6},{1,7},{2,0},{3,1},{4,2},{5,3},{6,4},{7,5},{8,14},{9,15},{10,... | collective-permute-start | bytes 589832 | tf_op jit(solution)/shard_map/ppermute | solution.py:51
  70.5 7.3 %collective-permute-done.13.r3 = bf16[384,256]{1,0:T(8,128)(2,1)S(1)} collective-permute-done((bf16[384,256]{1,0:T(8,128)(2,1)S(1)}, bf16[384,256]{1,0:T(8,128)(2,1)S(1)}, u32[]{:S(2)}, u32[]{:S(2)}) %collective-permute-start.13) | collective-permute-done | bytes 196640 | tf_op jit(solution)/shard_map/ppermute | solution.py:51
  78.5 2.7 %collective-permute-done.11.r1 = bf16[384,256]{1,0:T(8,128)(2,1)S(1)} collective-permute-done((bf16[384,256]{1,0:T(8,128)(2,1)S(1)}, bf16[384,256]{1,0:T(8,128)(2,1)S(1)}, u32[]{:S(2)}, u32[]{:S(2)}) %collective-permute-start.11) | collective-permute-done | bytes 196640 | tf_op jit(solution)/shard_map/ppermute | solution.py:51
  84.3 5.7 %collective-permute-done.18.refs_2_ = bf16[384,256]{1,0:T(8,128)(2,1)S(1)} collective-permute-done((bf16[384,256]{1,0:T(8,128)(2,1)S(1)}, bf16[384,256]{1,0:T(8,128)(2,1)S(1)}, u32[]{:S(2)}, u32[]{:S(2)}) %collective-permute-start.18) | collective-permute-done | bytes 196640 | tf_op jit(solution)/shard_map/ppermute | solution.py:51
  90.0 2.4 %collective-permute-done.16.refs_1_ = bf16[384,256]{1,0:T(8,128)(2,1)S(1)} collective-permute-done((bf16[384,256]{1,0:T(8,128)(2,1)S(1)}, bf16[384,256]{1,0:T(8,128)(2,1)S(1)}, u32[]{:S(2)}, u32[]{:S(2)}) %collective-permute-start.16) | collective-permute-done | bytes 196640 | tf_op jit(solution)/shard_map/ppermute | solution.py:51
  92.5 3.4 %collective-permute-done.14.refs_0_ = bf16[384,256]{1,0:T(8,128)(2,1)S(1)} collective-permute-done((bf16[384,256]{1,0:T(8,128)(2,1)S(1)}, bf16[384,256]{1,0:T(8,128)(2,1)S(1)}, u32[]{:S(2)}, u32[]{:S(2)}) %collective-permute-start.14) | collective-permute-done | bytes 196640 | tf_op jit(solution)/shard_map/ppermute | solution.py:51
  96.4 4.2 %shard_map.110.refs_3_ = f32[49,256,128]{2,1,0:T(8,128)S(1)} custom-call(s32[8]{0:T(128)S(1)} %stack.81.order, s32[24,16]{1,0:T(8,128)S(1)} %shard_map.103.index, bf16[24,16,128,128]{3,2,1,0:T(8,128)(2,1)} %bitcast.35, bf16[384,256]{1,0:T(8,128)(2,1)S(1)} %get-tuple-element.25.refs_0_, bf16[656,256]{1,0:T(8,128)(2,1)S(1)} %collective-permute-done.20.refs_1_.theirs), custom_call_target="tpu_custom_call" | custom-call | flops 805306368 | bytes 3145728 | tf_op jit(solution)/shard_map/pallas_call | solution.py:237
  100.5 5.2 %shard_map.111.refs_3_ = f32[49,256,128]{2,1,0:T(8,128)S(1)} custom-call(s32[8]{0:T(128)S(1)} %stack.81.order, s32[24,16]{1,0:T(8,128)S(1)} %shard_map.103.index, bf16[24,16,128,128]{3,2,1,0:T(8,128)(2,1)} %bitcast.36, bf16[384,256]{1,0:T(8,128)(2,1)S(1)} %collective-permute-done.14.refs_0_, ...), custom_call_target="tpu_custom_call", output_to_operand_aliasing={{}: (6, {})} | custom-call | flops 1207959552 | bytes 4718592 | tf_op jit(solution)/shard_map/pallas_call | solution.py:237
  105.8 2.1 %collective-permute-start.31 = (bf16[272,256]{1,0:T(8,128)(2,1)S(1)}, bf16[272,256]{1,0:T(8,128)(2,1)S(1)}, u32[]{:S(2)}, u32[]{:S(2)}) collective-permute-start(bf16[272,256]{1,0:T(8,128)(2,1)S(1)} %shard_map.117.refs_0_), channel_id=1, source_target_pairs={{0,64},{8,72},{16,80},{24,88},{32,96},{40,104},{48,112},{56,120},{... | collective-permute-start | bytes 417800 | tf_op jit(solution)/shard_map/ppermute | solution.py:43
  107.9 5.7 %shard_map.112 = (f32[49,256,128]{2,1,0:T(8,128)S(1)}, bf16[1152,256]{1,0:T(8,128)(2,1)S(1)}, bf16[1152,256]{1,0:T(8,128)(2,1)S(1)}, bf16[1152,256]{1,0:T(8,128)(2,1)S(1)}) custom-call(s32[8]{0:T(128)S(1)} %stack.81.order, s32[24,16]{1,0:T(8,128)S(1)} %shard_map.103.index, bf16[24,16,128,128]{3,2,1,0:T(8,128)(2,1)} %bitcast.37, ...), custom_call_target="tpu_custom_call", output_to_operand_aliasing={{0}: (6, {})} | custom-call | flops 1207959552 | bytes 4718592 | tf_op jit(solution)/shard_map/pallas_call | solution.py:237
  113.6 2.1 %collective-permute-start.21 = (bf16[1152,256]{1,0:T(8,128)(2,1)S(1)}, bf16[1152,256]{1,0:T(8,128)(2,1)S(1)}, u32[]{:S(2)}, u32[]{:S(2)}) collective-permute-start(bf16[1152,256]{1,0:T(8,128)(2,1)S(1)} %get-tuple-element.29), channel_id=1, source_target_pairs={{0,8},{1,33},{2,10},{3,35},{4,12},{5,37},{6,14},{7,39},{8,16},{9,4... | collective-permute-start | bytes 1769480 | tf_op jit(solution)/shard_map/ppermute | solution.py:34
  116.3 2.1 %collective-permute-start.23 = (bf16[1152,256]{1,0:T(8,128)(2,1)S(1)}, bf16[1152,256]{1,0:T(8,128)(2,1)S(1)}, u32[]{:S(2)}, u32[]{:S(2)}) collective-permute-start(bf16[1152,256]{1,0:T(8,128)(2,1)S(1)} %get-tuple-element.31), channel_id=1, source_target_pairs={{0,24},{1,97},{2,26},{3,99},{4,28},{5,101},{6,30},{7,103},{8,0},{9... | collective-permute-start | bytes 1769480 | tf_op jit(solution)/shard_map/ppermute | solution.py:34
  118.6 16.4 %collective-permute-done.32.refs_1_ = bf16[272,256]{1,0:T(8,128)(2,1)S(1)} collective-permute-done((bf16[272,256]{1,0:T(8,128)(2,1)S(1)}, bf16[272,256]{1,0:T(8,128)(2,1)S(1)}, u32[]{:S(2)}, u32[]{:S(2)}) %collective-permute-start.32) | collective-permute-done | bytes 139296 | tf_op jit(solution)/shard_map/ppermute | solution.py:43
  136.1 4.0 %collective-permute-done.35.refs_3_ = bf16[272,256]{1,0:T(8,128)(2,1)S(1)} collective-permute-done((bf16[272,256]{1,0:T(8,128)(2,1)S(1)}, bf16[272,256]{1,0:T(8,128)(2,1)S(1)}, u32[]{:S(2)}, u32[]{:S(2)}) %collective-permute-start.35) | collective-permute-done | bytes 139296 | tf_op jit(solution)/shard_map/ppermute | solution.py:51
  140.5 2.1 %collective-permute-done.34.refs_2_ = bf16[272,256]{1,0:T(8,128)(2,1)S(1)} collective-permute-done((bf16[272,256]{1,0:T(8,128)(2,1)S(1)}, bf16[272,256]{1,0:T(8,128)(2,1)S(1)}, u32[]{:S(2)}, u32[]{:S(2)}) %collective-permute-start.34) | collective-permute-done | bytes 139296 | tf_op jit(solution)/shard_map/ppermute | solution.py:51
  142.6 3.7 %collective-permute-done.33.refs_1_ = bf16[272,256]{1,0:T(8,128)(2,1)S(1)} collective-permute-done((bf16[272,256]{1,0:T(8,128)(2,1)S(1)}, bf16[272,256]{1,0:T(8,128)(2,1)S(1)}, u32[]{:S(2)}, u32[]{:S(2)}) %collective-permute-start.33) | collective-permute-done | bytes 139296 | tf_op jit(solution)/shard_map/ppermute | solution.py:51
  148.0 2.0 %collective-permute-start.28 = (bf16[384,256]{1,0:T(8,128)(2,1)S(1)}, bf16[384,256]{1,0:T(8,128)(2,1)S(1)}, u32[]{:S(2)}, u32[]{:S(2)}) collective-permute-start(bf16[384,256]{1,0:T(8,128)(2,1)S(1)} %get-tuple-element.36), channel_id=1, source_target_pairs={{0,16},{1,65},{2,18},{3,67},{4,20},{5,69},{6,22},{7,71},{8,24},{9,... | collective-permute-start | bytes 589832 | tf_op jit(solution)/shard_map/ppermute | solution.py:34
  150.8 4.4 %collective-permute-start.25 = (bf16[384,256]{1,0:T(8,128)(2,1)S(1)}, bf16[384,256]{1,0:T(8,128)(2,1)S(1)}, u32[]{:S(2)}, u32[]{:S(2)}) collective-permute-start(bf16[384,256]{1,0:T(8,128)(2,1)S(1)} %get-tuple-element.33), channel_id=1, source_target_pairs={{0,64},{1,17},{2,66},{3,19},{4,68},{5,21},{6,70},{7,23},{8,72},{9,... | collective-permute-start | bytes 589832 | tf_op jit(solution)/shard_map/ppermute | solution.py:34
  157.4 3.6 %collective-permute-done.25.refs_1_ = bf16[384,256]{1,0:T(8,128)(2,1)S(1)} collective-permute-done((bf16[384,256]{1,0:T(8,128)(2,1)S(1)}, bf16[384,256]{1,0:T(8,128)(2,1)S(1)}, u32[]{:S(2)}, u32[]{:S(2)}) %collective-permute-start.25) | collective-permute-done | bytes 196640 | tf_op jit(solution)/shard_map/ppermute | solution.py:34
  (92 shorter events, 23.7 us)
Async XLA Ops:
  0.6 8.6 %collective-permute-start.2 = (bf16[384,256]{1,0:T(8,128)(2,1)}, bf16[384,256]{1,0:T(8,128)(2,1)S(1)}, u32[]{:S(2)}, u32[]{:S(2)}) collective-permute-start(bf16[384,256]{1,0:T(8,128)(2,1)} %own.1), channel_id=1, source_target_pairs={{0,96},{1,25},{2,98},{3,27},{4,100},{5,29},{6,102},{7,31},{8,104},... | collective-permute-start | bytes 589832 | tf_op jit(solution)/shard_map/ppermute | solution.py:34
  3.6 7.5 %collective-permute-start.1 = (bf16[384,256]{1,0:T(8,128)(2,1)}, bf16[384,256]{1,0:T(8,128)(2,1)S(1)}, u32[]{:S(2)}, u32[]{:S(2)}) collective-permute-start(bf16[384,256]{1,0:T(8,128)(2,1)} %own.1), channel_id=1, source_target_pairs={{0,64},{1,17},{2,66},{3,19},{4,68},{5,21},{6,70},{7,23},{8,72},{9,... | collective-permute-start | bytes 589832 | tf_op jit(solution)/shard_map/ppermute | solution.py:34
  4.4 8.7 %collective-permute-start = (bf16[384,256]{1,0:T(8,128)(2,1)}, bf16[384,256]{1,0:T(8,128)(2,1)S(1)}, u32[]{:S(2)}, u32[]{:S(2)}) collective-permute-start(bf16[384,256]{1,0:T(8,128)(2,1)} %own.1), channel_id=1, source_target_pairs={{0,32},{1,9},{2,34},{3,11},{4,36},{5,13},{6,38},{7,15},{8,40},{9,1... | collective-permute-start | bytes 589832 | tf_op jit(solution)/shard_map/ppermute | solution.py:34
  13.1 38.6 %collective-permute-start.8 = (bf16[1152,256]{1,0:T(8,128)(2,1)S(1)}, bf16[1152,256]{1,0:T(8,128)(2,1)S(1)}, u32[]{:S(2)}, u32[]{:S(2)}) collective-permute-start(bf16[1152,256]{1,0:T(8,128)(2,1)S(1)} %shard_map.105), channel_id=1, source_target_pairs={{0,24},{1,97},{2,26},{3,99},{4,28},{5,101},{6,30},{7,103},{8,0},{9... | collective-permute-start | bytes 1769480 | tf_op jit(solution)/shard_map/ppermute | solution.py:34
  16.2 35.6 %collective-permute-start.7 = (bf16[1152,256]{1,0:T(8,128)(2,1)S(1)}, bf16[1152,256]{1,0:T(8,128)(2,1)S(1)}, u32[]{:S(2)}, u32[]{:S(2)}) collective-permute-start(bf16[1152,256]{1,0:T(8,128)(2,1)S(1)} %shard_map.105), channel_id=1, source_target_pairs={{0,16},{1,65},{2,18},{3,67},{4,20},{5,69},{6,22},{7,71},{8,24},{9,... | collective-permute-start | bytes 1769480 | tf_op jit(solution)/shard_map/ppermute | solution.py:34
  16.8 34.9 %collective-permute-start.6 = (bf16[1152,256]{1,0:T(8,128)(2,1)S(1)}, bf16[1152,256]{1,0:T(8,128)(2,1)S(1)}, u32[]{:S(2)}, u32[]{:S(2)}) collective-permute-start(bf16[1152,256]{1,0:T(8,128)(2,1)S(1)} %shard_map.105), channel_id=1, source_target_pairs={{0,8},{1,33},{2,10},{3,35},{4,12},{5,37},{6,14},{7,39},{8,16},{9,4... | collective-permute-start | bytes 1769480 | tf_op jit(solution)/shard_map/ppermute | solution.py:34
  17.8 18.4 %collective-permute-start.4 = (bf16[384,256]{1,0:T(8,128)(2,1)}, bf16[384,256]{1,0:T(8,128)(2,1)S(1)}, u32[]{:S(2)}, u32[]{:S(2)}) collective-permute-start(bf16[384,256]{1,0:T(8,128)(2,1)} %own.1), channel_id=1, source_target_pairs={{0,16},{1,65},{2,18},{3,67},{4,20},{5,69},{6,22},{7,71},{8,24},{9,... | collective-permute-start | bytes 589832 | tf_op jit(solution)/shard_map/ppermute | solution.py:34
  19.7 32.0 %collective-permute-start.3 = (bf16[384,256]{1,0:T(8,128)(2,1)}, bf16[384,256]{1,0:T(8,128)(2,1)S(1)}, u32[]{:S(2)}, u32[]{:S(2)}) collective-permute-start(bf16[384,256]{1,0:T(8,128)(2,1)} %own.1), channel_id=1, source_target_pairs={{0,8},{1,33},{2,10},{3,35},{4,12},{5,37},{6,14},{7,39},{8,16},{9,4... | collective-permute-start | bytes 589832 | tf_op jit(solution)/shard_map/ppermute | solution.py:34
  36.1 15.6 %collective-permute-start.5 = (bf16[384,256]{1,0:T(8,128)(2,1)}, bf16[384,256]{1,0:T(8,128)(2,1)}, u32[]{:S(2)}, u32[]{:S(2)}) collective-permute-start(bf16[384,256]{1,0:T(8,128)(2,1)} %own.1), channel_id=1, source_target_pairs={{0,24},{1,97},{2,26},{3,99},{4,28},{5,101},{6,30},{7,103},{8,0},{9... | collective-permute-start | bytes 589832 | tf_op jit(solution)/shard_map/ppermute | solution.py:34
  61.8 8.7 %collective-permute-start.9 = (bf16[384,256]{1,0:T(8,128)(2,1)S(1)}, bf16[384,256]{1,0:T(8,128)(2,1)S(1)}, u32[]{:S(2)}, u32[]{:S(2)}) collective-permute-start(bf16[384,256]{1,0:T(8,128)(2,1)S(1)} %slice_bitcast_fusion), channel_id=1, source_target_pairs={{0,1},{1,0},{2,3},{3,2},{4,5},{5,4},{6,7},{7,6},{8,9},{9,8},{10,11... | collective-permute-start | bytes 589832 | tf_op jit(solution)/shard_map/ppermute | solution.py:51
  65.1 12.7 %collective-permute-start.13 = (bf16[384,256]{1,0:T(8,128)(2,1)S(1)}, bf16[384,256]{1,0:T(8,128)(2,1)S(1)}, u32[]{:S(2)}, u32[]{:S(2)}) collective-permute-start(bf16[384,256]{1,0:T(8,128)(2,1)S(1)} %get-tuple-element.40), channel_id=1, source_target_pairs={{0,6},{1,7},{2,0},{3,1},{4,2},{5,3},{6,4},{7,5},{8,14},{9,15},{10,... | collective-permute-start | bytes 589832 | tf_op jit(solution)/shard_map/ppermute | solution.py:51
  69.2 9.3 %collective-permute-start.12 = (bf16[384,256]{1,0:T(8,128)(2,1)S(1)}, bf16[384,256]{1,0:T(8,128)(2,1)S(1)}, u32[]{:S(2)}, u32[]{:S(2)}) collective-permute-start(bf16[384,256]{1,0:T(8,128)(2,1)S(1)} %get-tuple-element.41), channel_id=1, source_target_pairs={{0,4},{1,5},{2,6},{3,7},{4,0},{5,1},{6,2},{7,3},{8,12},{9,13},{10,... | collective-permute-start | bytes 589832 | tf_op jit(solution)/shard_map/ppermute | solution.py:51
  69.2 12.0 %collective-permute-start.11 = (bf16[384,256]{1,0:T(8,128)(2,1)S(1)}, bf16[384,256]{1,0:T(8,128)(2,1)S(1)}, u32[]{:S(2)}, u32[]{:S(2)}) collective-permute-start(bf16[384,256]{1,0:T(8,128)(2,1)S(1)} %get-tuple-element.42), channel_id=1, source_target_pairs={{0,2},{1,3},{2,4},{3,5},{4,6},{5,7},{6,0},{7,1},{8,10},{9,11},{10,... | collective-permute-start | bytes 589832 | tf_op jit(solution)/shard_map/ppermute | solution.py:51
  82.3 13.8 %collective-permute-start.20 = (bf16[656,256]{1,0:T(8,128)(2,1)S(1)}, bf16[656,256]{1,0:T(8,128)(2,1)S(1)}, u32[]{:S(2)}, u32[]{:S(2)}) collective-permute-start(bf16[656,256]{1,0:T(8,128)(2,1)S(1)} %get-tuple-element.26.mine), channel_id=1, source_target_pairs={{0,1},{1,0},{2,3},{3,2},{4,5},{5,4},{6,7},{7,6},{8,9},{9,8},{10,11... | collective-permute-start | bytes 1007624 | tf_op jit(solution)/shard_map/ppermute | solution.py:51
  82.3 7.8 %collective-permute-start.18 = (bf16[384,256]{1,0:T(8,128)(2,1)S(1)}, bf16[384,256]{1,0:T(8,128)(2,1)S(1)}, u32[]{:S(2)}, u32[]{:S(2)}) collective-permute-start(bf16[384,256]{1,0:T(8,128)(2,1)S(1)} %get-tuple-element.25.refs_0_), channel_id=1, source_target_pairs={{0,6},{1,7},{2,0},{3,1},{4,2},{5,3},{6,4},{7,5},{8,14},{9,15},{10,... | collective-permute-start | bytes 589832 | tf_op jit(solution)/shard_map/ppermute | solution.py:51
  83.2 9.3 %collective-permute-start.16 = (bf16[384,256]{1,0:T(8,128)(2,1)S(1)}, bf16[384,256]{1,0:T(8,128)(2,1)S(1)}, u32[]{:S(2)}, u32[]{:S(2)}) collective-permute-start(bf16[384,256]{1,0:T(8,128)(2,1)S(1)} %get-tuple-element.25.refs_0_), channel_id=1, source_target_pairs={{0,4},{1,5},{2,6},{3,7},{4,0},{5,1},{6,2},{7,3},{8,12},{9,13},{10,... | collective-permute-start | bytes 589832 | tf_op jit(solution)/shard_map/ppermute | solution.py:51
  83.4 12.5 %collective-permute-start.14 = (bf16[384,256]{1,0:T(8,128)(2,1)S(1)}, bf16[384,256]{1,0:T(8,128)(2,1)S(1)}, u32[]{:S(2)}, u32[]{:S(2)}) collective-permute-start(bf16[384,256]{1,0:T(8,128)(2,1)S(1)} %get-tuple-element.25.refs_0_), channel_id=1, source_target_pairs={{0,2},{1,3},{2,4},{3,5},{4,6},{5,7},{6,0},{7,1},{8,10},{9,11},{10,... | collective-permute-start | bytes 589832 | tf_op jit(solution)/shard_map/ppermute | solution.py:51
  90.0 17.8 %collective-permute-start.19 = (bf16[384,256]{1,0:T(8,128)(2,1)S(1)}, bf16[384,256]{1,0:T(8,128)(2,1)S(1)}, u32[]{:S(2)}, u32[]{:S(2)}) collective-permute-start(bf16[384,256]{1,0:T(8,128)(2,1)S(1)} %collective-permute-done.18.refs_2_), channel_id=1, source_target_pairs={{0,1},{1,0},{2,3},{3,2},{4,5},{5,4},{6,7},{7,6},{8,9},{9,8},{10,11... | collective-permute-start | bytes 589832 | tf_op jit(solution)/shard_map/ppermute | solution.py:51
  92.5 15.4 %collective-permute-start.17 = (bf16[384,256]{1,0:T(8,128)(2,1)S(1)}, bf16[384,256]{1,0:T(8,128)(2,1)S(1)}, u32[]{:S(2)}, u32[]{:S(2)}) collective-permute-start(bf16[384,256]{1,0:T(8,128)(2,1)S(1)} %collective-permute-done.16.refs_1_), channel_id=1, source_target_pairs={{0,1},{1,0},{2,3},{3,2},{4,5},{5,4},{6,7},{7,6},{8,9},{9,8},{10,11... | collective-permute-start | bytes 589832 | tf_op jit(solution)/shard_map/ppermute | solution.py:51
  95.9 12.0 %collective-permute-start.15 = (bf16[384,256]{1,0:T(8,128)(2,1)S(1)}, bf16[384,256]{1,0:T(8,128)(2,1)S(1)}, u32[]{:S(2)}, u32[]{:S(2)}) collective-permute-start(bf16[384,256]{1,0:T(8,128)(2,1)S(1)} %collective-permute-done.14.refs_0_), channel_id=1, source_target_pairs={{0,1},{1,0},{2,3},{3,2},{4,5},{5,4},{6,7},{7,6},{8,9},{9,8},{10,11... | collective-permute-start | bytes 589832 | tf_op jit(solution)/shard_map/ppermute | solution.py:51
  96.1 9.6 %collective-permute-start.30 = (bf16[272,256]{1,0:T(8,128)(2,1)S(1)}, bf16[272,256]{1,0:T(8,128)(2,1)S(1)}, u32[]{:S(2)}, u32[]{:S(2)}) collective-permute-start(bf16[272,256]{1,0:T(8,128)(2,1)S(1)} %shard_map.116.refs_0_), channel_id=1, source_target_pairs={{0,32},{8,40},{16,48},{24,56},{32,0},{40,8},{48,16},{56,24},{64,96... | collective-permute-start | bytes 417800 | tf_op jit(solution)/shard_map/ppermute | solution.py:43
  105.8 12.7 %collective-permute-start.31 = (bf16[272,256]{1,0:T(8,128)(2,1)S(1)}, bf16[272,256]{1,0:T(8,128)(2,1)S(1)}, u32[]{:S(2)}, u32[]{:S(2)}) collective-permute-start(bf16[272,256]{1,0:T(8,128)(2,1)S(1)} %shard_map.117.refs_0_), channel_id=1, source_target_pairs={{0,64},{8,72},{16,80},{24,88},{32,96},{40,104},{48,112},{56,120},{... | collective-permute-start | bytes 417800 | tf_op jit(solution)/shard_map/ppermute | solution.py:43
  113.6 34.5 %collective-permute-start.21 = (bf16[1152,256]{1,0:T(8,128)(2,1)S(1)}, bf16[1152,256]{1,0:T(8,128)(2,1)S(1)}, u32[]{:S(2)}, u32[]{:S(2)}) collective-permute-start(bf16[1152,256]{1,0:T(8,128)(2,1)S(1)} %get-tuple-element.29), channel_id=1, source_target_pairs={{0,8},{1,33},{2,10},{3,35},{4,12},{5,37},{6,14},{7,39},{8,16},{9,4... | collective-permute-start | bytes 1769480 | tf_op jit(solution)/shard_map/ppermute | solution.py:34
  115.7 34.4 %collective-permute-start.22 = (bf16[1152,256]{1,0:T(8,128)(2,1)S(1)}, bf16[1152,256]{1,0:T(8,128)(2,1)S(1)}, u32[]{:S(2)}, u32[]{:S(2)}) collective-permute-start(bf16[1152,256]{1,0:T(8,128)(2,1)S(1)} %get-tuple-element.30), channel_id=1, source_target_pairs={{0,16},{1,65},{2,18},{3,67},{4,20},{5,69},{6,22},{7,71},{8,24},{9,... | collective-permute-start | bytes 1769480 | tf_op jit(solution)/shard_map/ppermute | solution.py:34
  116.3 33.8 %collective-permute-start.23 = (bf16[1152,256]{1,0:T(8,128)(2,1)S(1)}, bf16[1152,256]{1,0:T(8,128)(2,1)S(1)}, u32[]{:S(2)}, u32[]{:S(2)}) collective-permute-start(bf16[1152,256]{1,0:T(8,128)(2,1)S(1)} %get-tuple-element.31), channel_id=1, source_target_pairs={{0,24},{1,97},{2,26},{3,99},{4,28},{5,101},{6,30},{7,103},{8,0},{9... | collective-permute-start | bytes 1769480 | tf_op jit(solution)/shard_map/ppermute | solution.py:34
  118.5 16.5 %collective-permute-start.32 = (bf16[272,256]{1,0:T(8,128)(2,1)S(1)}, bf16[272,256]{1,0:T(8,128)(2,1)S(1)}, u32[]{:S(2)}, u32[]{:S(2)}) collective-permute-start(bf16[272,256]{1,0:T(8,128)(2,1)S(1)} %shard_map.118.refs_0_), channel_id=1, source_target_pairs={{0,8},{8,0},{16,24},{24,16},{32,40},{40,32},{48,56},{56,48},{64,72... | collective-permute-start | bytes 417800 | tf_op jit(solution)/shard_map/ppermute | solution.py:43
  136.1 6.6 %collective-permute-start.34 = (bf16[272,256]{1,0:T(8,128)(2,1)S(1)}, bf16[272,256]{1,0:T(8,128)(2,1)S(1)}, u32[]{:S(2)}, u32[]{:S(2)}) collective-permute-start(bf16[272,256]{1,0:T(8,128)(2,1)S(1)} %shard_map.119.refs_0_), channel_id=1, source_target_pairs={{0,4},{1,5},{2,6},{3,7},{4,0},{5,1},{6,2},{7,3},{8,12},{9,13},{10,... | collective-permute-start | bytes 417800 | tf_op jit(solution)/shard_map/ppermute | solution.py:51
  142.6 8.2 %collective-permute-start.27 = (bf16[384,256]{1,0:T(8,128)(2,1)S(1)}, bf16[384,256]{1,0:T(8,128)(2,1)S(1)}, u32[]{:S(2)}, u32[]{:S(2)}) collective-permute-start(bf16[384,256]{1,0:T(8,128)(2,1)S(1)} %get-tuple-element.35), channel_id=1, source_target_pairs={{0,8},{1,33},{2,10},{3,35},{4,12},{5,37},{6,14},{7,39},{8,16},{9,4... | collective-permute-start | bytes 589832 | tf_op jit(solution)/shard_map/ppermute | solution.py:34
  146.5 8.7 %collective-permute-start.36 = (bf16[272,256]{1,0:T(8,128)(2,1)S(1)}, bf16[272,256]{1,0:T(8,128)(2,1)S(1)}, u32[]{:S(2)}, u32[]{:S(2)}) collective-permute-start(bf16[272,256]{1,0:T(8,128)(2,1)S(1)} %shard_map.120.t0), channel_id=1, source_target_pairs={{0,16},{8,24},{16,0},{24,8},{32,48},{40,56},{48,32},{56,40},{64,80... | collective-permute-start | bytes 417800 | tf_op jit(solution)/shard_map/ppermute | solution.py:43
  148.0 7.9 %collective-permute-start.28 = (bf16[384,256]{1,0:T(8,128)(2,1)S(1)}, bf16[384,256]{1,0:T(8,128)(2,1)S(1)}, u32[]{:S(2)}, u32[]{:S(2)}) collective-permute-start(bf16[384,256]{1,0:T(8,128)(2,1)S(1)} %get-tuple-element.36), channel_id=1, source_target_pairs={{0,16},{1,65},{2,18},{3,67},{4,20},{5,69},{6,22},{7,71},{8,24},{9,... | collective-permute-start | bytes 589832 | tf_op jit(solution)/shard_map/ppermute | solution.py:34
  150.4 7.0 %collective-permute-start.24 = (bf16[384,256]{1,0:T(8,128)(2,1)S(1)}, bf16[384,256]{1,0:T(8,128)(2,1)S(1)}, u32[]{:S(2)}, u32[]{:S(2)}) collective-permute-start(bf16[384,256]{1,0:T(8,128)(2,1)S(1)} %get-tuple-element.32), channel_id=1, source_target_pairs={{0,32},{1,9},{2,34},{3,11},{4,36},{5,13},{6,38},{7,15},{8,40},{9,1... | collective-permute-start | bytes 589832 | tf_op jit(solution)/shard_map/ppermute | solution.py:34
  150.8 10.1 %collective-permute-start.25 = (bf16[384,256]{1,0:T(8,128)(2,1)S(1)}, bf16[384,256]{1,0:T(8,128)(2,1)S(1)}, u32[]{:S(2)}, u32[]{:S(2)}) collective-permute-start(bf16[384,256]{1,0:T(8,128)(2,1)S(1)} %get-tuple-element.33), channel_id=1, source_target_pairs={{0,64},{1,17},{2,66},{3,19},{4,68},{5,21},{6,70},{7,23},{8,72},{9,... | collective-permute-start | bytes 589832 | tf_op jit(solution)/shard_map/ppermute | solution.py:34
  (16 other events, 124.8 us)
